TPU v7x, 32 devices: a whole 2x2x4 slice. The times are simulated.
32 devices in a mesh: survey: 2 (over x), freq: 16 (over z, y, core).
Axes of the slice: x: 2, y: 2, z: 4, core: 2. Of those that a mesh axis runs over, the one named last changes fastest.
Arguments:
- source: float32 [32, 2, 512, 512], P(('survey', 'freq')), parts along dimension 0, may hold values from -6 to 6
- receiver: float32 [32, 2, 512, 512], P(('survey', 'freq')), parts along dimension 0, may hold values from -6 to 6
- velocity: float32 [8, 512, 512], P('survey', 'freq'), parts along dimension 0, may hold values from 1.5 to 4.5
- anisotropy: float32 [8, 512, 512], P('survey', 'freq'), parts along dimension 0, may hold values from 0 to 0.3
- frequency: float32 [2], replicated, may hold values from 60 to 250
Outputs:
- image: float32 [8, 512, 512], P('survey', 'freq'), parts along dimension 0
There are 2 independent parts, one for each index of `survey`. A program takes and returns all parts, laid end to end along the dimension named above; an argument that names none is the same for every part. Nothing has to cross between parts.
All inputs are finite; a program needn't handle non-finite values.
Results may differ from a plain program's by a relative error of at most 0.000029.
Values sent between devices are 32-bit elements; how exact they have to be, the bound alone decides.
No kernel may reach another device: no remote copies, remote signals or barrier semaphores. Data moves between devices by JAX's collectives and lax.ppermute only.
A program may use at most 128 MiB of HBM per device.

v0:
```python
import math
import numpy as np
import jax
import jax.numpy as jnp
from jax import lax
from jax.experimental import pallas as pl
from jax.experimental.pallas import tpu as pltpu
from jax.sharding import PartitionSpec as P


LANES = 128
SUB = 8
UP = 4
U0 = 2
U1 = 8
VLIM = 28 << 20
TOP = 1.7


def even_fit(fun, degree):
    top = TOP * TOP
    nodes = 0.5 * top * (1.0 + np.cos(np.pi * (np.arange(degree + 1) + 0.5) / (degree + 1)))
    return [float(c) for c in np.polynomial.polynomial.polyfit(nodes, fun(np.sqrt(nodes)), degree)]


SIN_C = even_fit(lambda x: np.sin(x) / x, 5)
COS_C = even_fit(np.cos, 6)


def horner(coefs, z):
    acc = z * coefs[-1] + coefs[-2]
    for c in coefs[-3::-1]:
        acc = acc * z + c
    return acc


def off_of(k):
    return ((k & 3) << 1) | (k >> 2)


def at_off(o):
    return ((o & 1) << 2) | (o >> 1)


def cut(b):
    return slice(b * LANES, (b + 1) * LANES)


def iotas():
    return (lax.broadcasted_iota(jnp.int32, (SUB, LANES), 0), lax.broadcasted_iota(jnp.int32, (SUB, LANES), 1))


def pick(parts, which, index):
    out = jnp.take_along_axis(parts[0], index, axis=1)
    for a in range(1, len(parts)):
        out = jnp.where(which == a, jnp.take_along_axis(parts[a], index, axis=1), out)
    return out


def spread(parts):
    nb, lane = len(parts), iotas()[1]
    return [pick(parts, lane // (LANES // nb), (lane * nb + b) % LANES) for b in range(nb)]


def spread4(parts):
    lane = iotas()[1]
    w = LANES // 4
    index = (lane % w) * 4 + lane // w
    p = [jnp.take_along_axis(x, index, axis=1) for x in parts]
    low, even = lane < 2 * w, (lane // w) % 2 == 0
    q = [None] * 4
    for a in range(2):
        x, y = p[a], p[a + 2]
        q[a] = jnp.where(low, x, pltpu.roll(y, 2 * w, 1))
        q[a + 2] = jnp.where(low, pltpu.roll(x, 2 * w, 1), y)
    out = [None] * 4
    for a in (0, 2):
        x, y = q[a], q[a + 1]
        out[a] = jnp.where(even, x, pltpu.roll(y, w, 1))
        out[a + 1] = jnp.where(even, pltpu.roll(x, LANES - w, 1), y)
    return out


def gather_back(parts):
    nb, lane = len(parts), iotas()[1]
    return [pick(parts, lane % nb, lane // nb + a * (LANES // nb)) for a in range(nb)]


def prep_models_kernel(vel, ani, *outs):
    depth, R, NY = vel.shape
    nb = NY // LANES
    for d in range(depth):
        for m, ref in enumerate((vel, ani)):
            for j in range(R // SUB):
                rows = slice(j * SUB, (j + 1) * SUB)
                new = spread([ref[d, rows, cut(b)] for b in range(nb)])
                for b in range(nb):
                    outs[d][m, rows, cut(b)] = new[b]


def prep_models(vel, ani):
    depth, R, NY = vel.shape
    return pl.pallas_call(
        prep_models_kernel, out_shape=[jax.ShapeDtypeStruct((2, R, NY), jnp.float32)] * depth, name="prep_models",
    )(vel, ani)


def prep_fields_kernel(where, src, rcv, out, buf, sem):
    G, NY = out.shape[1], out.shape[3]
    nb = NY // LANES
    chunks = 4
    C = G // chunks
    copies = []
    for h in range(chunks):
        for k in range(SUB):
            row = pl.multiple_of((where[0] ^ off_of(k)) * G + h * C, SUB)
            for a, ref in enumerate((src, rcv)):
                for c in range(2):
                    copies.append(pltpu.make_async_copy(
                        ref.at[c, pl.ds(row, C), :], buf.at[2 * a + c, pl.ds(h * C, C), k, :], sem.at[h]))
    for c in copies:
        c.start()
    for h in range(chunks):
        for c in copies[h * SUB * 4 : (h + 1) * SUB * 4]:
            c.wait()

        def body(j, _):
            for q in range(UP):
                i = j * UP + q
                for a in range(4):
                    new = spread4([buf[a, i, :, cut(b)] for b in range(nb)])
                    for b in range(nb):
                        out[a, i, :, cut(b)] = -new[b] if a == 3 else new[b]
            return 0

        lax.fori_loop(h * C // UP, (h + 1) * C // UP, body, 0)


def prep_fields(where, src, rcv, G, NY):
    shape = (4, G, SUB, NY)
    smem, vmem, anym = (pl.BlockSpec(memory_space=s) for s in (pltpu.SMEM, pltpu.VMEM, pl.ANY))
    return pl.pallas_call(
        prep_fields_kernel, out_shape=jax.ShapeDtypeStruct(shape, jnp.float32), in_specs=[smem, anym, anym], out_specs=vmem,
        scratch_shapes=[pltpu.VMEM(shape, jnp.float32), pltpu.SemaphoreType.DMA((4,))], name="prep_fields",
        compiler_params=pltpu.CompilerParams(vmem_limit_bytes=16 << 20),
    )(where, src, rcv)


def finish_kernel(scale, early, *refs):
    out = refs[-1]
    depth, R, NY = out.shape
    nb = NY // LANES
    for d in range(depth):
        for j in range(R // SUB):
            rows = slice(j * SUB, (j + 1) * SUB)
            parts = []
            for b in range(nb):
                if d < depth - 1:
                    parts.append(early[d, rows, cut(b)] * scale)
                else:
                    v = refs[0][rows, cut(b)]
                    for r in refs[1:-1]:
                        v = v + r[rows, cut(b)]
                    parts.append(v * scale)
            new = gather_back(parts)
            for b in range(nb):
                out[d, rows, cut(b)] = new[b]


def finish(scale, early, tail):
    depth, R, NY = early.shape
    return pl.pallas_call(
        lambda *r: finish_kernel(scale, *r), out_shape=jax.ShapeDtypeStruct((depth + 1, R, NY), jnp.float32), name="finish",
    )(early, *tail)


def wave_tools(where, G, NB):
    me_g = where[0]
    kk, lane = iotas()
    left_edge, right_edge = lane == 0, lane == LANES - 1
    g = me_g ^ off_of(kk)
    up_idx, dn_idx = (at_off(me_g ^ ((g + step) & 7)) for step in (-1, 1))
    has_up, has_dn = g > 0, g < SUB - 1

    def halos(buf):
        for c in range(4):
            for b in range(NB):
                v = buf[c, G, :, cut(b)]
                buf[c, 0, :, cut(b)] = jnp.where(has_up, jnp.take_along_axis(v, up_idx, axis=0), 0.0)
                v = buf[c, 1, :, cut(b)]
                buf[c, G + 1, :, cut(b)] = jnp.where(has_dn, jnp.take_along_axis(v, dn_idx, axis=0), 0.0)

    def around(up, mid, dn):
        r = [a + b for a, b in zip(up, dn)]
        t = [m + 0.25 * a for m, a in zip(mid, r)]
        left = [jnp.where(left_edge, 0.0, pltpu.roll(t[-1], 1, 1))] + t[:-1]
        right = t[1:] + [jnp.where(right_edge, 0.0, pltpu.roll(t[0], LANES - 1, 1))]
        return [a + (b + c) for a, b, c in zip(r, left, right)]

    def sweep(src_buf, put, base, count):
        def body(j, _):
            i0 = base + j * U1
            for f in range(2):
                rows = [[[src_buf[2 * f + c, i0 + q, :, cut(b)] for b in range(NB)] for q in range(U1 + 2)] for c in range(2)]
                for q in range(U1):
                    o = [around(rows[c][q], rows[c][q + 1], rows[c][q + 2]) for c in range(2)]
                    put(f, q, i0 + q, o, [rows[c][q + 1] for c in range(2)])
            return 0

        lax.fori_loop(0, count // U1, body, 0)

    return halos, sweep


def times(mod, i, b, x, y):
    br, bi = mod[0, i, :, cut(b)], mod[1, i, :, cut(b)]
    return br * x - bi * y, br * y + bi * x


def first_kernel(cfg, where, om_ref, *refs):
    metas, R = cfg["metas"], cfg["R"]
    blks, (cur, sh, e1, mod, sem_m) = refs[: len(metas)], refs[len(metas) :]
    G, NB = mod.shape[1], mod.shape[3] // LANES
    lo = where[1]
    bases = [lo * R, (1 - lo) * R][: G // R]
    model_copies = [[] for _ in bases]
    for ref, (k0, kb, half) in zip(blks, metas):
        for k in range(kb):
            for m in range(2):
                model_copies[half].append(pltpu.make_async_copy(
                    ref.at[k, m], mod.at[m, pl.ds(bases[half], R), k0 + k, :], sem_m.at[half]))
    for some in model_copies:
        for c in some:
            c.start()
    halos, sweep = wave_tools(where, G, NB)
    om = om_ref[0]
    k1 = 6.0 / om
    kp = 0.01 * om

    def stage0(i0):
        for q in range(U0):
            i = i0 + q
            for b in range(NB):
                v = mod[0, i, :, cut(b)]
                eta = mod[1, i, :, cut(b)]
                cf = (v * k1) * (1.0 + 2.0 * eta)
                d = cf * (10.0 / 3.0)
                den = 1.0 + d * d
                inv = 1.0 / (v * den)
                ph = kp * (den * inv)
                bi = (cf * (2.0 / 3.0)) * (v * inv)
                mod[0, i, :, cut(b)] = bi * d
                mod[1, i, :, cut(b)] = bi
                z = ph * ph
                sn = ph * horner(SIN_C, z)
                cs = horner(COS_C, z)
                for f in range(2):
                    re, im = cur[2 * f, i, :, cut(b)], cur[2 * f + 1, i, :, cut(b)]
                    sh[2 * f, i + 1, :, cut(b)] = re * cs - im * sn
                    sh[2 * f + 1, i + 1, :, cut(b)] = im * cs + re * sn

    for half, base in enumerate(bases):
        for c in model_copies[half]:
            c.wait()
        lax.fori_loop(0, R // U0, lambda j, _: (stage0(base + j * U0), 0)[1], 0)
    halos(sh)

    def put(f, q, i, o, mid):
        for b in range(NB):
            x, y = times(mod, i, b, o[0][b] - 5.0 * mid[0][b], o[1][b] - 5.0 * mid[1][b])
            e1[2 * f, i + 1, :, cut(b)] = x
            e1[2 * f + 1, i + 1, :, cut(b)] = y

    sweep(sh, put, 0, G)
    halos(e1)


def second_kernel(cfg, where, sh, e1, mod, *refs):
    last, R = cfg["last"], cfg["R"]
    G, NB = mod.shape[1], mod.shape[3] // LANES
    outs, refs = refs[: G // R], list(refs[G // R :])
    lo = where[1]
    bases = [lo * R, (1 - lo) * R][: G // R]
    st, (e2, img, sem_o, *keep) = (None, refs) if last else (refs[0], refs[1:])
    halos, sweep = wave_tools(where, G, NB)

    def put2(f, q, i, o, mid):
        for b in range(NB):
            x, y = times(mod, i, b, o[0][b], o[1][b])
            e2[2 * f, i + 1, :, cut(b)] = x
            e2[2 * f + 1, i + 1, :, cut(b)] = y

    sweep(e1, put2, 0, G)
    halos(e2)

    def put3(f, q, i, o, mid):
        for b in range(NB):
            x, y = times(mod, i, b, o[0][b], o[1][b])
            new = []
            for c, x in enumerate((x, y)):
                total = (x + mid[c][b]) + e1[2 * f + c, i + 1, :, cut(b)]
                new.append(sh[2 * f + c, i + 1, :, cut(b)] + (total + total))
                if not last:
                    st[2 * f + c, i, :, cut(b)] = new[c]
                elif f == 0:
                    keep[0][c, q, :, cut(b)] = new[c]
            if f == 1:
                sr, si = (keep[0][c, q, :, cut(b)] if last else st[c, i, :, cut(b)] for c in range(2))
                img[i, :, cut(b)] = sr * new[0] - si * new[1]

    out_copies = []
    for o_i in reversed(range(len(outs))):
        sweep(e2, put3, bases[o_i], R)
        for k in range(SUB):
            c = pltpu.make_async_copy(img.at[pl.ds(bases[o_i], R), k, :], outs[o_i].at[k], sem_o)
            c.start()
            out_copies.append(c)
    for c in out_copies:
        c.wait()


def spaces():
    return [pl.BlockSpec(memory_space=s) for s in (pltpu.SMEM, pltpu.VMEM, pl.ANY)]


def first_call(where, omega, blocks, metas, state, R):
    _, G, _, NY = state.shape
    smem, vmem, anym = spaces()
    pad = jax.ShapeDtypeStruct((4, G + 2, SUB, NY), jnp.float32)
    return pl.pallas_call(
        lambda *r: first_kernel(dict(metas=metas, R=R), *r), out_shape=[pad, pad, jax.ShapeDtypeStruct((2, G, SUB, NY), jnp.float32)],
        in_specs=[smem, smem] + [anym] * len(blocks) + [vmem], out_specs=[vmem] * 3,
        scratch_shapes=[pltpu.SemaphoreType.DMA((G // R,))], name="first_half",
        compiler_params=pltpu.CompilerParams(vmem_limit_bytes=VLIM),
    )(where, omega, *blocks, state)


def second_call(where, sh, e1, mod, last, R):
    _, G, _, NY = mod.shape
    smem, vmem, anym = spaces()
    out_shape = [jax.ShapeDtypeStruct((SUB, R, NY), jnp.float32)] * (G // R)
    out_specs = [anym] * (G // R)
    if not last:
        out_shape.append(jax.ShapeDtypeStruct((4, G, SUB, NY), jnp.float32))
        out_specs.append(vmem)
    scratch = [pltpu.VMEM((4, G + 2, SUB, NY), jnp.float32), pltpu.VMEM((G, SUB, NY), jnp.float32), pltpu.SemaphoreType.DMA(())]
    if last:
        scratch.append(pltpu.VMEM((2, U1, SUB, NY), jnp.float32))
    return pl.pallas_call(
        lambda *r: second_kernel(dict(last=last, R=R), *r), out_shape=out_shape,
        in_specs=[smem] + [vmem] * 3, out_specs=out_specs,
        scratch_shapes=scratch, name="second_half",
        compiler_params=pltpu.CompilerParams(vmem_limit_bytes=VLIM),
    )(where, sh, e1, mod)


HALF = SUB // 2


def swap(x, mask):
    n = lax.axis_size("freq")
    return lax.ppermute(x, "freq", [(i, i ^ mask) for i in range(n)])


def exchange_path(source, receiver, velocity, anisotropy, omega, scale):
    me = lax.axis_index("freq")
    depth_count, R, NY = velocity.shape
    G = R * lax.axis_size("freq") // SUB
    where = jnp.stack([me >> 1, me & 1]).astype(jnp.int32)
    own = prep_models(velocity, anisotropy)
    states = [prep_fields(where, source[p], receiver[p], G, NY) for p in range(source.shape[0])]
    metas = [(0, HALF, 0), (HALF, HALF, 0), (0, HALF, 1), (HALF, HALF, 1)]
    layers = []
    for d in range(depth_count):
        last = d == depth_count - 1
        parts = [own[d]] + [swap(own[d], far << 2) for far in range(1, HALF)]
        mine = jnp.stack(parts)
        near = swap(mine, 2)
        blocks = [mine, near, swap(mine, 1), swap(near, 1)]
        total = None
        for p, state in enumerate(states):
            mid = first_call(where, omega[p : p + 1], blocks, metas, state, R)
            res = second_call(where, *mid, last, R)
            total = res[:2] if total is None else [a + b for a, b in zip(total, res[:2])]
            states[p] = None if last else res[2]
        kept, sent = total
        got = swap(sent, 1)
        upper = kept[HALF:] + got[HALF:]
        near = swap(upper, 2)
        parts = [(kept[far] + got[far]) + near[far] for far in range(HALF)]
        parts = [parts[0]] + [swap(parts[far], far << 2) for far in range(1, HALF)]
        layers.append(parts if last else sum(parts[1:], parts[0]))
    return finish(scale, jnp.stack(layers[:-1]), layers[-1])


def apart(x):
    nb = x.shape[-1] // LANES
    return jnp.swapaxes(x.reshape(x.shape[:-1] + (LANES, nb)), -1, -2).reshape(x.shape)


def together(x):
    nb = x.shape[-1] // LANES
    return jnp.swapaxes(x.reshape(x.shape[:-1] + (nb, LANES)), -1, -2).reshape(x.shape)


def gather_path(source, receiver, velocity, anisotropy, omega, scale):
    depth_count = velocity.shape[0]
    both = lax.all_gather(apart(jnp.stack([velocity, anisotropy], axis=1)), "freq", axis=2, tiled=True)
    NX, NY = both.shape[2:]
    G = NX // SUB
    places = [off_of(k) for k in range(SUB)]
    back = [places.index(g) for g in range(SUB)]
    both = both.reshape(depth_count, 2, SUB, G, NY)
    both = jnp.stack([both[:, :, g] for g in places], axis=1)
    where = jnp.zeros((2,), jnp.int32)
    states = [prep_fields(where, source[p], receiver[p], G, NY) for p in range(source.shape[0])]
    layers = []
    for d in range(depth_count):
        total = None
        for p, state in enumerate(states):
            last = d == depth_count - 1
            mid = first_call(where, omega[p : p + 1], [both[d]], [(0, SUB, 0)], state, G)
            res = second_call(where, *mid, last, G)
            total = res[0] if total is None else total + res[0]
            states[p] = None if last else res[1]
        whole = jnp.concatenate([total[k] for k in back], axis=0)
        layers.append(lax.psum_scatter(whole, "freq", scatter_dimension=0, tiled=True))
    return together(jnp.stack(layers)) * scale


def use_exchange(n, rows, pairs, depth):
    return n == 2 * SUB and rows % SUB == 0 and pairs == 1 and depth == 4


def on_device(source, receiver, velocity, anisotropy, frequency):
    pair_count = source.shape[0]
    n = lax.axis_size("freq")
    freq_total = frequency.shape[0]
    pair_ids = lax.axis_index("freq") * pair_count + jnp.arange(pair_count, dtype=jnp.int32)
    lookup = pair_ids[:, None] % freq_total == jnp.arange(freq_total, dtype=jnp.int32)[None, :]
    omega = jnp.sum(jnp.where(lookup, frequency[None, :], 0.0), axis=1)
    exchange = use_exchange(n, velocity.shape[1], pair_count, velocity.shape[0])
    path = exchange_path if exchange else gather_path
    return path(source, receiver, velocity, anisotropy, omega, 1.0 / math.sqrt(pair_count * n))


def solution(mesh):
    in_specs = (
        P(("survey", "freq"), None, None, None),
        P(("survey", "freq"), None, None, None),
        P("survey", "freq", None),
        P("survey", "freq", None),
        P(),
    )
    out_specs = P("survey", "freq", None)
    return jax.shard_map(
        on_device, mesh=mesh, in_specs=in_specs, out_specs=out_specs, check_vma=False
    )
```

profile of v0, /device:TPU:0, one launch (start us, length us, event | category | flops | bytes accessed | tf_op | source)
XLA Modules:
  0.0 197.2 jit_solution(12890319281275657824)
XLA Ops:
  0.0 2.9 %prep_models.1 = (f32[2,32,512]{2,1,0:T(8,128)}, f32[2,32,512]{2,1,0:T(8,128)}, f32[2,32,512]{2,1,0:T(8,128)}, f32[2,32,512]{2,1,0:T(8,128)}) custom-call(f32[4,32,512]{2,1,0:T(8,128)} %vel.1, f32[4,32,512]{2,1,0:T(8,128)} %ani.1), custom_call_target="tpu_custom_call" | custom-call | tf_op jit(solution)/shard_map/prep_models/pallas_call | solution.py:103
  2.9 3.1 %collective-permute-start = (f32[2,32,512]{2,1,0:T(8,128)}, f32[2,32,512]{2,1,0:T(8,128)S(1)}, u32[]{:S(2)}, u32[]{:S(2)}) collective-permute-start(f32[2,32,512]{2,1,0:T(8,128)} %get-tuple-element.32), channel_id=1, source_target_pairs={{0,4},{1,5},{2,6},{3,7},{4,0},{5,1},{6,2},{7,3},{8,12},{9,13},{10,... | collective-permute-start | bytes 393224 | tf_op jit(solution)/shard_map/ppermute | solution.py:362
  9.4 3.5 %collective-permute-start.12 = (f32[2,32,512]{2,1,0:T(8,128)}, f32[2,32,512]{2,1,0:T(8,128)S(1)}, u32[]{:S(2)}, u32[]{:S(2)}) collective-permute-start(f32[2,32,512]{2,1,0:T(8,128)} %get-tuple-element.38), channel_id=1, source_target_pairs={{0,8},{1,9},{2,10},{3,11},{4,12},{5,13},{6,14},{7,15},{8,0},{9,1},... | collective-permute-start | bytes 393224 | tf_op jit(solution)/shard_map/ppermute | solution.py:362
  12.9 3.5 %collective-permute-start.13 = (f32[2,32,512]{2,1,0:T(8,128)}, f32[2,32,512]{2,1,0:T(8,128)S(1)}, u32[]{:S(2)}, u32[]{:S(2)}) collective-permute-start(f32[2,32,512]{2,1,0:T(8,128)} %get-tuple-element.38), channel_id=1, source_target_pairs={{0,12},{1,13},{2,14},{3,15},{4,8},{5,9},{6,10},{7,11},{8,4},{9,5},... | collective-permute-start | bytes 393224 | tf_op jit(solution)/shard_map/ppermute | solution.py:362
  21.6 9.0 %collective-permute-start.22 = (f32[2,32,512]{2,1,0:T(8,128)}, f32[2,32,512]{2,1,0:T(8,128)S(1)}, u32[]{:S(2)}, u32[]{:S(2)}) collective-permute-start(f32[2,32,512]{2,1,0:T(8,128)} %get-tuple-element.45), channel_id=1, source_target_pairs={{0,4},{1,5},{2,6},{3,7},{4,0},{5,1},{6,2},{7,3},{8,12},{9,13},{10,... | collective-permute-start | bytes 393224 | tf_op jit(solution)/shard_map/ppermute | solution.py:362
  33.0 4.1 %collective-permute-done.22 = f32[2,32,512]{2,1,0:T(8,128)S(1)} collective-permute-done((f32[2,32,512]{2,1,0:T(8,128)}, f32[2,32,512]{2,1,0:T(8,128)S(1)}, u32[]{:S(2)}, u32[]{:S(2)}) %collective-permute-start.22) | collective-permute-done | bytes 131104 | tf_op jit(solution)/shard_map/ppermute | solution.py:362
  37.1 6.6 %collective-permute-done.23 = f32[2,32,512]{2,1,0:T(8,128)S(1)} collective-permute-done((f32[2,32,512]{2,1,0:T(8,128)}, f32[2,32,512]{2,1,0:T(8,128)S(1)}, u32[]{:S(2)}, u32[]{:S(2)}) %collective-permute-start.23) | collective-permute-done | bytes 131104 | tf_op jit(solution)/shard_map/ppermute | solution.py:362
  49.3 5.6 %collective-permute-done.34 = f32[2,32,512]{2,1,0:T(8,128)S(1)} collective-permute-done((f32[2,32,512]{2,1,0:T(8,128)}, f32[2,32,512]{2,1,0:T(8,128)S(1)}, u32[]{:S(2)}, u32[]{:S(2)}) %collective-permute-start.34) | collective-permute-done | bytes 131104 | tf_op jit(solution)/shard_map/ppermute | solution.py:362
  64.0 9.9 %collective-permute-done.25.r_3_ = f32[4,2,32,512]{3,2,1,0:T(8,128)} collective-permute-done((f32[4,2,32,512]{3,2,1,0:T(8,128)S(1)}, f32[4,2,32,512]{3,2,1,0:T(8,128)}, u32[]{:S(2)}, u32[]{:S(2)}) %collective-permute-start.25) | collective-permute-done | bytes 524320 | tf_op jit(solution)/shard_map/ppermute | solution.py:362
  73.9 9.0 %collective-permute-done.36.r_3_ = f32[4,2,32,512]{3,2,1,0:T(8,128)} collective-permute-done((f32[4,2,32,512]{3,2,1,0:T(8,128)}, f32[4,2,32,512]{3,2,1,0:T(8,128)}, u32[]{:S(2)}, u32[]{:S(2)}) %collective-permute-start.36) | collective-permute-done | bytes 524320 | tf_op jit(solution)/shard_map/ppermute | solution.py:362
  85.9 11.3 %prep_fields.1.r_6_ = f32[4,64,8,512]{3,2,1,0:T(8,128)S(1)} custom-call(s32[2]{0:T(128)S(1)} %pad_add_fusion.where.r_0_, f32[2,512,512]{2,1,0:T(8,128)S(1)} %bitcast.85, f32[2,512,512]{2,1,0:T(8,128)S(1)} %bitcast.86), custom_call_target="tpu_custom_call" | custom-call | tf_op jit(solution)/shard_map/prep_fields/pallas_call | solution.py:142
  97.9 6.6 %first_half.4 = (f32[4,66,8,512]{3,2,1,0:T(8,128)S(1)}, f32[4,66,8,512]{3,2,1,0:T(8,128)S(1)}, f32[2,64,8,512]{3,2,1,0:T(8,128)S(1)}) custom-call(s32[2]{0:T(128)S(1)} %pad_add_fusion.where.r_0_, f32[1]{0:T(128)} %bitcast.4.r_1_, f32[4,2,32,512]{3,2,1,0:T(8,128)S(1)} %pad_maximum_fusion.r_2_, f32[4,2,32,512]{3,2,1,0:T(8,128)S(1)} %copy-done.5, ...), custom_call_target="tpu_custom_call" | custom-call | tf_op jit(solution)/shard_map/first_half/pallas_call | solution.py:330
  104.5 4.9 %second_half.4 = (f32[8,32,512]{2,1,0:T(8,128)S(1)}, f32[8,32,512]{2,1,0:T(8,128)S(1)}, f32[4,64,8,512]{3,2,1,0:T(8,128)S(1)}) custom-call(s32[2]{0:T(128)S(1)} %pad_add_fusion.where.r_0_, f32[4,66,8,512]{3,2,1,0:T(8,128)S(1)} %get-tuple-element.33.r_1_, f32[4,66,8,512]{3,2,1,0:T(8,128)S(1)} %get-tuple-element.34.r_2_, ...), custom_call_target="tpu_custom_call" | custom-call | tf_op jit(solution)/shard_map/second_half/pallas_call | solution.py:349
  109.5 6.5 %first_half.5 = (f32[4,66,8,512]{3,2,1,0:T(8,128)S(1)}, f32[4,66,8,512]{3,2,1,0:T(8,128)S(1)}, f32[2,64,8,512]{3,2,1,0:T(8,128)S(1)}) custom-call(s32[2]{0:T(128)S(1)} %pad_add_fusion.where.r_0_, f32[1]{0:T(128)} %bitcast.4.r_1_, f32[4,2,32,512]{3,2,1,0:T(8,128)S(1)} %copy-done.3, f32[4,2,32,512]{3,2,1,0:T(8,128)} %collective-permute-done.14.r_3_, ...), custom_call_target="tpu_custom_call" | custom-call | tf_op jit(solution)/shard_map/first_half/pallas_call | solution.py:330
  116.0 4.9 %second_half.5 = (f32[8,32,512]{2,1,0:T(8,128)S(1)}, f32[8,32,512]{2,1,0:T(8,128)S(1)}, f32[4,64,8,512]{3,2,1,0:T(8,128)S(1)}) custom-call(s32[2]{0:T(128)S(1)} %pad_add_fusion.where.r_0_, f32[4,66,8,512]{3,2,1,0:T(8,128)S(1)} %get-tuple-element.40.r_1_, f32[4,66,8,512]{3,2,1,0:T(8,128)S(1)} %get-tuple-element.41.r_2_, ...), custom_call_target="tpu_custom_call" | custom-call | tf_op jit(solution)/shard_map/second_half/pallas_call | solution.py:349
  120.9 6.5 %first_half.6 = (f32[4,66,8,512]{3,2,1,0:T(8,128)S(1)}, f32[4,66,8,512]{3,2,1,0:T(8,128)S(1)}, f32[2,64,8,512]{3,2,1,0:T(8,128)S(1)}) custom-call(s32[2]{0:T(128)S(1)} %pad_add_fusion.where.r_0_, f32[1]{0:T(128)} %bitcast.4.r_1_, f32[4,2,32,512]{3,2,1,0:T(8,128)S(1)} %pad_maximum_fusion.2.r_2_, f32[4,2,32,512]{3,2,1,0:T(8,128)} %collective-permute-done.25.r_3_, ...), custom_call_target="tpu_custom_call" | custom-call | tf_op jit(solution)/shard_map/first_half/pallas_call | solution.py:330
  127.4 4.9 %second_half.6 = (f32[8,32,512]{2,1,0:T(8,128)S(1)}, f32[8,32,512]{2,1,0:T(8,128)S(1)}, f32[4,64,8,512]{3,2,1,0:T(8,128)S(1)}) custom-call(s32[2]{0:T(128)S(1)} %pad_add_fusion.where.r_0_, f32[4,66,8,512]{3,2,1,0:T(8,128)S(1)} %get-tuple-element.47.r_1_, f32[4,66,8,512]{3,2,1,0:T(8,128)S(1)} %get-tuple-element.48.r_2_, ...), custom_call_target="tpu_custom_call" | custom-call | tf_op jit(solution)/shard_map/second_half/pallas_call | solution.py:349
  132.3 6.3 %first_half.7 = (f32[4,66,8,512]{3,2,1,0:T(8,128)S(1)}, f32[4,66,8,512]{3,2,1,0:T(8,128)S(1)}, f32[2,64,8,512]{3,2,1,0:T(8,128)S(1)}) custom-call(s32[2]{0:T(128)S(1)} %pad_add_fusion.where.r_0_, f32[1]{0:T(128)} %bitcast.4.r_1_, f32[4,2,32,512]{3,2,1,0:T(8,128)} %pad_maximum_fusion.3.r_2_, f32[4,2,32,512]{3,2,1,0:T(8,128)} %collective-permute-done.36.r_3_, ...), custom_call_target="tpu_custom_call" | custom-call | tf_op jit(solution)/shard_map/first_half/pallas_call | solution.py:330
  138.6 5.2 %second_half.7 = (f32[8,32,512]{2,1,0:T(8,128)S(1)}, f32[8,32,512]{2,1,0:T(8,128)S(1)}) custom-call(s32[2]{0:T(128)S(1)} %pad_add_fusion.where.r_0_, f32[4,66,8,512]{3,2,1,0:T(8,128)S(1)} %get-tuple-element.54.r_1_, f32[4,66,8,512]{3,2,1,0:T(8,128)S(1)} %get-tuple-element.55.r_2_, f32[2,64,8,512]{3,2,1,0:T(8,128)S(1)} %get-tuple-element.56.r_3_), custom_call_target="tpu_custom_call" | custom-call | tf_op jit(solution)/shard_map/second_half/pallas_call | solution.py:349
  150.2 4.8 %collective-permute-done.40 = f32[4,32,512]{2,1,0:T(8,128)S(1)} collective-permute-done((f32[4,32,512]{2,1,0:T(8,128)S(1)}, f32[4,32,512]{2,1,0:T(8,128)S(1)}, u32[]{:S(2)}, u32[]{:S(2)}) %collective-permute-start.40) | collective-permute-done | bytes 262176 | tf_op jit(solution)/shard_map/ppermute | solution.py:362
  155.7 5.1 %collective-permute-start.41 = (f32[32,512]{1,0:T(8,128)S(1)}, f32[32,512]{1,0:T(8,128)S(1)}, u32[]{:S(2)}, u32[]{:S(2)}) collective-permute-start(f32[32,512]{1,0:T(8,128)S(1)} %get-tuple-element.61), channel_id=1, source_target_pairs={{0,4},{1,5},{2,6},{3,7},{4,0},{5,1},{6,2},{7,3},{8,12},{9,13},{10,... | collective-permute-start | bytes 196616 | tf_op jit(solution)/shard_map/ppermute | solution.py:362
  163.3 2.9 %collective-permute-done.18 = f32[4,32,512]{2,1,0:T(8,128)S(1)} collective-permute-done((f32[4,32,512]{2,1,0:T(8,128)S(1)}, f32[4,32,512]{2,1,0:T(8,128)S(1)}, u32[]{:S(2)}, u32[]{:S(2)}) %collective-permute-start.18) | collective-permute-done | bytes 262176 | tf_op jit(solution)/shard_map/ppermute | solution.py:362
  166.3 5.1 %collective-permute-start.8 = (f32[32,512]{1,0:T(8,128)S(1)}, f32[32,512]{1,0:T(8,128)S(1)}, u32[]{:S(2)}, u32[]{:S(2)}) collective-permute-start(f32[32,512]{1,0:T(8,128)S(1)} %get-tuple-element.63), channel_id=1, source_target_pairs={{0,4},{1,5},{2,6},{3,7},{4,0},{5,1},{6,2},{7,3},{8,12},{9,13},{10,... | collective-permute-start | bytes 196616 | tf_op jit(solution)/shard_map/ppermute | solution.py:362
  171.5 4.8 %collective-permute-start.9 = (f32[32,512]{1,0:T(8,128)S(1)}, f32[32,512]{1,0:T(8,128)S(1)}, u32[]{:S(2)}, u32[]{:S(2)}) collective-permute-start(f32[32,512]{1,0:T(8,128)S(1)} %get-tuple-element.65), channel_id=1, source_target_pairs={{0,8},{1,9},{2,10},{3,11},{4,12},{5,13},{6,14},{7,15},{8,0},{9,1},... | collective-permute-start | bytes 196616 | tf_op jit(solution)/shard_map/ppermute | solution.py:362
  (125 shorter events, 59.9 us)
Async XLA Ops:
  5.9 13.1 %collective-permute-start.1 = (f32[2,32,512]{2,1,0:T(8,128)}, f32[2,32,512]{2,1,0:T(8,128)S(1)}, u32[]{:S(2)}, u32[]{:S(2)}) collective-permute-start(f32[2,32,512]{2,1,0:T(8,128)} %get-tuple-element.32), channel_id=1, source_target_pairs={{0,8},{1,9},{2,10},{3,11},{4,12},{5,13},{6,14},{7,15},{8,0},{9,1},... | collective-permute-start | bytes 393224 | tf_op jit(solution)/shard_map/ppermute | solution.py:362
  8.5 13.0 %collective-permute-start.11 = (f32[2,32,512]{2,1,0:T(8,128)}, f32[2,32,512]{2,1,0:T(8,128)S(1)}, u32[]{:S(2)}, u32[]{:S(2)}) collective-permute-start(f32[2,32,512]{2,1,0:T(8,128)} %get-tuple-element.38), channel_id=1, source_target_pairs={{0,4},{1,5},{2,6},{3,7},{4,0},{5,1},{6,2},{7,3},{8,12},{9,13},{10,... | collective-permute-start | bytes 393224 | tf_op jit(solution)/shard_map/ppermute | solution.py:362
  9.4 21.1 %collective-permute-start.12 = (f32[2,32,512]{2,1,0:T(8,128)}, f32[2,32,512]{2,1,0:T(8,128)S(1)}, u32[]{:S(2)}, u32[]{:S(2)}) collective-permute-start(f32[2,32,512]{2,1,0:T(8,128)} %get-tuple-element.38), channel_id=1, source_target_pairs={{0,8},{1,9},{2,10},{3,11},{4,12},{5,13},{6,14},{7,15},{8,0},{9,1},... | collective-permute-start | bytes 393224 | tf_op jit(solution)/shard_map/ppermute | solution.py:362
  12.9 18.6 %collective-permute-start.13 = (f32[2,32,512]{2,1,0:T(8,128)}, f32[2,32,512]{2,1,0:T(8,128)S(1)}, u32[]{:S(2)}, u32[]{:S(2)}) collective-permute-start(f32[2,32,512]{2,1,0:T(8,128)} %get-tuple-element.38), channel_id=1, source_target_pairs={{0,12},{1,13},{2,14},{3,15},{4,8},{5,9},{6,10},{7,11},{8,4},{9,5},... | collective-permute-start | bytes 393224 | tf_op jit(solution)/shard_map/ppermute | solution.py:362
  20.0 37.9 %collective-permute-start.3 = (f32[4,2,32,512]{3,2,1,0:T(8,128)S(1)}, f32[4,2,32,512]{3,2,1,0:T(8,128)S(1)}, u32[]{:S(2)}, u32[]{:S(2)}) collective-permute-start(f32[4,2,32,512]{3,2,1,0:T(8,128)S(1)} %pad_maximum_fusion.r_2_), channel_id=1, source_target_pairs={{0,2},{1,3},{2,0},{3,1},{4,6},{5,7},{6,4},{7,5},{8,10},{9,11},{10,... | collective-permute-start | bytes 1572872 | tf_op jit(solution)/shard_map/ppermute | solution.py:362
  21.6 37.2 %collective-permute-start.4 = (f32[4,2,32,512]{3,2,1,0:T(8,128)S(1)}, f32[4,2,32,512]{3,2,1,0:T(8,128)S(1)}, u32[]{:S(2)}, u32[]{:S(2)}) collective-permute-start(f32[4,2,32,512]{3,2,1,0:T(8,128)S(1)} %pad_maximum_fusion.r_2_), channel_id=1, source_target_pairs={{0,1},{1,0},{2,3},{3,2},{4,5},{5,4},{6,7},{7,6},{8,9},{9,8},{10,11... | collective-permute-start | bytes 1572872 | tf_op jit(solution)/shard_map/ppermute | solution.py:362
  21.6 15.5 %collective-permute-start.22 = (f32[2,32,512]{2,1,0:T(8,128)}, f32[2,32,512]{2,1,0:T(8,128)S(1)}, u32[]{:S(2)}, u32[]{:S(2)}) collective-permute-start(f32[2,32,512]{2,1,0:T(8,128)} %get-tuple-element.45), channel_id=1, source_target_pairs={{0,4},{1,5},{2,6},{3,7},{4,0},{5,1},{6,2},{7,3},{8,12},{9,13},{10,... | collective-permute-start | bytes 393224 | tf_op jit(solution)/shard_map/ppermute | solution.py:362
  30.6 13.2 %collective-permute-start.23 = (f32[2,32,512]{2,1,0:T(8,128)}, f32[2,32,512]{2,1,0:T(8,128)S(1)}, u32[]{:S(2)}, u32[]{:S(2)}) collective-permute-start(f32[2,32,512]{2,1,0:T(8,128)} %get-tuple-element.45), channel_id=1, source_target_pairs={{0,8},{1,9},{2,10},{3,11},{4,12},{5,13},{6,14},{7,15},{8,0},{9,1},... | collective-permute-start | bytes 393224 | tf_op jit(solution)/shard_map/ppermute | solution.py:362
  31.5 12.3 %collective-permute-start.24 = (f32[2,32,512]{2,1,0:T(8,128)}, f32[2,32,512]{2,1,0:T(8,128)S(1)}, u32[]{:S(2)}, u32[]{:S(2)}) collective-permute-start(f32[2,32,512]{2,1,0:T(8,128)} %get-tuple-element.45), channel_id=1, source_target_pairs={{0,12},{1,13},{2,14},{3,15},{4,8},{5,9},{6,10},{7,11},{8,4},{9,5},... | collective-permute-start | bytes 393224 | tf_op jit(solution)/shard_map/ppermute | solution.py:362
  48.1 14.5 %collective-permute-start.14 = (f32[4,2,32,512]{3,2,1,0:T(8,128)S(1)}, f32[4,2,32,512]{3,2,1,0:T(8,128)}, u32[]{:S(2)}, u32[]{:S(2)}) collective-permute-start(f32[4,2,32,512]{3,2,1,0:T(8,128)S(1)} %pad_maximum_fusion.1.r_2_), channel_id=1, source_target_pairs={{0,2},{1,3},{2,0},{3,1},{4,6},{5,7},{6,4},{7,5},{8,10},{9,11},{10,... | collective-permute-start | bytes 1572872 | tf_op jit(solution)/shard_map/ppermute | solution.py:362
  55.0 18.9 %collective-permute-start.25 = (f32[4,2,32,512]{3,2,1,0:T(8,128)S(1)}, f32[4,2,32,512]{3,2,1,0:T(8,128)}, u32[]{:S(2)}, u32[]{:S(2)}) collective-permute-start(f32[4,2,32,512]{3,2,1,0:T(8,128)S(1)} %pad_maximum_fusion.2.r_2_), channel_id=1, source_target_pairs={{0,2},{1,3},{2,0},{3,1},{4,6},{5,7},{6,4},{7,5},{8,10},{9,11},{10,... | collective-permute-start | bytes 1572872 | tf_op jit(solution)/shard_map/ppermute | solution.py:362
  57.9 25.0 %collective-permute-start.36 = (f32[4,2,32,512]{3,2,1,0:T(8,128)}, f32[4,2,32,512]{3,2,1,0:T(8,128)}, u32[]{:S(2)}, u32[]{:S(2)}) collective-permute-start(f32[4,2,32,512]{3,2,1,0:T(8,128)} %pad_maximum_fusion.3.r_2_), channel_id=1, source_target_pairs={{0,2},{1,3},{2,0},{3,1},{4,6},{5,7},{6,4},{7,5},{8,10},{9,11},{10,... | collective-permute-start | bytes 1572872 | tf_op jit(solution)/shard_map/ppermute | solution.py:362
  59.6 23.3 %collective-permute-start.5 = (f32[4,2,32,512]{3,2,1,0:T(8,128)S(1)}, f32[4,2,32,512]{3,2,1,0:T(8,128)S(1)}, u32[]{:S(2)}, u32[]{:S(2)}) collective-permute-start(f32[4,2,32,512]{3,2,1,0:T(8,128)S(1)} %collective-permute-done.3.r_3_), channel_id=1, source_target_pairs={{0,1},{1,0},{2,3},{3,2},{4,5},{5,4},{6,7},{7,6},{8,9},{9,8},{10,11... | collective-permute-start | bytes 1572872 | tf_op jit(solution)/shard_map/ppermute | solution.py:362
  62.7 46.8 %collective-permute-start.16 = (f32[4,2,32,512]{3,2,1,0:T(8,128)}, f32[4,2,32,512]{3,2,1,0:T(8,128)}, u32[]{:S(2)}, u32[]{:S(2)}) collective-permute-start(f32[4,2,32,512]{3,2,1,0:T(8,128)} %collective-permute-done.14.r_3_), channel_id=1, source_target_pairs={{0,1},{1,0},{2,3},{3,2},{4,5},{5,4},{6,7},{7,6},{8,9},{9,8},{10,11... | collective-permute-start | bytes 1572872 | tf_op jit(solution)/shard_map/ppermute | solution.py:362
  63.5 57.4 %collective-permute-start.26 = (f32[4,2,32,512]{3,2,1,0:T(8,128)S(1)}, f32[4,2,32,512]{3,2,1,0:T(8,128)}, u32[]{:S(2)}, u32[]{:S(2)}) collective-permute-start(f32[4,2,32,512]{3,2,1,0:T(8,128)S(1)} %pad_maximum_fusion.2.r_2_), channel_id=1, source_target_pairs={{0,1},{1,0},{2,3},{3,2},{4,5},{5,4},{6,7},{7,6},{8,9},{9,8},{10,11... | collective-permute-start | bytes 1572872 | tf_op jit(solution)/shard_map/ppermute | solution.py:362
  73.9 47.0 %collective-permute-start.27 = (f32[4,2,32,512]{3,2,1,0:T(8,128)}, f32[4,2,32,512]{3,2,1,0:T(8,128)}, u32[]{:S(2)}, u32[]{:S(2)}) collective-permute-start(f32[4,2,32,512]{3,2,1,0:T(8,128)} %collective-permute-done.25.r_3_), channel_id=1, source_target_pairs={{0,1},{1,0},{2,3},{3,2},{4,5},{5,4},{6,7},{7,6},{8,9},{9,8},{10,11... | collective-permute-start | bytes 1572872 | tf_op jit(solution)/shard_map/ppermute | solution.py:362
  82.9 49.4 %collective-permute-start.37 = (f32[4,2,32,512]{3,2,1,0:T(8,128)}, f32[4,2,32,512]{3,2,1,0:T(8,128)}, u32[]{:S(2)}, u32[]{:S(2)}) collective-permute-start(f32[4,2,32,512]{3,2,1,0:T(8,128)} %pad_maximum_fusion.3.r_2_), channel_id=1, source_target_pairs={{0,1},{1,0},{2,3},{3,2},{4,5},{5,4},{6,7},{7,6},{8,9},{9,8},{10,11... | collective-permute-start | bytes 1572872 | tf_op jit(solution)/shard_map/ppermute | solution.py:362
  83.7 48.6 %collective-permute-start.38 = (f32[4,2,32,512]{3,2,1,0:T(8,128)}, f32[4,2,32,512]{3,2,1,0:T(8,128)}, u32[]{:S(2)}, u32[]{:S(2)}) collective-permute-start(f32[4,2,32,512]{3,2,1,0:T(8,128)} %collective-permute-done.36.r_3_), channel_id=1, source_target_pairs={{0,1},{1,0},{2,3},{3,2},{4,5},{5,4},{6,7},{7,6},{8,9},{9,8},{10,11... | collective-permute-start | bytes 1572872 | tf_op jit(solution)/shard_map/ppermute | solution.py:362
  146.5 14.4 %collective-permute-start.7 = (f32[4,32,512]{2,1,0:T(8,128)S(1)}, f32[4,32,512]{2,1,0:T(8,128)S(1)}, u32[]{:S(2)}, u32[]{:S(2)}) collective-permute-start(f32[4,32,512]{2,1,0:T(8,128)S(1)} %slice_add_fusion.3), channel_id=1, source_target_pairs={{0,2},{1,3},{2,0},{3,1},{4,6},{5,7},{6,4},{7,5},{8,10},{9,11},{10,... | collective-permute-start | bytes 786440 | tf_op jit(solution)/shard_map/ppermute | solution.py:362
  148.0 18.2 %collective-permute-start.18 = (f32[4,32,512]{2,1,0:T(8,128)S(1)}, f32[4,32,512]{2,1,0:T(8,128)S(1)}, u32[]{:S(2)}, u32[]{:S(2)}) collective-permute-start(f32[4,32,512]{2,1,0:T(8,128)S(1)} %slice_add_fusion.2), channel_id=1, source_target_pairs={{0,2},{1,3},{2,0},{3,1},{4,6},{5,7},{6,4},{7,5},{8,10},{9,11},{10,... | collective-permute-start | bytes 786440 | tf_op jit(solution)/shard_map/ppermute | solution.py:362
  148.8 22.7 %collective-permute-start.29 = (f32[4,32,512]{2,1,0:T(8,128)S(1)}, f32[4,32,512]{2,1,0:T(8,128)S(1)}, u32[]{:S(2)}, u32[]{:S(2)}) collective-permute-start(f32[4,32,512]{2,1,0:T(8,128)S(1)} %slice_add_fusion.1), channel_id=1, source_target_pairs={{0,2},{1,3},{2,0},{3,1},{4,6},{5,7},{6,4},{7,5},{8,10},{9,11},{10,... | collective-permute-start | bytes 786440 | tf_op jit(solution)/shard_map/ppermute | solution.py:362
  155.7 37.0 %collective-permute-start.41 = (f32[32,512]{1,0:T(8,128)S(1)}, f32[32,512]{1,0:T(8,128)S(1)}, u32[]{:S(2)}, u32[]{:S(2)}) collective-permute-start(f32[32,512]{1,0:T(8,128)S(1)} %get-tuple-element.61), channel_id=1, source_target_pairs={{0,4},{1,5},{2,6},{3,7},{4,0},{5,1},{6,2},{7,3},{8,12},{9,13},{10,... | collective-permute-start | bytes 196616 | tf_op jit(solution)/shard_map/ppermute | solution.py:362
  160.9 31.9 %collective-permute-start.42 = (f32[32,512]{1,0:T(8,128)S(1)}, f32[32,512]{1,0:T(8,128)S(1)}, u32[]{:S(2)}, u32[]{:S(2)}) collective-permute-start(f32[32,512]{1,0:T(8,128)S(1)} %get-tuple-element.60), channel_id=1, source_target_pairs={{0,8},{1,9},{2,10},{3,11},{4,12},{5,13},{6,14},{7,15},{8,0},{9,1},... | collective-permute-start | bytes 196616 | tf_op jit(solution)/shard_map/ppermute | solution.py:362
  161.0 15.3 %collective-permute-start.10 = (f32[32,512]{1,0:T(8,128)S(1)}, f32[32,512]{1,0:T(8,128)S(1)}, u32[]{:S(2)}, u32[]{:S(2)}) collective-permute-start(f32[32,512]{1,0:T(8,128)S(1)} %get-tuple-element.64), channel_id=1, source_target_pairs={{0,12},{1,13},{2,14},{3,15},{4,8},{5,9},{6,10},{7,11},{8,4},{9,5},... | collective-permute-start | bytes 196616 | tf_op jit(solution)/shard_map/ppermute | solution.py:362
  (36 other events, 324.7 us)
where the time goes:
time: 198 us; the launch traced here: 197 us
  starting transfers between devices  66.2 us (33%)
  Pallas kernels  62.2 us (31%)
  waiting for transfers between devices  55.8 us (28%)
  other arithmetic  7.17 us (4%)
  local copies, waits for them, and re-layouts  5.49 us (3%)
    ppermute x44, starting transfers between devices, swap(): return lax.ppermute(x, 'freq', [(i, i ^ mask) for i in range(n)])  66.2 us
    ppermute x44, waiting for transfers between devices, swap(): return lax.ppermute(x, 'freq', [(i, i ^ mask) for i in range(n)])  55.8 us
    pallas_call x4, Pallas kernels, first_call(): pl.pallas_call(lambda *r: first_kernel(dict(metas=metas, R=R), *r), out_s...  25.9 us
    pallas_call x4, Pallas kernels, second_call(): pl.pallas_call(lambda *r: second_kernel(dict(last=last, R=R), *r), out_sh...  19.9 us
    pallas_call x1, Pallas kernels, prep_fields(): pl.pallas_call(prep_fields_kernel, out_shape=jax.ShapeDtypeStruct(shape,...  11.3 us
    unnamed x32, local copies, waits for them, and re-layouts  5.49 us
    another operation x4, other arithmetic, exchange_path(): mine = jnp.stack(parts)  4.71 us
  transfers between devices with their start and end apart: 44, of which 15 were waited for; matrix products, arithmetic and copies ran while one was open for 4% of the time, Pallas kernels for 23%

commit v1 on v0

--- a/solution.py
+++ b/solution.py
@@ -10,7 +10,7 @@
 
 LANES = 128
 SUB = 8
-UP = 4
+UP = 8
 U0 = 2
 U1 = 8
 VLIM = 28 << 20
@@ -58,11 +58,8 @@
 
 
 def spread(parts):
-    nb, lane = len(parts), iotas()[1]
-    return [pick(parts, lane // (LANES // nb), (lane * nb + b) % LANES) for b in range(nb)]
-
-
-def spread4(parts):
+    if len(parts) != 4:
+        return spread_any(parts)
     lane = iotas()[1]
     w = LANES // 4
     index = (lane % w) * 4 + lane // w
@@ -81,97 +78,152 @@
     return out
 
 
+def spread_any(parts):
+    nb, lane = len(parts), iotas()[1]
+    return [pick(parts, lane // (LANES // nb), (lane * nb + b) % LANES) for b in range(nb)]
+
+
 def gather_back(parts):
     nb, lane = len(parts), iotas()[1]
     return [pick(parts, lane % nb, lane // nb + a * (LANES // nb)) for a in range(nb)]
 
 
-def prep_models_kernel(vel, ani, *outs):
-    depth, R, NY = vel.shape
+def spaces():
+    return [pl.BlockSpec(memory_space=s) for s in (pltpu.SMEM, pltpu.VMEM, pltpu.HBM)]
+
+
+def prep_models_kernel(depths, vel, ani, *refs):
+    outs, (buf, sem) = refs[: len(depths)], refs[len(depths) :]
+    _, R, NY = vel.shape
     nb = NY // LANES
-    for d in range(depth):
-        for m, ref in enumerate((vel, ani)):
+    copies = [
+        pltpu.make_async_copy(ref.at[d], buf.at[m, n], sem.at[m, n])
+        for n, d in enumerate(depths) for m, ref in enumerate((vel, ani))
+    ]
+    for c in copies:
+        c.start()
+    for n in range(len(depths)):
+        for m in range(2):
+            copies[2 * n + m].wait()
             for j in range(R // SUB):
                 rows = slice(j * SUB, (j + 1) * SUB)
-                new = spread([ref[d, rows, cut(b)] for b in range(nb)])
+                new = spread([buf[m, n, rows, cut(b)] for b in range(nb)])
                 for b in range(nb):
-                    outs[d][m, rows, cut(b)] = new[b]
-
-
-def prep_models(vel, ani):
-    depth, R, NY = vel.shape
+                    outs[n][m, rows, cut(b)] = new[b]
+
+
+def prep_models(vel, ani, depths):
+    _, R, NY = vel.shape
+    _, vmem, hbm = spaces()
     return pl.pallas_call(
-        prep_models_kernel, out_shape=[jax.ShapeDtypeStruct((2, R, NY), jnp.float32)] * depth, name="prep_models",
+        lambda *r: prep_models_kernel(depths, *r), out_shape=[jax.ShapeDtypeStruct((2, R, NY), jnp.float32)] * len(depths),
+        in_specs=[hbm, hbm], out_specs=[vmem] * len(depths),
+        scratch_shapes=[pltpu.VMEM((2, len(depths), R, NY), jnp.float32), pltpu.SemaphoreType.DMA((2, len(depths)))],
+        name="prep_models", compiler_params=pltpu.CompilerParams(vmem_limit_bytes=4 << 20),
     )(vel, ani)
 
 
-def prep_fields_kernel(where, src, rcv, out, buf, sem):
+def prep_field_kernel(p, sign, where, field, out, buf, sem):
     G, NY = out.shape[1], out.shape[3]
     nb = NY // LANES
-    chunks = 4
+    chunks = sem.shape[0]
     C = G // chunks
     copies = []
     for h in range(chunks):
         for k in range(SUB):
             row = pl.multiple_of((where[0] ^ off_of(k)) * G + h * C, SUB)
-            for a, ref in enumerate((src, rcv)):
-                for c in range(2):
-                    copies.append(pltpu.make_async_copy(
-                        ref.at[c, pl.ds(row, C), :], buf.at[2 * a + c, pl.ds(h * C, C), k, :], sem.at[h]))
+            for c in range(2):
+                copies.append(pltpu.make_async_copy(
+                    field.at[p, c, pl.ds(row, C), :], buf.at[c, pl.ds(h * C, C), k, :], sem.at[h]))
     for c in copies:
         c.start()
     for h in range(chunks):
-        for c in copies[h * SUB * 4 : (h + 1) * SUB * 4]:
+        for c in copies[h * SUB * 2 : (h + 1) * SUB * 2]:
             c.wait()
 
         def body(j, _):
             for q in range(UP):
                 i = j * UP + q
-                for a in range(4):
-                    new = spread4([buf[a, i, :, cut(b)] for b in range(nb)])
+                for a in range(2):
+                    new = spread([buf[a, i, :, cut(b)] for b in range(nb)])
                     for b in range(nb):
-                        out[a, i, :, cut(b)] = -new[b] if a == 3 else new[b]
+                        out[a, i, :, cut(b)] = sign * new[b] if a == 1 and sign < 0 else new[b]
             return 0
 
         lax.fori_loop(h * C // UP, (h + 1) * C // UP, body, 0)
 
 
-def prep_fields(where, src, rcv, G, NY):
-    shape = (4, G, SUB, NY)
-    smem, vmem, anym = (pl.BlockSpec(memory_space=s) for s in (pltpu.SMEM, pltpu.VMEM, pl.ANY))
+def prep_field(where, field, p, sign, G):
+    NY = field.shape[-1]
+    shape = (2, G, SUB, NY)
+    smem, vmem, hbm = spaces()
     return pl.pallas_call(
-        prep_fields_kernel, out_shape=jax.ShapeDtypeStruct(shape, jnp.float32), in_specs=[smem, anym, anym], out_specs=vmem,
-        scratch_shapes=[pltpu.VMEM(shape, jnp.float32), pltpu.SemaphoreType.DMA((4,))], name="prep_fields",
-        compiler_params=pltpu.CompilerParams(vmem_limit_bytes=16 << 20),
-    )(where, src, rcv)
-
-
-def finish_kernel(scale, early, *refs):
-    out = refs[-1]
-    depth, R, NY = out.shape
+        lambda *r: prep_field_kernel(p, sign, *r), out_shape=jax.ShapeDtypeStruct(shape, jnp.float32), in_specs=[smem, hbm], out_specs=vmem,
+        scratch_shapes=[pltpu.VMEM(shape, jnp.float32), pltpu.SemaphoreType.DMA((4,))], name="prep_field",
+        compiler_params=pltpu.CompilerParams(vmem_limit_bytes=12 << 20),
+    )(where, field)
+
+
+def finish_early_kernel(scale, early, out, buf, sem):
+    depth, R, NY = early.shape
     nb = NY // LANES
     for d in range(depth):
         for j in range(R // SUB):
             rows = slice(j * SUB, (j + 1) * SUB)
-            parts = []
+            new = gather_back([early[d, rows, cut(b)] * scale for b in range(nb)])
             for b in range(nb):
-                if d < depth - 1:
-                    parts.append(early[d, rows, cut(b)] * scale)
-                else:
-                    v = refs[0][rows, cut(b)]
-                    for r in refs[1:-1]:
-                        v = v + r[rows, cut(b)]
-                    parts.append(v * scale)
-            new = gather_back(parts)
-            for b in range(nb):
-                out[d, rows, cut(b)] = new[b]
-
-
-def finish(scale, early, tail):
+                buf[d, rows, cut(b)] = new[b]
+    copy = pltpu.make_async_copy(buf, out.at[pl.ds(0, depth)], sem)
+    copy.start()
+    copy.wait()
+
+
+def finish_early(scale, early):
     depth, R, NY = early.shape
+    _, vmem, hbm = spaces()
     return pl.pallas_call(
-        lambda *r: finish_kernel(scale, *r), out_shape=jax.ShapeDtypeStruct((depth + 1, R, NY), jnp.float32), name="finish",
-    )(early, *tail)
+        lambda *r: finish_early_kernel(scale, *r),
+        out_shape=jax.ShapeDtypeStruct((depth + 1, R, NY), jnp.float32), in_specs=[vmem], out_specs=hbm,
+        scratch_shapes=[pltpu.VMEM((depth, R, NY), jnp.float32), pltpu.SemaphoreType.DMA(())], name="finish_early",
+        compiler_params=pltpu.CompilerParams(vmem_limit_bytes=4 << 20),
+    )(early)
+
+
+def finish_last_kernel(scale, own, *refs):
+    far, (before, out, got, buf, sem, sem_o) = refs[:-6], refs[-6:]
+    R, NY = buf.shape
+    nb = NY // LANES
+    copies = [pltpu.make_async_copy(ref, got.at[n], sem.at[n]) for n, ref in enumerate((own, *far))]
+    for c in copies:
+        c.start()
+    for c in copies:
+        c.wait()
+    for j in range(R // SUB):
+        rows = slice(j * SUB, (j + 1) * SUB)
+        parts = []
+        for b in range(nb):
+            v = got[0, rows, cut(b)]
+            for n in range(1, got.shape[0]):
+                v = v + got[n, rows, cut(b)]
+            parts.append(v * scale)
+        new = gather_back(parts)
+        for b in range(nb):
+            buf[rows, cut(b)] = new[b]
+    last = pltpu.make_async_copy(buf, out.at[out.shape[0] - 1], sem_o)
+    last.start()
+    last.wait()
+
+
+def finish_last(scale, parts, before):
+    R, NY = parts[0].shape
+    _, _, hbm = spaces()
+    n = len(parts)
+    return pl.pallas_call(
+        lambda *r: finish_last_kernel(scale, *r), out_shape=jax.ShapeDtypeStruct(before.shape, jnp.float32),
+        in_specs=[hbm] * (n + 1), out_specs=hbm, input_output_aliases={n: 0},
+        scratch_shapes=[pltpu.VMEM((n, R, NY), jnp.float32), pltpu.VMEM((R, NY), jnp.float32), pltpu.SemaphoreType.DMA((n,)), pltpu.SemaphoreType.DMA(())],
+        name="finish_last", compiler_params=pltpu.CompilerParams(vmem_limit_bytes=4 << 20),
+    )(*parts, before)
 
 
 def wave_tools(where, G, NB):
@@ -219,7 +271,7 @@
 
 def first_kernel(cfg, where, om_ref, *refs):
     metas, R = cfg["metas"], cfg["R"]
-    blks, (cur, sh, e1, mod, sem_m) = refs[: len(metas)], refs[len(metas) :]
+    blks, (*cur, sh, e1, mod, sem_m) = refs[: len(metas)], refs[len(metas) :]
     G, NB = mod.shape[1], mod.shape[3] // LANES
     lo = where[1]
     bases = [lo * R, (1 - lo) * R][: G // R]
@@ -255,7 +307,7 @@
                 sn = ph * horner(SIN_C, z)
                 cs = horner(COS_C, z)
                 for f in range(2):
-                    re, im = cur[2 * f, i, :, cut(b)], cur[2 * f + 1, i, :, cut(b)]
+                    re, im = cur[f][0, i, :, cut(b)], cur[f][1, i, :, cut(b)]
                     sh[2 * f, i + 1, :, cut(b)] = re * cs - im * sn
                     sh[2 * f + 1, i + 1, :, cut(b)] = im * cs + re * sn
 
@@ -281,7 +333,7 @@
     outs, refs = refs[: G // R], list(refs[G // R :])
     lo = where[1]
     bases = [lo * R, (1 - lo) * R][: G // R]
-    st, (e2, img, sem_o, *keep) = (None, refs) if last else (refs[0], refs[1:])
+    st, (e2, img, sem_o, *keep) = (None, refs) if last else (refs[:2], refs[2:])
     halos, sweep = wave_tools(where, G, NB)
 
     def put2(f, q, i, o, mid):
@@ -301,11 +353,11 @@
                 total = (x + mid[c][b]) + e1[2 * f + c, i + 1, :, cut(b)]
                 new.append(sh[2 * f + c, i + 1, :, cut(b)] + (total + total))
                 if not last:
-                    st[2 * f + c, i, :, cut(b)] = new[c]
+                    st[f][c, i, :, cut(b)] = new[c]
                 elif f == 0:
                     keep[0][c, q, :, cut(b)] = new[c]
             if f == 1:
-                sr, si = (keep[0][c, q, :, cut(b)] if last else st[c, i, :, cut(b)] for c in range(2))
+                sr, si = (keep[0][c, q, :, cut(b)] if last else st[0][c, i, :, cut(b)] for c in range(2))
                 img[i, :, cut(b)] = sr * new[0] - si * new[1]
 
     out_copies = []
@@ -319,20 +371,16 @@
         c.wait()
 
 
-def spaces():
-    return [pl.BlockSpec(memory_space=s) for s in (pltpu.SMEM, pltpu.VMEM, pl.ANY)]
-
-
 def first_call(where, omega, blocks, metas, state, R):
-    _, G, _, NY = state.shape
+    _, G, _, NY = state[0].shape
     smem, vmem, anym = spaces()
     pad = jax.ShapeDtypeStruct((4, G + 2, SUB, NY), jnp.float32)
     return pl.pallas_call(
         lambda *r: first_kernel(dict(metas=metas, R=R), *r), out_shape=[pad, pad, jax.ShapeDtypeStruct((2, G, SUB, NY), jnp.float32)],
-        in_specs=[smem, smem] + [anym] * len(blocks) + [vmem], out_specs=[vmem] * 3,
+        in_specs=[smem, smem] + [anym] * len(blocks) + [vmem] * 2, out_specs=[vmem] * 3,
         scratch_shapes=[pltpu.SemaphoreType.DMA((G // R,))], name="first_half",
         compiler_params=pltpu.CompilerParams(vmem_limit_bytes=VLIM),
-    )(where, omega, *blocks, state)
+    )(where, omega, *blocks, *state)
 
 
 def second_call(where, sh, e1, mod, last, R):
@@ -341,8 +389,8 @@
     out_shape = [jax.ShapeDtypeStruct((SUB, R, NY), jnp.float32)] * (G // R)
     out_specs = [anym] * (G // R)
     if not last:
-        out_shape.append(jax.ShapeDtypeStruct((4, G, SUB, NY), jnp.float32))
-        out_specs.append(vmem)
+        out_shape += [jax.ShapeDtypeStruct((2, G, SUB, NY), jnp.float32)] * 2
+        out_specs += [vmem] * 2
     scratch = [pltpu.VMEM((4, G + 2, SUB, NY), jnp.float32), pltpu.VMEM((G, SUB, NY), jnp.float32), pltpu.SemaphoreType.DMA(())]
     if last:
         scratch.append(pltpu.VMEM((2, U1, SUB, NY), jnp.float32))
@@ -364,33 +412,36 @@
 
 def exchange_path(source, receiver, velocity, anisotropy, omega, scale):
     me = lax.axis_index("freq")
-    depth_count, R, NY = velocity.shape
+    depth_count, R, _ = velocity.shape
     G = R * lax.axis_size("freq") // SUB
     where = jnp.stack([me >> 1, me & 1]).astype(jnp.int32)
-    own = prep_models(velocity, anisotropy)
-    states = [prep_fields(where, source[p], receiver[p], G, NY) for p in range(source.shape[0])]
+    own = list(prep_models(velocity, anisotropy, (0,)))
+    own += prep_models(velocity, anisotropy, tuple(range(1, depth_count)))
+    state = [prep_field(where, source, 0, 1.0, G)]
+    state.append(prep_field(where, receiver, 0, -1.0, G))
     metas = [(0, HALF, 0), (HALF, HALF, 0), (0, HALF, 1), (HALF, HALF, 1)]
-    layers = []
+    early = []
     for d in range(depth_count):
         last = d == depth_count - 1
         parts = [own[d]] + [swap(own[d], far << 2) for far in range(1, HALF)]
         mine = jnp.stack(parts)
         near = swap(mine, 2)
         blocks = [mine, near, swap(mine, 1), swap(near, 1)]
-        total = None
-        for p, state in enumerate(states):
-            mid = first_call(where, omega[p : p + 1], blocks, metas, state, R)
-            res = second_call(where, *mid, last, R)
-            total = res[:2] if total is None else [a + b for a, b in zip(total, res[:2])]
-            states[p] = None if last else res[2]
-        kept, sent = total
+        mid = first_call(where, omega, blocks, metas, state, R)
+        kept, sent, *state = second_call(where, *mid, last, R)
         got = swap(sent, 1)
         upper = kept[HALF:] + got[HALF:]
         near = swap(upper, 2)
-        parts = [(kept[far] + got[far]) + near[far] for far in range(HALF)]
-        parts = [parts[0]] + [swap(parts[far], far << 2) for far in range(1, HALF)]
-        layers.append(parts if last else sum(parts[1:], parts[0]))
-    return finish(scale, jnp.stack(layers[:-1]), layers[-1])
+        if not last:
+            early.append((kept, got, near))
+        if d == depth_count - 2:
+            parts = [jnp.stack([(k[far] + g[far]) + n[far] for k, g, n in early]) for far in range(HALF)]
+            parts = [parts[0]] + [swap(parts[far], far << 2) for far in range(1, HALF)]
+            before = finish_early(scale, sum(parts[1:], parts[0]))
+        if last:
+            parts = [(kept[far] + got[far]) + near[far] for far in range(HALF)]
+            parts = [parts[0]] + [swap(parts[far], far << 2) for far in range(1, HALF)]
+            return finish_last(scale, parts, before)
 
 
 def apart(x):
@@ -413,7 +464,7 @@
     both = both.reshape(depth_count, 2, SUB, G, NY)
     both = jnp.stack([both[:, :, g] for g in places], axis=1)
     where = jnp.zeros((2,), jnp.int32)
-    states = [prep_fields(where, source[p], receiver[p], G, NY) for p in range(source.shape[0])]
+    states = [[prep_field(where, source, p, 1.0, G), prep_field(where, receiver, p, -1.0, G)] for p in range(source.shape[0])]
     layers = []
     for d in range(depth_count):
         total = None
@@ -422,7 +473,7 @@
             mid = first_call(where, omega[p : p + 1], [both[d]], [(0, SUB, 0)], state, G)
             res = second_call(where, *mid, last, G)
             total = res[0] if total is None else total + res[0]
-            states[p] = None if last else res[1]
+            states[p] = None if last else res[1:]
         whole = jnp.concatenate([total[k] for k in back], axis=0)
         layers.append(lax.psum_scatter(whole, "freq", scatter_dimension=0, tiled=True))
     return together(jnp.stack(layers)) * scale

time: 198 us -> 180 us (0.909)
  starting transfers between devices: 66.2 us -> 46.9 us
  waiting for transfers between devices: 55.8 us -> 64.5 us
  other arithmetic: 7.17 us -> 2.15 us
    ppermute x44 -> x38, starting transfers between devices: 66.2 us -> 46.9 us  [swap(): return lax.ppermute(x, 'freq', [(i, i ^ mask) for i in range(n)])]
    ppermute x44 -> x38, waiting for transfers between devices: 55.8 us -> 64.5 us  [swap(): return lax.ppermute(x, 'freq', [(i, i ^ mask) for i in range(n)])]
    another operation x4, other arithmetic: 4.71 us -> 0.96 us  [exchange_path(): mine = jnp.stack(parts)]
    unnamed x32 -> x22, local copies, waits for them, and re-layouts: 5.49 us -> 3.53 us
    pallas_call x3 -> x6, Pallas kernels: 16.5 us -> 16.6 us  [the longest x2 11.7 us: prep_field(): pl.pallas_call(lambda *r: prep_field_kernel(p, sign, *r), out_shape=jax.S...]
  transfers between devices with their start and end apart: 44 -> 38, of which waited for: 15 -> 14; matrix products, arithmetic and copies ran while one was open for 4% -> 1% of each run, Pallas kernels for 23% -> 34%
where the time goes in v1:
time: 180 us; the launch traced here: 179 us
  waiting for transfers between devices  64.5 us (36%)
  Pallas kernels  61.9 us (34%)
  starting transfers between devices  46.9 us (26%)
  local copies, waits for them, and re-layouts  3.53 us (2%)
  other arithmetic  2.15 us (1%)
    ppermute x38, waiting for transfers between devices, swap(): return lax.ppermute(x, 'freq', [(i, i ^ mask) for i in range(n)])  64.5 us
    ppermute x38, starting transfers between devices, swap(): return lax.ppermute(x, 'freq', [(i, i ^ mask) for i in range(n)])  46.9 us
    pallas_call x4, Pallas kernels, first_call(): pl.pallas_call(lambda *r: first_kernel(dict(metas=metas, R=R), *r), out_s...  25.5 us
    pallas_call x4, Pallas kernels, second_call(): pl.pallas_call(lambda *r: second_kernel(dict(last=last, R=R), *r), out_sh...  19.8 us
    pallas_call x2, Pallas kernels, prep_field(): pl.pallas_call(lambda *r: prep_field_kernel(p, sign, *r), out_shape=jax.S...  11.7 us
  transfers between devices with their start and end apart: 38, of which 14 were waited for; matrix products, arithmetic and copies ran while one was open for 1% of the time, Pallas kernels for 34%

profile of v1, /device:TPU:0, one launch (start us, length us, event | category | flops | bytes accessed | tf_op | source)
XLA Modules:
  0.0 179.4 jit_solution(14151373246695662240)
XLA Ops:
  11.1 3.5 %collective-permute-start.13 = (f32[2,32,512]{2,1,0:T(8,128)S(1)}, f32[2,32,512]{2,1,0:T(8,128)S(1)}, u32[]{:S(2)}, u32[]{:S(2)}) collective-permute-start(f32[2,32,512]{2,1,0:T(8,128)S(1)} %get-tuple-element.36), channel_id=1, source_target_pairs={{0,8},{1,9},{2,10},{3,11},{4,12},{5,13},{6,14},{7,15},{8,0},{9,1},... | collective-permute-start | bytes 393224 | tf_op jit(solution)/shard_map/ppermute | solution.py:410
  14.6 3.9 %collective-permute-done.19 = f32[2,32,512]{2,1,0:T(8,128)S(1)} collective-permute-done((f32[2,32,512]{2,1,0:T(8,128)S(1)}, f32[2,32,512]{2,1,0:T(8,128)S(1)}, u32[]{:S(2)}, u32[]{:S(2)}) %collective-permute-start.19) | collective-permute-done | bytes 131104 | tf_op jit(solution)/shard_map/ppermute | solution.py:410
  18.5 9.8 %collective-permute-start.7 = (f32[2,32,512]{2,1,0:T(8,128)S(1)}, f32[2,32,512]{2,1,0:T(8,128)S(1)}, u32[]{:S(2)}, u32[]{:S(2)}) collective-permute-start(f32[2,32,512]{2,1,0:T(8,128)S(1)} %get-tuple-element.35), channel_id=1, source_target_pairs={{0,8},{1,9},{2,10},{3,11},{4,12},{5,13},{6,14},{7,15},{8,0},{9,1},... | collective-permute-start | bytes 393224 | tf_op jit(solution)/shard_map/ppermute | solution.py:410
  41.0 3.2 %collective-permute-start.1 = (f32[2,32,512]{2,1,0:T(8,128)S(1)}, f32[2,32,512]{2,1,0:T(8,128)S(1)}, u32[]{:S(2)}, u32[]{:S(2)}) collective-permute-start(f32[2,32,512]{2,1,0:T(8,128)S(1)} %get-tuple-element.34), channel_id=1, source_target_pairs={{0,8},{1,9},{2,10},{3,11},{4,12},{5,13},{6,14},{7,15},{8,0},{9,1},... | collective-permute-start | bytes 393224 | tf_op jit(solution)/shard_map/ppermute | solution.py:410
  44.3 6.1 %collective-permute-done.1 = f32[2,32,512]{2,1,0:T(8,128)S(1)} collective-permute-done((f32[2,32,512]{2,1,0:T(8,128)S(1)}, f32[2,32,512]{2,1,0:T(8,128)S(1)}, u32[]{:S(2)}, u32[]{:S(2)}) %collective-permute-start.1) | collective-permute-done | bytes 131104 | tf_op jit(solution)/shard_map/ppermute | solution.py:410
  52.9 4.2 %collective-permute-done.2 = f32[2,32,512]{2,1,0:T(8,128)S(1)} collective-permute-done((f32[2,32,512]{2,1,0:T(8,128)S(1)}, f32[2,32,512]{2,1,0:T(8,128)S(1)}, u32[]{:S(2)}, u32[]{:S(2)}) %collective-permute-start.2) | collective-permute-done | bytes 131104 | tf_op jit(solution)/shard_map/ppermute | solution.py:410
  62.0 10.2 %collective-permute-done.9.r_3_ = f32[4,2,32,512]{3,2,1,0:T(8,128)} collective-permute-done((f32[4,2,32,512]{3,2,1,0:T(8,128)}, f32[4,2,32,512]{3,2,1,0:T(8,128)}, u32[]{:S(2)}, u32[]{:S(2)}) %collective-permute-start.9) | collective-permute-done | bytes 524320 | tf_op jit(solution)/shard_map/ppermute | solution.py:410
  72.3 5.9 %prep_field.2.r_6_ = f32[2,64,8,512]{3,2,1,0:T(8,128)S(1)} custom-call(s32[2]{0:T(128)S(1)} %pad_add_fusion.r_0_, f32[1,2,512,512]{3,2,1,0:T(8,128)S(1)} %copy-done), custom_call_target="tpu_custom_call" | custom-call | tf_op jit(solution)/shard_map/prep_field/pallas_call | solution.py:160
  81.1 5.9 %prep_field.3.r_7_ = f32[2,64,8,512]{3,2,1,0:T(8,128)S(1)} custom-call(s32[2]{0:T(128)S(1)} %pad_add_fusion.r_0_, f32[1,2,512,512]{3,2,1,0:T(8,128)S(1)} %copy-done.1), custom_call_target="tpu_custom_call" | custom-call | tf_op jit(solution)/shard_map/prep_field/pallas_call | solution.py:160
  87.0 6.4 %first_half.4 = (f32[4,66,8,512]{3,2,1,0:T(8,128)S(1)}, f32[4,66,8,512]{3,2,1,0:T(8,128)S(1)}, f32[2,64,8,512]{3,2,1,0:T(8,128)S(1)}) custom-call(s32[2]{0:T(128)S(1)} %pad_add_fusion.r_0_, f32[1]{0:T(128)} %bitcast.4.r_1_, f32[4,2,32,512]{3,2,1,0:T(8,128)S(1)} %copy-done.3, f32[4,2,32,512]{3,2,1,0:T(8,128)} %collective-permute-done.21.r_3_, ...), custom_call_target="tpu_custom_call" | custom-call | tf_op jit(solution)/shard_map/first_half/pallas_call | solution.py:378
  93.5 4.9 %second_half.4 = (f32[8,32,512]{2,1,0:T(8,128)S(1)}, f32[8,32,512]{2,1,0:T(8,128)S(1)}, f32[2,64,8,512]{3,2,1,0:T(8,128)S(1)}, f32[2,64,8,512]{3,2,1,0:T(8,128)S(1)}) custom-call(s32[2]{0:T(128)S(1)} %pad_add_fusion.r_0_, f32[4,66,8,512]{3,2,1,0:T(8,128)S(1)} %get-tuple-element.37.r_1_, f32[4,66,8,512]{3,2,1,0:T(8,128)S(1)} %get-tuple-element.38.r_2_, ...), custom_call_target="tpu_custom_call" | custom-call | tf_op jit(solution)/shard_map/second_half/pallas_call | solution.py:397
  98.5 6.4 %first_half.5 = (f32[4,66,8,512]{3,2,1,0:T(8,128)S(1)}, f32[4,66,8,512]{3,2,1,0:T(8,128)S(1)}, f32[2,64,8,512]{3,2,1,0:T(8,128)S(1)}) custom-call(s32[2]{0:T(128)S(1)} %pad_add_fusion.r_0_, f32[1]{0:T(128)} %bitcast.4.r_1_, f32[4,2,32,512]{3,2,1,0:T(8,128)S(1)} %pad_maximum_fusion.2.r_2_, f32[4,2,32,512]{3,2,1,0:T(8,128)} %collective-permute-done.15.r_3_, ...), custom_call_target="tpu_custom_call" | custom-call | tf_op jit(solution)/shard_map/first_half/pallas_call | solution.py:378
  104.9 5.1 %second_half.5 = (f32[8,32,512]{2,1,0:T(8,128)S(1)}, f32[8,32,512]{2,1,0:T(8,128)S(1)}, f32[2,64,8,512]{3,2,1,0:T(8,128)S(1)}, f32[2,64,8,512]{3,2,1,0:T(8,128)S(1)}) custom-call(s32[2]{0:T(128)S(1)} %pad_add_fusion.r_0_, f32[4,66,8,512]{3,2,1,0:T(8,128)S(1)} %get-tuple-element.42.r_1_, f32[4,66,8,512]{3,2,1,0:T(8,128)S(1)} %get-tuple-element.43.r_2_, ...), custom_call_target="tpu_custom_call" | custom-call | tf_op jit(solution)/shard_map/second_half/pallas_call | solution.py:397
  110.6 6.2 %first_half.6 = (f32[4,66,8,512]{3,2,1,0:T(8,128)S(1)}, f32[4,66,8,512]{3,2,1,0:T(8,128)S(1)}, f32[2,64,8,512]{3,2,1,0:T(8,128)S(1)}) custom-call(s32[2]{0:T(128)S(1)} %pad_add_fusion.r_0_, f32[1]{0:T(128)} %bitcast.4.r_1_, f32[4,2,32,512]{3,2,1,0:T(8,128)} %pad_maximum_fusion.1.r_2_, f32[4,2,32,512]{3,2,1,0:T(8,128)} %collective-permute-done.9.r_3_, ...), custom_call_target="tpu_custom_call" | custom-call | tf_op jit(solution)/shard_map/first_half/pallas_call | solution.py:378
  116.8 4.9 %second_half.6 = (f32[8,32,512]{2,1,0:T(8,128)S(1)}, f32[8,32,512]{2,1,0:T(8,128)S(1)}, f32[2,64,8,512]{3,2,1,0:T(8,128)S(1)}, f32[2,64,8,512]{3,2,1,0:T(8,128)S(1)}) custom-call(s32[2]{0:T(128)S(1)} %pad_add_fusion.r_0_, f32[4,66,8,512]{3,2,1,0:T(8,128)S(1)} %get-tuple-element.47.r_1_, f32[4,66,8,512]{3,2,1,0:T(8,128)S(1)} %get-tuple-element.48.r_2_, ...), custom_call_target="tpu_custom_call" | custom-call | tf_op jit(solution)/shard_map/second_half/pallas_call | solution.py:397
  121.8 6.4 %first_half.7 = (f32[4,66,8,512]{3,2,1,0:T(8,128)S(1)}, f32[4,66,8,512]{3,2,1,0:T(8,128)S(1)}, f32[2,64,8,512]{3,2,1,0:T(8,128)S(1)}) custom-call(s32[2]{0:T(128)S(1)} %pad_add_fusion.r_0_, f32[1]{0:T(128)} %bitcast.4.r_1_, f32[4,2,32,512]{3,2,1,0:T(8,128)S(1)} %pad_maximum_fusion.r_2_, f32[4,2,32,512]{3,2,1,0:T(8,128)} %collective-permute-done.3.r_3_, ...), custom_call_target="tpu_custom_call" | custom-call | tf_op jit(solution)/shard_map/first_half/pallas_call | solution.py:378
  128.2 4.9 %second_half.7 = (f32[8,32,512]{2,1,0:T(8,128)S(1)}, f32[8,32,512]{2,1,0:T(8,128)S(1)}) custom-call(s32[2]{0:T(128)S(1)} %pad_add_fusion.r_0_, f32[4,66,8,512]{3,2,1,0:T(8,128)S(1)} %get-tuple-element.52.r_1_, f32[4,66,8,512]{3,2,1,0:T(8,128)S(1)} %get-tuple-element.53.r_2_, f32[2,64,8,512]{3,2,1,0:T(8,128)S(1)} %get-tuple-element.54.r_3_), custom_call_target="tpu_custom_call" | custom-call | tf_op jit(solution)/shard_map/second_half/pallas_call | solution.py:397
  138.2 4.8 %collective-permute-done.30 = f32[4,32,512]{2,1,0:T(8,128)S(1)} collective-permute-done((f32[4,32,512]{2,1,0:T(8,128)S(1)}, f32[4,32,512]{2,1,0:T(8,128)S(1)}, u32[]{:S(2)}, u32[]{:S(2)}) %collective-permute-start.30) | collective-permute-done | bytes 262176 | tf_op jit(solution)/shard_map/ppermute | solution.py:410
  143.1 5.5 %collective-permute-done.32 = f32[4,32,512]{2,1,0:T(8,128)S(1)} collective-permute-done((f32[4,32,512]{2,1,0:T(8,128)S(1)}, f32[4,32,512]{2,1,0:T(8,128)S(1)}, u32[]{:S(2)}, u32[]{:S(2)}) %collective-permute-start.32) | collective-permute-done | bytes 262176 | tf_op jit(solution)/shard_map/ppermute | solution.py:410
  148.7 5.5 %collective-permute-done.34 = f32[4,32,512]{2,1,0:T(8,128)S(1)} collective-permute-done((f32[4,32,512]{2,1,0:T(8,128)S(1)}, f32[4,32,512]{2,1,0:T(8,128)S(1)}, u32[]{:S(2)}, u32[]{:S(2)}) %collective-permute-start.34) | collective-permute-done | bytes 262176 | tf_op jit(solution)/shard_map/ppermute | solution.py:410
  155.5 3.5 %collective-permute-start.37 = (f32[3,32,512]{2,1,0:T(8,128)S(1)}, f32[3,32,512]{2,1,0:T(8,128)S(1)}, u32[]{:S(2)}, u32[]{:S(2)}) collective-permute-start(f32[3,32,512]{2,1,0:T(8,128)S(1)} %pad_maximum_fusion.6), channel_id=1, source_target_pairs={{0,12},{1,13},{2,14},{3,15},{4,8},{5,9},{6,10},{7,11},{8,4},{9,5},... | collective-permute-start | bytes 589832 | tf_op jit(solution)/shard_map/ppermute | solution.py:410
  160.0 4.0 %collective-permute-done.35 = f32[3,32,512]{2,1,0:T(8,128)S(1)} collective-permute-done((f32[3,32,512]{2,1,0:T(8,128)S(1)}, f32[3,32,512]{2,1,0:T(8,128)S(1)}, u32[]{:S(2)}, u32[]{:S(2)}) %collective-permute-start.35) | collective-permute-done | bytes 196640 | tf_op jit(solution)/shard_map/ppermute | solution.py:410
  164.0 9.6 %collective-permute-done.36 = f32[3,32,512]{2,1,0:T(8,128)S(1)} collective-permute-done((f32[3,32,512]{2,1,0:T(8,128)S(1)}, f32[3,32,512]{2,1,0:T(8,128)S(1)}, u32[]{:S(2)}, u32[]{:S(2)}) %collective-permute-start.36) | collective-permute-done | bytes 196640 | tf_op jit(solution)/shard_map/ppermute | solution.py:410
  174.8 3.2 %collective-permute-done.27.r_2_ = f32[32,512]{1,0:T(8,128)S(1)} collective-permute-done((f32[32,512]{1,0:T(8,128)S(1)}, f32[32,512]{1,0:T(8,128)S(1)}, u32[]{:S(2)}, u32[]{:S(2)}) %collective-permute-start.27) | collective-permute-done | bytes 65568 | tf_op jit(solution)/shard_map/ppermute | solution.py:410
  (106 shorter events, 44.7 us)
Async XLA Ops:
  10.1 18.3 %collective-permute-start.12 = (f32[2,32,512]{2,1,0:T(8,128)S(1)}, f32[2,32,512]{2,1,0:T(8,128)S(1)}, u32[]{:S(2)}, u32[]{:S(2)}) collective-permute-start(f32[2,32,512]{2,1,0:T(8,128)S(1)} %get-tuple-element.36), channel_id=1, source_target_pairs={{0,4},{1,5},{2,6},{3,7},{4,0},{5,1},{6,2},{7,3},{8,12},{9,13},{10,... | collective-permute-start | bytes 393224 | tf_op jit(solution)/shard_map/ppermute | solution.py:410
  11.1 20.1 %collective-permute-start.13 = (f32[2,32,512]{2,1,0:T(8,128)S(1)}, f32[2,32,512]{2,1,0:T(8,128)S(1)}, u32[]{:S(2)}, u32[]{:S(2)}) collective-permute-start(f32[2,32,512]{2,1,0:T(8,128)S(1)} %get-tuple-element.36), channel_id=1, source_target_pairs={{0,8},{1,9},{2,10},{3,11},{4,12},{5,13},{6,14},{7,15},{8,0},{9,1},... | collective-permute-start | bytes 393224 | tf_op jit(solution)/shard_map/ppermute | solution.py:410
  14.6 16.6 %collective-permute-start.14 = (f32[2,32,512]{2,1,0:T(8,128)S(1)}, f32[2,32,512]{2,1,0:T(8,128)S(1)}, u32[]{:S(2)}, u32[]{:S(2)}) collective-permute-start(f32[2,32,512]{2,1,0:T(8,128)S(1)} %get-tuple-element.36), channel_id=1, source_target_pairs={{0,12},{1,13},{2,14},{3,15},{4,8},{5,9},{6,10},{7,11},{8,4},{9,5},... | collective-permute-start | bytes 393224 | tf_op jit(solution)/shard_map/ppermute | solution.py:410
  18.5 18.3 %collective-permute-start.7 = (f32[2,32,512]{2,1,0:T(8,128)S(1)}, f32[2,32,512]{2,1,0:T(8,128)S(1)}, u32[]{:S(2)}, u32[]{:S(2)}) collective-permute-start(f32[2,32,512]{2,1,0:T(8,128)S(1)} %get-tuple-element.35), channel_id=1, source_target_pairs={{0,8},{1,9},{2,10},{3,11},{4,12},{5,13},{6,14},{7,15},{8,0},{9,1},... | collective-permute-start | bytes 393224 | tf_op jit(solution)/shard_map/ppermute | solution.py:410
  28.4 29.8 %collective-permute-start.21 = (f32[4,2,32,512]{3,2,1,0:T(8,128)S(1)}, f32[4,2,32,512]{3,2,1,0:T(8,128)}, u32[]{:S(2)}, u32[]{:S(2)}) collective-permute-start(f32[4,2,32,512]{3,2,1,0:T(8,128)S(1)} %pad_maximum_fusion.3.r_2_), channel_id=1, source_target_pairs={{0,2},{1,3},{2,0},{3,1},{4,6},{5,7},{6,4},{7,5},{8,10},{9,11},{10,... | collective-permute-start | bytes 1572872 | tf_op jit(solution)/shard_map/ppermute | solution.py:410
  31.2 28.1 %collective-permute-start.22 = (f32[4,2,32,512]{3,2,1,0:T(8,128)S(1)}, f32[4,2,32,512]{3,2,1,0:T(8,128)S(1)}, u32[]{:S(2)}, u32[]{:S(2)}) collective-permute-start(f32[4,2,32,512]{3,2,1,0:T(8,128)S(1)} %pad_maximum_fusion.3.r_2_), channel_id=1, source_target_pairs={{0,1},{1,0},{2,3},{3,2},{4,5},{5,4},{6,7},{7,6},{8,9},{9,8},{10,11... | collective-permute-start | bytes 1572872 | tf_op jit(solution)/shard_map/ppermute | solution.py:410
  31.2 28.8 %collective-permute-start.15 = (f32[4,2,32,512]{3,2,1,0:T(8,128)S(1)}, f32[4,2,32,512]{3,2,1,0:T(8,128)}, u32[]{:S(2)}, u32[]{:S(2)}) collective-permute-start(f32[4,2,32,512]{3,2,1,0:T(8,128)S(1)} %pad_maximum_fusion.2.r_2_), channel_id=1, source_target_pairs={{0,2},{1,3},{2,0},{3,1},{4,6},{5,7},{6,4},{7,5},{8,10},{9,11},{10,... | collective-permute-start | bytes 1572872 | tf_op jit(solution)/shard_map/ppermute | solution.py:410
  44.2 16.3 %collective-permute-start.16 = (f32[4,2,32,512]{3,2,1,0:T(8,128)S(1)}, f32[4,2,32,512]{3,2,1,0:T(8,128)S(1)}, u32[]{:S(2)}, u32[]{:S(2)}) collective-permute-start(f32[4,2,32,512]{3,2,1,0:T(8,128)S(1)} %pad_maximum_fusion.2.r_2_), channel_id=1, source_target_pairs={{0,1},{1,0},{2,3},{3,2},{4,5},{5,4},{6,7},{7,6},{8,9},{9,8},{10,11... | collective-permute-start | bytes 1572872 | tf_op jit(solution)/shard_map/ppermute | solution.py:410
  57.1 15.1 %collective-permute-start.9 = (f32[4,2,32,512]{3,2,1,0:T(8,128)}, f32[4,2,32,512]{3,2,1,0:T(8,128)}, u32[]{:S(2)}, u32[]{:S(2)}) collective-permute-start(f32[4,2,32,512]{3,2,1,0:T(8,128)} %pad_maximum_fusion.1.r_2_), channel_id=1, source_target_pairs={{0,2},{1,3},{2,0},{3,1},{4,6},{5,7},{6,4},{7,5},{8,10},{9,11},{10,... | collective-permute-start | bytes 1572872 | tf_op jit(solution)/shard_map/ppermute | solution.py:410
  58.3 22.3 %collective-permute-start.3 = (f32[4,2,32,512]{3,2,1,0:T(8,128)S(1)}, f32[4,2,32,512]{3,2,1,0:T(8,128)}, u32[]{:S(2)}, u32[]{:S(2)}) collective-permute-start(f32[4,2,32,512]{3,2,1,0:T(8,128)S(1)} %pad_maximum_fusion.r_2_), channel_id=1, source_target_pairs={{0,2},{1,3},{2,0},{3,1},{4,6},{5,7},{6,4},{7,5},{8,10},{9,11},{10,... | collective-permute-start | bytes 1572872 | tf_op jit(solution)/shard_map/ppermute | solution.py:410
  60.0 20.6 %collective-permute-start.23 = (f32[4,2,32,512]{3,2,1,0:T(8,128)}, f32[4,2,32,512]{3,2,1,0:T(8,128)}, u32[]{:S(2)}, u32[]{:S(2)}) collective-permute-start(f32[4,2,32,512]{3,2,1,0:T(8,128)} %collective-permute-done.21.r_3_), channel_id=1, source_target_pairs={{0,1},{1,0},{2,3},{3,2},{4,5},{5,4},{6,7},{7,6},{8,9},{9,8},{10,11... | collective-permute-start | bytes 1572872 | tf_op jit(solution)/shard_map/ppermute | solution.py:410
  60.0 38.3 %collective-permute-start.17 = (f32[4,2,32,512]{3,2,1,0:T(8,128)}, f32[4,2,32,512]{3,2,1,0:T(8,128)}, u32[]{:S(2)}, u32[]{:S(2)}) collective-permute-start(f32[4,2,32,512]{3,2,1,0:T(8,128)} %collective-permute-done.15.r_3_), channel_id=1, source_target_pairs={{0,1},{1,0},{2,3},{3,2},{4,5},{5,4},{6,7},{7,6},{8,9},{9,8},{10,11... | collective-permute-start | bytes 1572872 | tf_op jit(solution)/shard_map/ppermute | solution.py:410
  61.3 48.7 %collective-permute-start.10 = (f32[4,2,32,512]{3,2,1,0:T(8,128)}, f32[4,2,32,512]{3,2,1,0:T(8,128)}, u32[]{:S(2)}, u32[]{:S(2)}) collective-permute-start(f32[4,2,32,512]{3,2,1,0:T(8,128)} %pad_maximum_fusion.1.r_2_), channel_id=1, source_target_pairs={{0,1},{1,0},{2,3},{3,2},{4,5},{5,4},{6,7},{7,6},{8,9},{9,8},{10,11... | collective-permute-start | bytes 1572872 | tf_op jit(solution)/shard_map/ppermute | solution.py:410
  72.2 38.4 %collective-permute-start.11 = (f32[4,2,32,512]{3,2,1,0:T(8,128)}, f32[4,2,32,512]{3,2,1,0:T(8,128)S(1)}, u32[]{:S(2)}, u32[]{:S(2)}) collective-permute-start(f32[4,2,32,512]{3,2,1,0:T(8,128)} %collective-permute-done.9.r_3_), channel_id=1, source_target_pairs={{0,1},{1,0},{2,3},{3,2},{4,5},{5,4},{6,7},{7,6},{8,9},{9,8},{10,11... | collective-permute-start | bytes 1572872 | tf_op jit(solution)/shard_map/ppermute | solution.py:410
  80.6 41.2 %collective-permute-start.4 = (f32[4,2,32,512]{3,2,1,0:T(8,128)S(1)}, f32[4,2,32,512]{3,2,1,0:T(8,128)S(1)}, u32[]{:S(2)}, u32[]{:S(2)}) collective-permute-start(f32[4,2,32,512]{3,2,1,0:T(8,128)S(1)} %pad_maximum_fusion.r_2_), channel_id=1, source_target_pairs={{0,1},{1,0},{2,3},{3,2},{4,5},{5,4},{6,7},{7,6},{8,9},{9,8},{10,11... | collective-permute-start | bytes 1572872 | tf_op jit(solution)/shard_map/ppermute | solution.py:410
  80.6 41.2 %collective-permute-start.5 = (f32[4,2,32,512]{3,2,1,0:T(8,128)}, f32[4,2,32,512]{3,2,1,0:T(8,128)S(1)}, u32[]{:S(2)}, u32[]{:S(2)}) collective-permute-start(f32[4,2,32,512]{3,2,1,0:T(8,128)} %collective-permute-done.3.r_3_), channel_id=1, source_target_pairs={{0,1},{1,0},{2,3},{3,2},{4,5},{5,4},{6,7},{7,6},{8,9},{9,8},{10,11... | collective-permute-start | bytes 1572872 | tf_op jit(solution)/shard_map/ppermute | solution.py:410
  98.4 35.4 %collective-permute-start.29 = (f32[8,32,512]{2,1,0:T(8,128)S(1)}, f32[8,32,512]{2,1,0:T(8,128)S(1)}, u32[]{:S(2)}, u32[]{:S(2)}) collective-permute-start(f32[8,32,512]{2,1,0:T(8,128)S(1)} %get-tuple-element.58), channel_id=1, source_target_pairs={{0,1},{1,0},{2,3},{3,2},{4,5},{5,4},{6,7},{7,6},{8,9},{9,8},{10,11... | collective-permute-start | bytes 1572872 | tf_op jit(solution)/shard_map/ppermute | solution.py:410
  110.0 24.1 %collective-permute-start.31 = (f32[8,32,512]{2,1,0:T(8,128)S(1)}, f32[8,32,512]{2,1,0:T(8,128)S(1)}, u32[]{:S(2)}, u32[]{:S(2)}) collective-permute-start(f32[8,32,512]{2,1,0:T(8,128)S(1)} %get-tuple-element.60), channel_id=1, source_target_pairs={{0,1},{1,0},{2,3},{3,2},{4,5},{5,4},{6,7},{7,6},{8,9},{9,8},{10,11... | collective-permute-start | bytes 1572872 | tf_op jit(solution)/shard_map/ppermute | solution.py:410
  136.0 18.2 %collective-permute-start.34 = (f32[4,32,512]{2,1,0:T(8,128)S(1)}, f32[4,32,512]{2,1,0:T(8,128)S(1)}, u32[]{:S(2)}, u32[]{:S(2)}) collective-permute-start(f32[4,32,512]{2,1,0:T(8,128)S(1)} %slice_add_fusion), channel_id=1, source_target_pairs={{0,2},{1,3},{2,0},{3,1},{4,6},{5,7},{6,4},{7,5},{8,10},{9,11},{10,... | collective-permute-start | bytes 786440 | tf_op jit(solution)/shard_map/ppermute | solution.py:410
  136.4 22.5 %collective-permute-start.25 = (f32[4,32,512]{2,1,0:T(8,128)S(1)}, f32[4,32,512]{2,1,0:T(8,128)S(1)}, u32[]{:S(2)}, u32[]{:S(2)}) collective-permute-start(f32[4,32,512]{2,1,0:T(8,128)S(1)} %slice_add_fusion.3), channel_id=1, source_target_pairs={{0,2},{1,3},{2,0},{3,1},{4,6},{5,7},{6,4},{7,5},{8,10},{9,11},{10,... | collective-permute-start | bytes 786440 | tf_op jit(solution)/shard_map/ppermute | solution.py:410
  154.4 19.2 %collective-permute-start.36 = (f32[3,32,512]{2,1,0:T(8,128)S(1)}, f32[3,32,512]{2,1,0:T(8,128)S(1)}, u32[]{:S(2)}, u32[]{:S(2)}) collective-permute-start(f32[3,32,512]{2,1,0:T(8,128)S(1)} %pad_maximum_fusion.5), channel_id=1, source_target_pairs={{0,8},{1,9},{2,10},{3,11},{4,12},{5,13},{6,14},{7,15},{8,0},{9,1},... | collective-permute-start | bytes 589832 | tf_op jit(solution)/shard_map/ppermute | solution.py:410
  155.5 18.2 %collective-permute-start.37 = (f32[3,32,512]{2,1,0:T(8,128)S(1)}, f32[3,32,512]{2,1,0:T(8,128)S(1)}, u32[]{:S(2)}, u32[]{:S(2)}) collective-permute-start(f32[3,32,512]{2,1,0:T(8,128)S(1)} %pad_maximum_fusion.6), channel_id=1, source_target_pairs={{0,12},{1,13},{2,14},{3,15},{4,8},{5,9},{6,10},{7,11},{8,4},{9,5},... | collective-permute-start | bytes 589832 | tf_op jit(solution)/shard_map/ppermute | solution.py:410
  159.0 15.8 %collective-permute-start.26 = (f32[32,512]{1,0:T(8,128)S(1)}, f32[32,512]{1,0:T(8,128)S(1)}, u32[]{:S(2)}, u32[]{:S(2)}) collective-permute-start(f32[32,512]{1,0:T(8,128)S(1)} %get-tuple-element.77), channel_id=1, source_target_pairs={{0,4},{1,5},{2,6},{3,7},{4,0},{5,1},{6,2},{7,3},{8,12},{9,13},{10,... | collective-permute-start | bytes 196616 | tf_op jit(solution)/shard_map/ppermute | solution.py:410
  159.1 18.9 %collective-permute-start.27 = (f32[32,512]{1,0:T(8,128)S(1)}, f32[32,512]{1,0:T(8,128)S(1)}, u32[]{:S(2)}, u32[]{:S(2)}) collective-permute-start(f32[32,512]{1,0:T(8,128)S(1)} %get-tuple-element.76), channel_id=1, source_target_pairs={{0,8},{1,9},{2,10},{3,11},{4,12},{5,13},{6,14},{7,15},{8,0},{9,1},... | collective-permute-start | bytes 196616 | tf_op jit(solution)/shard_map/ppermute | solution.py:410
  (25 other events, 290.2 us)

commit v2 on v1

--- a/solution.py
+++ b/solution.py
@@ -10,9 +10,7 @@
 
 LANES = 128
 SUB = 8
-UP = 8
-U0 = 2
-U1 = 8
+U1 = SUB
 VLIM = 28 << 20
 TOP = 1.7
 
@@ -23,8 +21,8 @@
     return [float(c) for c in np.polynomial.polynomial.polyfit(nodes, fun(np.sqrt(nodes)), degree)]
 
 
-SIN_C = even_fit(lambda x: np.sin(x) / x, 5)
-COS_C = even_fit(np.cos, 6)
+SIN_C = even_fit(lambda x: np.sin(x) / x, 4)
+COS_C = even_fit(np.cos, 5)
 
 
 def horner(coefs, z):
@@ -78,6 +76,21 @@
     return out
 
 
+def turn(v):
+    sub = iotas()[0]
+    v = list(v)
+    step = SUB // 2
+    while step:
+        low = (sub & step) == 0
+        for a in range(SUB):
+            if a & step == 0:
+                x, y = v[a], v[a + step]
+                v[a] = jnp.where(low, x, pltpu.roll(y, step, 0))
+                v[a + step] = jnp.where(low, pltpu.roll(x, SUB - step, 0), y)
+        step //= 2
+    return v
+
+
 def spread_any(parts):
     nb, lane = len(parts), iotas()[1]
     return [pick(parts, lane // (LANES // nb), (lane * nb + b) % LANES) for b in range(nb)]
@@ -92,74 +105,54 @@
     return [pl.BlockSpec(memory_space=s) for s in (pltpu.SMEM, pltpu.VMEM, pltpu.HBM)]
 
 
-def prep_models_kernel(depths, vel, ani, *refs):
-    outs, (buf, sem) = refs[: len(depths)], refs[len(depths) :]
+def prep_models_kernel(depths, vel, ani, *outs):
     _, R, NY = vel.shape
     nb = NY // LANES
-    copies = [
-        pltpu.make_async_copy(ref.at[d], buf.at[m, n], sem.at[m, n])
-        for n, d in enumerate(depths) for m, ref in enumerate((vel, ani))
-    ]
-    for c in copies:
-        c.start()
-    for n in range(len(depths)):
-        for m in range(2):
-            copies[2 * n + m].wait()
+    for n, d in enumerate(depths):
+        for m, ref in enumerate((vel, ani)):
             for j in range(R // SUB):
                 rows = slice(j * SUB, (j + 1) * SUB)
-                new = spread([buf[m, n, rows, cut(b)] for b in range(nb)])
+                new = spread([ref[d, rows, cut(b)] for b in range(nb)])
                 for b in range(nb):
                     outs[n][m, rows, cut(b)] = new[b]
 
 
 def prep_models(vel, ani, depths):
     _, R, NY = vel.shape
-    _, vmem, hbm = spaces()
+    _, vmem, _ = spaces()
     return pl.pallas_call(
         lambda *r: prep_models_kernel(depths, *r), out_shape=[jax.ShapeDtypeStruct((2, R, NY), jnp.float32)] * len(depths),
-        in_specs=[hbm, hbm], out_specs=[vmem] * len(depths),
-        scratch_shapes=[pltpu.VMEM((2, len(depths), R, NY), jnp.float32), pltpu.SemaphoreType.DMA((2, len(depths)))],
+        in_specs=[vmem] * 2, out_specs=[vmem] * len(depths),
         name="prep_models", compiler_params=pltpu.CompilerParams(vmem_limit_bytes=4 << 20),
     )(vel, ani)
 
 
-def prep_field_kernel(p, sign, where, field, out, buf, sem):
+def prep_field_kernel(p, sign, where, field, out):
     G, NY = out.shape[1], out.shape[3]
     nb = NY // LANES
-    chunks = sem.shape[0]
-    C = G // chunks
-    copies = []
-    for h in range(chunks):
-        for k in range(SUB):
-            row = pl.multiple_of((where[0] ^ off_of(k)) * G + h * C, SUB)
-            for c in range(2):
-                copies.append(pltpu.make_async_copy(
-                    field.at[p, c, pl.ds(row, C), :], buf.at[c, pl.ds(h * C, C), k, :], sem.at[h]))
-    for c in copies:
-        c.start()
-    for h in range(chunks):
-        for c in copies[h * SUB * 2 : (h + 1) * SUB * 2]:
-            c.wait()
-
-        def body(j, _):
-            for q in range(UP):
-                i = j * UP + q
-                for a in range(2):
-                    new = spread([buf[a, i, :, cut(b)] for b in range(nb)])
-                    for b in range(nb):
-                        out[a, i, :, cut(b)] = sign * new[b] if a == 1 and sign < 0 else new[b]
-            return 0
-
-        lax.fori_loop(h * C // UP, (h + 1) * C // UP, body, 0)
+    starts = [(where[0] ^ off_of(k)) * G for k in range(SUB)]
+
+    def body(j, _):
+        for c in range(2):
+            cols = []
+            for b in range(nb):
+                rows = [field[p, c, pl.ds(pl.multiple_of(starts[k] + j * SUB, SUB), SUB), cut(b)] for k in range(SUB)]
+                cols.append(turn(rows))
+            for q in range(SUB):
+                new = spread([cols[b][q] for b in range(nb)])
+                for b in range(nb):
+                    out[c, j * SUB + q, :, cut(b)] = -new[b] if c == 1 and sign < 0 else new[b]
+        return 0
+
+    lax.fori_loop(0, G // SUB, body, 0)
 
 
 def prep_field(where, field, p, sign, G):
     NY = field.shape[-1]
     shape = (2, G, SUB, NY)
-    smem, vmem, hbm = spaces()
-    return pl.pallas_call(
-        lambda *r: prep_field_kernel(p, sign, *r), out_shape=jax.ShapeDtypeStruct(shape, jnp.float32), in_specs=[smem, hbm], out_specs=vmem,
-        scratch_shapes=[pltpu.VMEM(shape, jnp.float32), pltpu.SemaphoreType.DMA((4,))], name="prep_field",
+    smem, vmem, _ = spaces()
+    return pl.pallas_call(
+        lambda *r: prep_field_kernel(p, sign, *r), out_shape=jax.ShapeDtypeStruct(shape, jnp.float32), in_specs=[smem, vmem], out_specs=vmem, name="prep_field",
         compiler_params=pltpu.CompilerParams(vmem_limit_bytes=12 << 20),
     )(where, field)
 
@@ -249,7 +242,7 @@
         right = t[1:] + [jnp.where(right_edge, 0.0, pltpu.roll(t[0], LANES - 1, 1))]
         return [a + (b + c) for a, b, c in zip(r, left, right)]
 
-    def sweep(src_buf, put, base, count):
+    def sweep(src_buf, put, base, count, done=None):
         def body(j, _):
             i0 = base + j * U1
             for f in range(2):
@@ -257,6 +250,8 @@
                 for q in range(U1):
                     o = [around(rows[c][q], rows[c][q + 1], rows[c][q + 2]) for c in range(2)]
                     put(f, q, i0 + q, o, [rows[c][q + 1] for c in range(2)])
+            if done is not None:
+                done(i0)
             return 0
 
         lax.fori_loop(0, count // U1, body, 0)
@@ -271,50 +266,46 @@
 
 def first_kernel(cfg, where, om_ref, *refs):
     metas, R = cfg["metas"], cfg["R"]
-    blks, (*cur, sh, e1, mod, sem_m) = refs[: len(metas)], refs[len(metas) :]
+    blks, (*cur, sh, e1, mod) = refs[: len(metas)], refs[len(metas) :]
     G, NB = mod.shape[1], mod.shape[3] // LANES
     lo = where[1]
     bases = [lo * R, (1 - lo) * R][: G // R]
-    model_copies = [[] for _ in bases]
+    places = [[None] * SUB for _ in bases]
     for ref, (k0, kb, half) in zip(blks, metas):
         for k in range(kb):
-            for m in range(2):
-                model_copies[half].append(pltpu.make_async_copy(
-                    ref.at[k, m], mod.at[m, pl.ds(bases[half], R), k0 + k, :], sem_m.at[half]))
-    for some in model_copies:
-        for c in some:
-            c.start()
+            places[half][k0 + k] = (ref, k)
     halos, sweep = wave_tools(where, G, NB)
     om = om_ref[0]
     k1 = 6.0 / om
     kp = 0.01 * om
 
-    def stage0(i0):
-        for q in range(U0):
-            i = i0 + q
+    def cell(i, b, v, eta):
+        cf = (v * k1) * (1.0 + 2.0 * eta)
+        d = cf * (10.0 / 3.0)
+        den = 1.0 + d * d
+        inv = 1.0 / (v * den)
+        ph = kp * (den * inv)
+        bi = (cf * (2.0 / 3.0)) * (v * inv)
+        mod[0, i, :, cut(b)] = bi * d
+        mod[1, i, :, cut(b)] = bi
+        z = ph * ph
+        sn = ph * horner(SIN_C, z)
+        cs = horner(COS_C, z)
+        for f in range(2):
+            re, im = cur[f][0, i, :, cut(b)], cur[f][1, i, :, cut(b)]
+            sh[2 * f, i + 1, :, cut(b)] = re * cs - im * sn
+            sh[2 * f + 1, i + 1, :, cut(b)] = im * cs + re * sn
+
+    for half, base in enumerate(bases):
+        def stage0(j, _):
+            rows = pl.ds(pl.multiple_of(j * SUB, SUB), SUB)
             for b in range(NB):
-                v = mod[0, i, :, cut(b)]
-                eta = mod[1, i, :, cut(b)]
-                cf = (v * k1) * (1.0 + 2.0 * eta)
-                d = cf * (10.0 / 3.0)
-                den = 1.0 + d * d
-                inv = 1.0 / (v * den)
-                ph = kp * (den * inv)
-                bi = (cf * (2.0 / 3.0)) * (v * inv)
-                mod[0, i, :, cut(b)] = bi * d
-                mod[1, i, :, cut(b)] = bi
-                z = ph * ph
-                sn = ph * horner(SIN_C, z)
-                cs = horner(COS_C, z)
-                for f in range(2):
-                    re, im = cur[f][0, i, :, cut(b)], cur[f][1, i, :, cut(b)]
-                    sh[2 * f, i + 1, :, cut(b)] = re * cs - im * sn
-                    sh[2 * f + 1, i + 1, :, cut(b)] = im * cs + re * sn
-
-    for half, base in enumerate(bases):
-        for c in model_copies[half]:
-            c.wait()
-        lax.fori_loop(0, R // U0, lambda j, _: (stage0(base + j * U0), 0)[1], 0)
+                v, eta = (turn([ref[k, m, rows, cut(b)] for ref, k in places[half]]) for m in range(2))
+                for q in range(SUB):
+                    cell(base + j * SUB + q, b, v[q], eta[q])
+            return 0
+
+        lax.fori_loop(0, R // SUB, stage0, 0)
     halos(sh)
 
     def put(f, q, i, o, mid):
@@ -333,7 +324,7 @@
     outs, refs = refs[: G // R], list(refs[G // R :])
     lo = where[1]
     bases = [lo * R, (1 - lo) * R][: G // R]
-    st, (e2, img, sem_o, *keep) = (None, refs) if last else (refs[:2], refs[2:])
+    st, (e2, *keep) = (None, refs) if last else (refs[:2], refs[2:])
     halos, sweep = wave_tools(where, G, NB)
 
     def put2(f, q, i, o, mid):
@@ -358,40 +349,39 @@
                     keep[0][c, q, :, cut(b)] = new[c]
             if f == 1:
                 sr, si = (keep[0][c, q, :, cut(b)] if last else st[0][c, i, :, cut(b)] for c in range(2))
-                img[i, :, cut(b)] = sr * new[0] - si * new[1]
-
-    out_copies = []
+                images[b][q] = sr * new[0] - si * new[1]
+
+    images = [[None] * SUB for _ in range(NB)]
     for o_i in reversed(range(len(outs))):
-        sweep(e2, put3, bases[o_i], R)
-        for k in range(SUB):
-            c = pltpu.make_async_copy(img.at[pl.ds(bases[o_i], R), k, :], outs[o_i].at[k], sem_o)
-            c.start()
-            out_copies.append(c)
-    for c in out_copies:
-        c.wait()
+        def send(i0):
+            rows = pl.ds(pl.multiple_of(i0 - bases[o_i], SUB), SUB)
+            for b in range(NB):
+                for k, v in enumerate(turn(images[b])):
+                    outs[o_i][k, rows, cut(b)] = v
+
+        sweep(e2, put3, bases[o_i], R, send)
 
 
 def first_call(where, omega, blocks, metas, state, R):
     _, G, _, NY = state[0].shape
-    smem, vmem, anym = spaces()
+    smem, vmem, _ = spaces()
     pad = jax.ShapeDtypeStruct((4, G + 2, SUB, NY), jnp.float32)
     return pl.pallas_call(
         lambda *r: first_kernel(dict(metas=metas, R=R), *r), out_shape=[pad, pad, jax.ShapeDtypeStruct((2, G, SUB, NY), jnp.float32)],
-        in_specs=[smem, smem] + [anym] * len(blocks) + [vmem] * 2, out_specs=[vmem] * 3,
-        scratch_shapes=[pltpu.SemaphoreType.DMA((G // R,))], name="first_half",
+        in_specs=[smem, smem] + [vmem] * (len(blocks) + 2), out_specs=[vmem] * 3, name="first_half",
         compiler_params=pltpu.CompilerParams(vmem_limit_bytes=VLIM),
     )(where, omega, *blocks, *state)
 
 
 def second_call(where, sh, e1, mod, last, R):
     _, G, _, NY = mod.shape
-    smem, vmem, anym = spaces()
+    smem, vmem, _ = spaces()
     out_shape = [jax.ShapeDtypeStruct((SUB, R, NY), jnp.float32)] * (G // R)
-    out_specs = [anym] * (G // R)
+    out_specs = [vmem] * (G // R)
     if not last:
         out_shape += [jax.ShapeDtypeStruct((2, G, SUB, NY), jnp.float32)] * 2
         out_specs += [vmem] * 2
-    scratch = [pltpu.VMEM((4, G + 2, SUB, NY), jnp.float32), pltpu.VMEM((G, SUB, NY), jnp.float32), pltpu.SemaphoreType.DMA(())]
+    scratch = [pltpu.VMEM((4, G + 2, SUB, NY), jnp.float32)]
     if last:
         scratch.append(pltpu.VMEM((2, U1, SUB, NY), jnp.float32))
     return pl.pallas_call(

time: 180 us -> 173 us (0.961)
  Pallas kernels: 61.9 us -> 53 us
    pallas_call x2, Pallas kernels: 11.7 us -> 8.62 us  [prep_field(): pl.pallas_call(lambda *r: prep_field_kernel(p, sign, *r), out_shape=jax.S...]
    pallas_call x4, Pallas kernels: 19.8 us -> 17.2 us  [second_call(): pl.pallas_call(lambda *r: second_kernel(dict(last=last, R=R), *r), out_sh...]
    pallas_call x4, Pallas kernels: 25.5 us -> 23.1 us  [first_call(): pl.pallas_call(lambda *r: first_kernel(dict(metas=metas, R=R), *r), out_s...]
  transfers between devices with their start and end apart: 38 -> 38, of which waited for: 14 -> 14; matrix products, arithmetic and copies ran while one was open for 1% -> 1% of each run, Pallas kernels for 34% -> 30%
where the time goes in v2:
time: 173 us; the launch traced here: 172 us
  waiting for transfers between devices  66.2 us (38%)
  Pallas kernels  53 us (31%)
  starting transfers between devices  47.1 us (27%)
  local copies, waits for them, and re-layouts  3.53 us (2%)
  other arithmetic  2.15 us (1%)
    ppermute x38, waiting for transfers between devices, swap(): return lax.ppermute(x, 'freq', [(i, i ^ mask) for i in range(n)])  66.2 us
    ppermute x38, starting transfers between devices, swap(): return lax.ppermute(x, 'freq', [(i, i ^ mask) for i in range(n)])  47.1 us
    pallas_call x4, Pallas kernels, first_call(): pl.pallas_call(lambda *r: first_kernel(dict(metas=metas, R=R), *r), out_s...  23.1 us
    pallas_call x4, Pallas kernels, second_call(): pl.pallas_call(lambda *r: second_kernel(dict(last=last, R=R), *r), out_sh...  17.2 us
    pallas_call x2, Pallas kernels, prep_field(): pl.pallas_call(lambda *r: prep_field_kernel(p, sign, *r), out_shape=jax.S...  8.62 us
    unnamed x22, local copies, waits for them, and re-layouts  3.53 us
  transfers between devices with their start and end apart: 38, of which 14 were waited for; matrix products, arithmetic and copies ran while one was open for 1% of the time, Pallas kernels for 30%

profile of v2, /device:TPU:0, one launch (start us, length us, event | category | flops | bytes accessed | tf_op | source)
XLA Modules:
  0.0 172.2 jit_solution(13416279543584931127)
XLA Ops:
  10.3 3.5 %collective-permute-start.13 = (f32[2,32,512]{2,1,0:T(8,128)S(1)}, f32[2,32,512]{2,1,0:T(8,128)S(1)}, u32[]{:S(2)}, u32[]{:S(2)}) collective-permute-start(f32[2,32,512]{2,1,0:T(8,128)S(1)} %get-tuple-element.36), channel_id=1, source_target_pairs={{0,8},{1,9},{2,10},{3,11},{4,12},{5,13},{6,14},{7,15},{8,0},{9,1},... | collective-permute-start | bytes 393224 | tf_op jit(solution)/shard_map/ppermute | solution.py:400
  14.1 4.1 %collective-permute-done.19 = f32[2,32,512]{2,1,0:T(8,128)S(1)} collective-permute-done((f32[2,32,512]{2,1,0:T(8,128)S(1)}, f32[2,32,512]{2,1,0:T(8,128)S(1)}, u32[]{:S(2)}, u32[]{:S(2)}) %collective-permute-start.19) | collective-permute-done | bytes 131104 | tf_op jit(solution)/shard_map/ppermute | solution.py:400
  18.2 9.8 %collective-permute-start.7 = (f32[2,32,512]{2,1,0:T(8,128)S(1)}, f32[2,32,512]{2,1,0:T(8,128)S(1)}, u32[]{:S(2)}, u32[]{:S(2)}) collective-permute-start(f32[2,32,512]{2,1,0:T(8,128)S(1)} %get-tuple-element.35), channel_id=1, source_target_pairs={{0,8},{1,9},{2,10},{3,11},{4,12},{5,13},{6,14},{7,15},{8,0},{9,1},... | collective-permute-start | bytes 393224 | tf_op jit(solution)/shard_map/ppermute | solution.py:400
  40.6 3.2 %collective-permute-start.1 = (f32[2,32,512]{2,1,0:T(8,128)S(1)}, f32[2,32,512]{2,1,0:T(8,128)S(1)}, u32[]{:S(2)}, u32[]{:S(2)}) collective-permute-start(f32[2,32,512]{2,1,0:T(8,128)S(1)} %get-tuple-element.34), channel_id=1, source_target_pairs={{0,8},{1,9},{2,10},{3,11},{4,12},{5,13},{6,14},{7,15},{8,0},{9,1},... | collective-permute-start | bytes 393224 | tf_op jit(solution)/shard_map/ppermute | solution.py:400
  43.9 6.1 %collective-permute-done.1 = f32[2,32,512]{2,1,0:T(8,128)S(1)} collective-permute-done((f32[2,32,512]{2,1,0:T(8,128)S(1)}, f32[2,32,512]{2,1,0:T(8,128)S(1)}, u32[]{:S(2)}, u32[]{:S(2)}) %collective-permute-start.1) | collective-permute-done | bytes 131104 | tf_op jit(solution)/shard_map/ppermute | solution.py:400
  52.5 4.2 %collective-permute-done.2 = f32[2,32,512]{2,1,0:T(8,128)S(1)} collective-permute-done((f32[2,32,512]{2,1,0:T(8,128)S(1)}, f32[2,32,512]{2,1,0:T(8,128)S(1)}, u32[]{:S(2)}, u32[]{:S(2)}) %collective-permute-start.2) | collective-permute-done | bytes 131104 | tf_op jit(solution)/shard_map/ppermute | solution.py:400
  61.6 10.2 %collective-permute-done.9.r_3_ = f32[4,2,32,512]{3,2,1,0:T(8,128)} collective-permute-done((f32[4,2,32,512]{3,2,1,0:T(8,128)}, f32[4,2,32,512]{3,2,1,0:T(8,128)}, u32[]{:S(2)}, u32[]{:S(2)}) %collective-permute-start.9) | collective-permute-done | bytes 524320 | tf_op jit(solution)/shard_map/ppermute | solution.py:400
  71.9 4.3 %prep_field.2.r_6_ = f32[2,64,8,512]{3,2,1,0:T(8,128)S(1)} custom-call(s32[2]{0:T(128)S(1)} %pad_add_fusion.r_0_, f32[1,2,512,512]{3,2,1,0:T(8,128)S(1)} %copy-done), custom_call_target="tpu_custom_call" | custom-call | tf_op jit(solution)/shard_map/prep_field/pallas_call | solution.py:154
  76.2 4.0 %collective-permute-done.3.r_3_ = f32[4,2,32,512]{3,2,1,0:T(8,128)} collective-permute-done((f32[4,2,32,512]{3,2,1,0:T(8,128)S(1)}, f32[4,2,32,512]{3,2,1,0:T(8,128)}, u32[]{:S(2)}, u32[]{:S(2)}) %collective-permute-start.3) | collective-permute-done | bytes 524320 | tf_op jit(solution)/shard_map/ppermute | solution.py:400
  80.7 4.3 %prep_field.3.r_7_ = f32[2,64,8,512]{3,2,1,0:T(8,128)S(1)} custom-call(s32[2]{0:T(128)S(1)} %pad_add_fusion.r_0_, f32[1,2,512,512]{3,2,1,0:T(8,128)S(1)} %copy-done.1), custom_call_target="tpu_custom_call" | custom-call | tf_op jit(solution)/shard_map/prep_field/pallas_call | solution.py:154
  85.1 5.8 %first_half.4 = (f32[4,66,8,512]{3,2,1,0:T(8,128)S(1)}, f32[4,66,8,512]{3,2,1,0:T(8,128)S(1)}, f32[2,64,8,512]{3,2,1,0:T(8,128)S(1)}) custom-call(s32[2]{0:T(128)S(1)} %pad_add_fusion.r_0_, f32[1]{0:T(128)} %bitcast.4.r_1_, f32[4,2,32,512]{3,2,1,0:T(8,128)S(1)} %copy-done.3, f32[4,2,32,512]{3,2,1,0:T(8,128)} %collective-permute-done.21.r_3_, ...), custom_call_target="tpu_custom_call" | custom-call | tf_op jit(solution)/shard_map/first_half/pallas_call | solution.py:369
  90.9 4.3 %second_half.4 = (f32[8,32,512]{2,1,0:T(8,128)S(1)}, f32[8,32,512]{2,1,0:T(8,128)S(1)}, f32[2,64,8,512]{3,2,1,0:T(8,128)S(1)}, f32[2,64,8,512]{3,2,1,0:T(8,128)S(1)}) custom-call(s32[2]{0:T(128)S(1)} %pad_add_fusion.r_0_, f32[4,66,8,512]{3,2,1,0:T(8,128)S(1)} %get-tuple-element.37.r_1_, f32[4,66,8,512]{3,2,1,0:T(8,128)S(1)} %get-tuple-element.38.r_2_, ...), custom_call_target="tpu_custom_call" | custom-call | tf_op jit(solution)/shard_map/second_half/pallas_call | solution.py:387
  95.3 5.8 %first_half.5 = (f32[4,66,8,512]{3,2,1,0:T(8,128)S(1)}, f32[4,66,8,512]{3,2,1,0:T(8,128)S(1)}, f32[2,64,8,512]{3,2,1,0:T(8,128)S(1)}) custom-call(s32[2]{0:T(128)S(1)} %pad_add_fusion.r_0_, f32[1]{0:T(128)} %bitcast.4.r_1_, f32[4,2,32,512]{3,2,1,0:T(8,128)S(1)} %pad_maximum_fusion.2.r_2_, f32[4,2,32,512]{3,2,1,0:T(8,128)} %collective-permute-done.15.r_3_, ...), custom_call_target="tpu_custom_call" | custom-call | tf_op jit(solution)/shard_map/first_half/pallas_call | solution.py:369
  101.0 4.3 %second_half.5 = (f32[8,32,512]{2,1,0:T(8,128)S(1)}, f32[8,32,512]{2,1,0:T(8,128)S(1)}, f32[2,64,8,512]{3,2,1,0:T(8,128)S(1)}, f32[2,64,8,512]{3,2,1,0:T(8,128)S(1)}) custom-call(s32[2]{0:T(128)S(1)} %pad_add_fusion.r_0_, f32[4,66,8,512]{3,2,1,0:T(8,128)S(1)} %get-tuple-element.42.r_1_, f32[4,66,8,512]{3,2,1,0:T(8,128)S(1)} %get-tuple-element.43.r_2_, ...), custom_call_target="tpu_custom_call" | custom-call | tf_op jit(solution)/shard_map/second_half/pallas_call | solution.py:387
  105.9 5.9 %first_half.6 = (f32[4,66,8,512]{3,2,1,0:T(8,128)S(1)}, f32[4,66,8,512]{3,2,1,0:T(8,128)S(1)}, f32[2,64,8,512]{3,2,1,0:T(8,128)S(1)}) custom-call(s32[2]{0:T(128)S(1)} %pad_add_fusion.r_0_, f32[1]{0:T(128)} %bitcast.4.r_1_, f32[4,2,32,512]{3,2,1,0:T(8,128)} %pad_maximum_fusion.1.r_2_, f32[4,2,32,512]{3,2,1,0:T(8,128)} %collective-permute-done.9.r_3_, ...), custom_call_target="tpu_custom_call" | custom-call | tf_op jit(solution)/shard_map/first_half/pallas_call | solution.py:369
  111.8 4.3 %second_half.6 = (f32[8,32,512]{2,1,0:T(8,128)S(1)}, f32[8,32,512]{2,1,0:T(8,128)S(1)}, f32[2,64,8,512]{3,2,1,0:T(8,128)S(1)}, f32[2,64,8,512]{3,2,1,0:T(8,128)S(1)}) custom-call(s32[2]{0:T(128)S(1)} %pad_add_fusion.r_0_, f32[4,66,8,512]{3,2,1,0:T(8,128)S(1)} %get-tuple-element.47.r_1_, f32[4,66,8,512]{3,2,1,0:T(8,128)S(1)} %get-tuple-element.48.r_2_, ...), custom_call_target="tpu_custom_call" | custom-call | tf_op jit(solution)/shard_map/second_half/pallas_call | solution.py:387
  116.2 5.6 %first_half.7 = (f32[4,66,8,512]{3,2,1,0:T(8,128)S(1)}, f32[4,66,8,512]{3,2,1,0:T(8,128)S(1)}, f32[2,64,8,512]{3,2,1,0:T(8,128)S(1)}) custom-call(s32[2]{0:T(128)S(1)} %pad_add_fusion.r_0_, f32[1]{0:T(128)} %bitcast.4.r_1_, f32[4,2,32,512]{3,2,1,0:T(8,128)S(1)} %pad_maximum_fusion.r_2_, f32[4,2,32,512]{3,2,1,0:T(8,128)} %collective-permute-done.3.r_3_, ...), custom_call_target="tpu_custom_call" | custom-call | tf_op jit(solution)/shard_map/first_half/pallas_call | solution.py:369
  121.8 4.3 %second_half.7 = (f32[8,32,512]{2,1,0:T(8,128)S(1)}, f32[8,32,512]{2,1,0:T(8,128)S(1)}) custom-call(s32[2]{0:T(128)S(1)} %pad_add_fusion.r_0_, f32[4,66,8,512]{3,2,1,0:T(8,128)S(1)} %get-tuple-element.52.r_1_, f32[4,66,8,512]{3,2,1,0:T(8,128)S(1)} %get-tuple-element.53.r_2_, f32[2,64,8,512]{3,2,1,0:T(8,128)S(1)} %get-tuple-element.54.r_3_), custom_call_target="tpu_custom_call" | custom-call | tf_op jit(solution)/shard_map/second_half/pallas_call | solution.py:387
  131.2 4.8 %collective-permute-done.30 = f32[4,32,512]{2,1,0:T(8,128)S(1)} collective-permute-done((f32[4,32,512]{2,1,0:T(8,128)S(1)}, f32[4,32,512]{2,1,0:T(8,128)S(1)}, u32[]{:S(2)}, u32[]{:S(2)}) %collective-permute-start.30) | collective-permute-done | bytes 262176 | tf_op jit(solution)/shard_map/ppermute | solution.py:400
  136.1 5.5 %collective-permute-done.32 = f32[4,32,512]{2,1,0:T(8,128)S(1)} collective-permute-done((f32[4,32,512]{2,1,0:T(8,128)S(1)}, f32[4,32,512]{2,1,0:T(8,128)S(1)}, u32[]{:S(2)}, u32[]{:S(2)}) %collective-permute-start.32) | collective-permute-done | bytes 262176 | tf_op jit(solution)/shard_map/ppermute | solution.py:400
  141.7 5.5 %collective-permute-done.34 = f32[4,32,512]{2,1,0:T(8,128)S(1)} collective-permute-done((f32[4,32,512]{2,1,0:T(8,128)S(1)}, f32[4,32,512]{2,1,0:T(8,128)S(1)}, u32[]{:S(2)}, u32[]{:S(2)}) %collective-permute-start.34) | collective-permute-done | bytes 262176 | tf_op jit(solution)/shard_map/ppermute | solution.py:400
  148.4 3.5 %collective-permute-start.37 = (f32[3,32,512]{2,1,0:T(8,128)S(1)}, f32[3,32,512]{2,1,0:T(8,128)S(1)}, u32[]{:S(2)}, u32[]{:S(2)}) collective-permute-start(f32[3,32,512]{2,1,0:T(8,128)S(1)} %pad_maximum_fusion.6), channel_id=1, source_target_pairs={{0,12},{1,13},{2,14},{3,15},{4,8},{5,9},{6,10},{7,11},{8,4},{9,5},... | collective-permute-start | bytes 589832 | tf_op jit(solution)/shard_map/ppermute | solution.py:400
  153.0 4.0 %collective-permute-done.35 = f32[3,32,512]{2,1,0:T(8,128)S(1)} collective-permute-done((f32[3,32,512]{2,1,0:T(8,128)S(1)}, f32[3,32,512]{2,1,0:T(8,128)S(1)}, u32[]{:S(2)}, u32[]{:S(2)}) %collective-permute-start.35) | collective-permute-done | bytes 196640 | tf_op jit(solution)/shard_map/ppermute | solution.py:400
  157.0 9.6 %collective-permute-done.36 = f32[3,32,512]{2,1,0:T(8,128)S(1)} collective-permute-done((f32[3,32,512]{2,1,0:T(8,128)S(1)}, f32[3,32,512]{2,1,0:T(8,128)S(1)}, u32[]{:S(2)}, u32[]{:S(2)}) %collective-permute-start.36) | collective-permute-done | bytes 196640 | tf_op jit(solution)/shard_map/ppermute | solution.py:400
  (106 shorter events, 45.0 us)
Async XLA Ops:
  9.4 18.7 %collective-permute-start.12 = (f32[2,32,512]{2,1,0:T(8,128)S(1)}, f32[2,32,512]{2,1,0:T(8,128)S(1)}, u32[]{:S(2)}, u32[]{:S(2)}) collective-permute-start(f32[2,32,512]{2,1,0:T(8,128)S(1)} %get-tuple-element.36), channel_id=1, source_target_pairs={{0,4},{1,5},{2,6},{3,7},{4,0},{5,1},{6,2},{7,3},{8,12},{9,13},{10,... | collective-permute-start | bytes 393224 | tf_op jit(solution)/shard_map/ppermute | solution.py:400
  10.3 20.5 %collective-permute-start.13 = (f32[2,32,512]{2,1,0:T(8,128)S(1)}, f32[2,32,512]{2,1,0:T(8,128)S(1)}, u32[]{:S(2)}, u32[]{:S(2)}) collective-permute-start(f32[2,32,512]{2,1,0:T(8,128)S(1)} %get-tuple-element.36), channel_id=1, source_target_pairs={{0,8},{1,9},{2,10},{3,11},{4,12},{5,13},{6,14},{7,15},{8,0},{9,1},... | collective-permute-start | bytes 393224 | tf_op jit(solution)/shard_map/ppermute | solution.py:400
  13.8 17.0 %collective-permute-start.14 = (f32[2,32,512]{2,1,0:T(8,128)S(1)}, f32[2,32,512]{2,1,0:T(8,128)S(1)}, u32[]{:S(2)}, u32[]{:S(2)}) collective-permute-start(f32[2,32,512]{2,1,0:T(8,128)S(1)} %get-tuple-element.36), channel_id=1, source_target_pairs={{0,12},{1,13},{2,14},{3,15},{4,8},{5,9},{6,10},{7,11},{8,4},{9,5},... | collective-permute-start | bytes 393224 | tf_op jit(solution)/shard_map/ppermute | solution.py:400
  18.2 18.3 %collective-permute-start.7 = (f32[2,32,512]{2,1,0:T(8,128)S(1)}, f32[2,32,512]{2,1,0:T(8,128)S(1)}, u32[]{:S(2)}, u32[]{:S(2)}) collective-permute-start(f32[2,32,512]{2,1,0:T(8,128)S(1)} %get-tuple-element.35), channel_id=1, source_target_pairs={{0,8},{1,9},{2,10},{3,11},{4,12},{5,13},{6,14},{7,15},{8,0},{9,1},... | collective-permute-start | bytes 393224 | tf_op jit(solution)/shard_map/ppermute | solution.py:400
  28.1 29.8 %collective-permute-start.21 = (f32[4,2,32,512]{3,2,1,0:T(8,128)S(1)}, f32[4,2,32,512]{3,2,1,0:T(8,128)}, u32[]{:S(2)}, u32[]{:S(2)}) collective-permute-start(f32[4,2,32,512]{3,2,1,0:T(8,128)S(1)} %pad_maximum_fusion.3.r_2_), channel_id=1, source_target_pairs={{0,2},{1,3},{2,0},{3,1},{4,6},{5,7},{6,4},{7,5},{8,10},{9,11},{10,... | collective-permute-start | bytes 1572872 | tf_op jit(solution)/shard_map/ppermute | solution.py:400
  30.8 28.0 %collective-permute-start.22 = (f32[4,2,32,512]{3,2,1,0:T(8,128)S(1)}, f32[4,2,32,512]{3,2,1,0:T(8,128)S(1)}, u32[]{:S(2)}, u32[]{:S(2)}) collective-permute-start(f32[4,2,32,512]{3,2,1,0:T(8,128)S(1)} %pad_maximum_fusion.3.r_2_), channel_id=1, source_target_pairs={{0,1},{1,0},{2,3},{3,2},{4,5},{5,4},{6,7},{7,6},{8,9},{9,8},{10,11... | collective-permute-start | bytes 1572872 | tf_op jit(solution)/shard_map/ppermute | solution.py:400
  30.8 28.8 %collective-permute-start.15 = (f32[4,2,32,512]{3,2,1,0:T(8,128)S(1)}, f32[4,2,32,512]{3,2,1,0:T(8,128)}, u32[]{:S(2)}, u32[]{:S(2)}) collective-permute-start(f32[4,2,32,512]{3,2,1,0:T(8,128)S(1)} %pad_maximum_fusion.2.r_2_), channel_id=1, source_target_pairs={{0,2},{1,3},{2,0},{3,1},{4,6},{5,7},{6,4},{7,5},{8,10},{9,11},{10,... | collective-permute-start | bytes 1572872 | tf_op jit(solution)/shard_map/ppermute | solution.py:400
  43.9 16.3 %collective-permute-start.16 = (f32[4,2,32,512]{3,2,1,0:T(8,128)S(1)}, f32[4,2,32,512]{3,2,1,0:T(8,128)S(1)}, u32[]{:S(2)}, u32[]{:S(2)}) collective-permute-start(f32[4,2,32,512]{3,2,1,0:T(8,128)S(1)} %pad_maximum_fusion.2.r_2_), channel_id=1, source_target_pairs={{0,1},{1,0},{2,3},{3,2},{4,5},{5,4},{6,7},{7,6},{8,9},{9,8},{10,11... | collective-permute-start | bytes 1572872 | tf_op jit(solution)/shard_map/ppermute | solution.py:400
  56.7 15.1 %collective-permute-start.9 = (f32[4,2,32,512]{3,2,1,0:T(8,128)}, f32[4,2,32,512]{3,2,1,0:T(8,128)}, u32[]{:S(2)}, u32[]{:S(2)}) collective-permute-start(f32[4,2,32,512]{3,2,1,0:T(8,128)} %pad_maximum_fusion.1.r_2_), channel_id=1, source_target_pairs={{0,2},{1,3},{2,0},{3,1},{4,6},{5,7},{6,4},{7,5},{8,10},{9,11},{10,... | collective-permute-start | bytes 1572872 | tf_op jit(solution)/shard_map/ppermute | solution.py:400
  57.9 22.3 %collective-permute-start.3 = (f32[4,2,32,512]{3,2,1,0:T(8,128)S(1)}, f32[4,2,32,512]{3,2,1,0:T(8,128)}, u32[]{:S(2)}, u32[]{:S(2)}) collective-permute-start(f32[4,2,32,512]{3,2,1,0:T(8,128)S(1)} %pad_maximum_fusion.r_2_), channel_id=1, source_target_pairs={{0,2},{1,3},{2,0},{3,1},{4,6},{5,7},{6,4},{7,5},{8,10},{9,11},{10,... | collective-permute-start | bytes 1572872 | tf_op jit(solution)/shard_map/ppermute | solution.py:400
  59.6 20.6 %collective-permute-start.23 = (f32[4,2,32,512]{3,2,1,0:T(8,128)}, f32[4,2,32,512]{3,2,1,0:T(8,128)}, u32[]{:S(2)}, u32[]{:S(2)}) collective-permute-start(f32[4,2,32,512]{3,2,1,0:T(8,128)} %collective-permute-done.21.r_3_), channel_id=1, source_target_pairs={{0,1},{1,0},{2,3},{3,2},{4,5},{5,4},{6,7},{7,6},{8,9},{9,8},{10,11... | collective-permute-start | bytes 1572872 | tf_op jit(solution)/shard_map/ppermute | solution.py:400
  59.7 35.5 %collective-permute-start.17 = (f32[4,2,32,512]{3,2,1,0:T(8,128)}, f32[4,2,32,512]{3,2,1,0:T(8,128)}, u32[]{:S(2)}, u32[]{:S(2)}) collective-permute-start(f32[4,2,32,512]{3,2,1,0:T(8,128)} %collective-permute-done.15.r_3_), channel_id=1, source_target_pairs={{0,1},{1,0},{2,3},{3,2},{4,5},{5,4},{6,7},{7,6},{8,9},{9,8},{10,11... | collective-permute-start | bytes 1572872 | tf_op jit(solution)/shard_map/ppermute | solution.py:400
  61.0 44.4 %collective-permute-start.10 = (f32[4,2,32,512]{3,2,1,0:T(8,128)}, f32[4,2,32,512]{3,2,1,0:T(8,128)}, u32[]{:S(2)}, u32[]{:S(2)}) collective-permute-start(f32[4,2,32,512]{3,2,1,0:T(8,128)} %pad_maximum_fusion.1.r_2_), channel_id=1, source_target_pairs={{0,1},{1,0},{2,3},{3,2},{4,5},{5,4},{6,7},{7,6},{8,9},{9,8},{10,11... | collective-permute-start | bytes 1572872 | tf_op jit(solution)/shard_map/ppermute | solution.py:400
  71.8 34.1 %collective-permute-start.11 = (f32[4,2,32,512]{3,2,1,0:T(8,128)}, f32[4,2,32,512]{3,2,1,0:T(8,128)S(1)}, u32[]{:S(2)}, u32[]{:S(2)}) collective-permute-start(f32[4,2,32,512]{3,2,1,0:T(8,128)} %collective-permute-done.9.r_3_), channel_id=1, source_target_pairs={{0,1},{1,0},{2,3},{3,2},{4,5},{5,4},{6,7},{7,6},{8,9},{9,8},{10,11... | collective-permute-start | bytes 1572872 | tf_op jit(solution)/shard_map/ppermute | solution.py:400
  80.2 36.0 %collective-permute-start.4 = (f32[4,2,32,512]{3,2,1,0:T(8,128)S(1)}, f32[4,2,32,512]{3,2,1,0:T(8,128)S(1)}, u32[]{:S(2)}, u32[]{:S(2)}) collective-permute-start(f32[4,2,32,512]{3,2,1,0:T(8,128)S(1)} %pad_maximum_fusion.r_2_), channel_id=1, source_target_pairs={{0,1},{1,0},{2,3},{3,2},{4,5},{5,4},{6,7},{7,6},{8,9},{9,8},{10,11... | collective-permute-start | bytes 1572872 | tf_op jit(solution)/shard_map/ppermute | solution.py:400
  80.2 36.0 %collective-permute-start.5 = (f32[4,2,32,512]{3,2,1,0:T(8,128)}, f32[4,2,32,512]{3,2,1,0:T(8,128)S(1)}, u32[]{:S(2)}, u32[]{:S(2)}) collective-permute-start(f32[4,2,32,512]{3,2,1,0:T(8,128)} %collective-permute-done.3.r_3_), channel_id=1, source_target_pairs={{0,1},{1,0},{2,3},{3,2},{4,5},{5,4},{6,7},{7,6},{8,9},{9,8},{10,11... | collective-permute-start | bytes 1572872 | tf_op jit(solution)/shard_map/ppermute | solution.py:400
  95.2 31.5 %collective-permute-start.29 = (f32[8,32,512]{2,1,0:T(8,128)S(1)}, f32[8,32,512]{2,1,0:T(8,128)S(1)}, u32[]{:S(2)}, u32[]{:S(2)}) collective-permute-start(f32[8,32,512]{2,1,0:T(8,128)S(1)} %get-tuple-element.58), channel_id=1, source_target_pairs={{0,1},{1,0},{2,3},{3,2},{4,5},{5,4},{6,7},{7,6},{8,9},{9,8},{10,11... | collective-permute-start | bytes 1572872 | tf_op jit(solution)/shard_map/ppermute | solution.py:400
  105.3 21.8 %collective-permute-start.31 = (f32[8,32,512]{2,1,0:T(8,128)S(1)}, f32[8,32,512]{2,1,0:T(8,128)S(1)}, u32[]{:S(2)}, u32[]{:S(2)}) collective-permute-start(f32[8,32,512]{2,1,0:T(8,128)S(1)} %get-tuple-element.60), channel_id=1, source_target_pairs={{0,1},{1,0},{2,3},{3,2},{4,5},{5,4},{6,7},{7,6},{8,9},{9,8},{10,11... | collective-permute-start | bytes 1572872 | tf_op jit(solution)/shard_map/ppermute | solution.py:400
  129.0 18.2 %collective-permute-start.34 = (f32[4,32,512]{2,1,0:T(8,128)S(1)}, f32[4,32,512]{2,1,0:T(8,128)S(1)}, u32[]{:S(2)}, u32[]{:S(2)}) collective-permute-start(f32[4,32,512]{2,1,0:T(8,128)S(1)} %slice_add_fusion), channel_id=1, source_target_pairs={{0,2},{1,3},{2,0},{3,1},{4,6},{5,7},{6,4},{7,5},{8,10},{9,11},{10,... | collective-permute-start | bytes 786440 | tf_op jit(solution)/shard_map/ppermute | solution.py:400
  129.4 22.5 %collective-permute-start.25 = (f32[4,32,512]{2,1,0:T(8,128)S(1)}, f32[4,32,512]{2,1,0:T(8,128)S(1)}, u32[]{:S(2)}, u32[]{:S(2)}) collective-permute-start(f32[4,32,512]{2,1,0:T(8,128)S(1)} %slice_add_fusion.3), channel_id=1, source_target_pairs={{0,2},{1,3},{2,0},{3,1},{4,6},{5,7},{6,4},{7,5},{8,10},{9,11},{10,... | collective-permute-start | bytes 786440 | tf_op jit(solution)/shard_map/ppermute | solution.py:400
  147.4 19.2 %collective-permute-start.36 = (f32[3,32,512]{2,1,0:T(8,128)S(1)}, f32[3,32,512]{2,1,0:T(8,128)S(1)}, u32[]{:S(2)}, u32[]{:S(2)}) collective-permute-start(f32[3,32,512]{2,1,0:T(8,128)S(1)} %pad_maximum_fusion.5), channel_id=1, source_target_pairs={{0,8},{1,9},{2,10},{3,11},{4,12},{5,13},{6,14},{7,15},{8,0},{9,1},... | collective-permute-start | bytes 589832 | tf_op jit(solution)/shard_map/ppermute | solution.py:400
  148.4 18.2 %collective-permute-start.37 = (f32[3,32,512]{2,1,0:T(8,128)S(1)}, f32[3,32,512]{2,1,0:T(8,128)S(1)}, u32[]{:S(2)}, u32[]{:S(2)}) collective-permute-start(f32[3,32,512]{2,1,0:T(8,128)S(1)} %pad_maximum_fusion.6), channel_id=1, source_target_pairs={{0,12},{1,13},{2,14},{3,15},{4,8},{5,9},{6,10},{7,11},{8,4},{9,5},... | collective-permute-start | bytes 589832 | tf_op jit(solution)/shard_map/ppermute | solution.py:400
  152.0 15.8 %collective-permute-start.26 = (f32[32,512]{1,0:T(8,128)S(1)}, f32[32,512]{1,0:T(8,128)S(1)}, u32[]{:S(2)}, u32[]{:S(2)}) collective-permute-start(f32[32,512]{1,0:T(8,128)S(1)} %get-tuple-element.77), channel_id=1, source_target_pairs={{0,4},{1,5},{2,6},{3,7},{4,0},{5,1},{6,2},{7,3},{8,12},{9,13},{10,... | collective-permute-start | bytes 196616 | tf_op jit(solution)/shard_map/ppermute | solution.py:400
  152.1 18.9 %collective-permute-start.27 = (f32[32,512]{1,0:T(8,128)S(1)}, f32[32,512]{1,0:T(8,128)S(1)}, u32[]{:S(2)}, u32[]{:S(2)}) collective-permute-start(f32[32,512]{1,0:T(8,128)S(1)} %get-tuple-element.76), channel_id=1, source_target_pairs={{0,8},{1,9},{2,10},{3,11},{4,12},{5,13},{6,14},{7,15},{8,0},{9,1},... | collective-permute-start | bytes 196616 | tf_op jit(solution)/shard_map/ppermute | solution.py:400
  (25 other events, 287.7 us)

commit v3 on v2

--- a/solution.py
+++ b/solution.py
@@ -108,21 +108,25 @@
 def prep_models_kernel(depths, vel, ani, *outs):
     _, R, NY = vel.shape
     nb = NY // LANES
-    for n, d in enumerate(depths):
+    for d in range(vel.shape[0]) if len(outs) > len(depths) else depths:
         for m, ref in enumerate((vel, ani)):
             for j in range(R // SUB):
                 rows = slice(j * SUB, (j + 1) * SUB)
                 new = spread([ref[d, rows, cut(b)] for b in range(nb)])
                 for b in range(nb):
-                    outs[n][m, rows, cut(b)] = new[b]
-
-
-def prep_models(vel, ani, depths):
-    _, R, NY = vel.shape
+                    if d in depths:
+                        outs[depths.index(d)][m, rows, cut(b)] = new[b]
+                    if len(outs) > len(depths):
+                        outs[-1][d, m, rows, cut(b)] = new[b]
+
+
+def prep_models(vel, ani, depths, everything):
+    depth, R, NY = vel.shape
     _, vmem, _ = spaces()
+    shapes = [(2, R, NY)] * len(depths) + [(depth, 2, R, NY)] * everything
     return pl.pallas_call(
-        lambda *r: prep_models_kernel(depths, *r), out_shape=[jax.ShapeDtypeStruct((2, R, NY), jnp.float32)] * len(depths),
-        in_specs=[vmem] * 2, out_specs=[vmem] * len(depths),
+        lambda *r: prep_models_kernel(depths, *r), out_shape=[jax.ShapeDtypeStruct(x, jnp.float32) for x in shapes],
+        in_specs=[vmem] * 2, out_specs=[vmem] * len(shapes),
         name="prep_models", compiler_params=pltpu.CompilerParams(vmem_limit_bytes=4 << 20),
     )(vel, ani)
 
@@ -271,9 +275,9 @@
     lo = where[1]
     bases = [lo * R, (1 - lo) * R][: G // R]
     places = [[None] * SUB for _ in bases]
-    for ref, (k0, kb, half) in zip(blks, metas):
+    for ref, (k0, kb, half, first) in zip(blks, metas):
         for k in range(kb):
-            places[half][k0 + k] = (ref, k)
+            places[half][k0 + k] = (ref, first + k)
     halos, sweep = wave_tools(where, G, NB)
     om = om_ref[0]
     k1 = 6.0 / om
@@ -405,33 +409,38 @@
     depth_count, R, _ = velocity.shape
     G = R * lax.axis_size("freq") // SUB
     where = jnp.stack([me >> 1, me & 1]).astype(jnp.int32)
-    own = list(prep_models(velocity, anisotropy, (0,)))
-    own += prep_models(velocity, anisotropy, tuple(range(1, depth_count)))
+    own = list(prep_models(velocity, anisotropy, (0,), False))
+    *rest, all_own = prep_models(velocity, anisotropy, tuple(range(1, depth_count)), True)
+    own += rest
     state = [prep_field(where, source, 0, 1.0, G)]
     state.append(prep_field(where, receiver, 0, -1.0, G))
-    metas = [(0, HALF, 0), (HALF, HALF, 0), (0, HALF, 1), (HALF, HALF, 1)]
-    early = []
+    all_near = swap(all_own, 2)
+    shared = [all_own, all_near, swap(all_own, 1), swap(all_near, 1)]
+    corners = [(0, 0), (HALF, 0), (0, 1), (HALF, 1)]
+    sums = []
     for d in range(depth_count):
         last = d == depth_count - 1
-        parts = [own[d]] + [swap(own[d], far << 2) for far in range(1, HALF)]
+        parts = [swap(own[d], far << 2) for far in range(1, HALF)]
         mine = jnp.stack(parts)
         near = swap(mine, 2)
-        blocks = [mine, near, swap(mine, 1), swap(near, 1)]
+        blocks = shared + [mine, near, swap(mine, 1), swap(near, 1)]
+        metas = [(k0, 1, half, d) for k0, half in corners] + [(k0 + 1, HALF - 1, half, 0) for k0, half in corners]
         mid = first_call(where, omega, blocks, metas, state, R)
         kept, sent, *state = second_call(where, *mid, last, R)
         got = swap(sent, 1)
         upper = kept[HALF:] + got[HALF:]
-        near = swap(upper, 2)
-        if not last:
-            early.append((kept, got, near))
-        if d == depth_count - 2:
-            parts = [jnp.stack([(k[far] + g[far]) + n[far] for k, g, n in early]) for far in range(HALF)]
-            parts = [parts[0]] + [swap(parts[far], far << 2) for far in range(1, HALF)]
-            before = finish_early(scale, sum(parts[1:], parts[0]))
-        if last:
-            parts = [(kept[far] + got[far]) + near[far] for far in range(HALF)]
-            parts = [parts[0]] + [swap(parts[far], far << 2) for far in range(1, HALF)]
-            return finish_last(scale, parts, before)
+        sums.append((kept, got, swap(upper, 2)))
+
+    def z_sum(chosen):
+        many = [[(k[far] + g[far]) + n[far] for k, g, n in chosen] for far in range(HALF)]
+        parts = [x[0] if len(x) == 1 else jnp.stack(x) for x in many]
+        return [parts[0]] + [swap(parts[far], far << 2) for far in range(1, HALF)]
+
+    early = z_sum(sums[:-2])
+    middle = z_sum(sums[-2:-1])
+    tail = z_sum(sums[-1:])
+    before = finish_early(scale, jnp.concatenate([sum(early[1:], early[0]), sum(middle[1:], middle[0])[None]]))
+    return finish_last(scale, tail, before)
 
 
 def apart(x):
@@ -460,7 +469,7 @@
         total = None
         for p, state in enumerate(states):
             last = d == depth_count - 1
-            mid = first_call(where, omega[p : p + 1], [both[d]], [(0, SUB, 0)], state, G)
+            mid = first_call(where, omega[p : p + 1], [both[d]], [(0, SUB, 0, 0)], state, G)
             res = second_call(where, *mid, last, G)
             total = res[0] if total is None else total + res[0]
             states[p] = None if last else res[1:]

time: 173 us -> 169 us (0.977)
  waiting for transfers between devices: 66.2 us -> 47.8 us
  starting transfers between devices: 47.1 us -> 58.9 us
    ppermute x38 -> x44, waiting for transfers between devices: 66.2 us -> 47.8 us  [swap(): return lax.ppermute(x, 'freq', [(i, i ^ mask) for i in range(n)])]
    ppermute x38 -> x44, starting transfers between devices: 47.1 us -> 58.9 us  [swap(): return lax.ppermute(x, 'freq', [(i, i ^ mask) for i in range(n)])]
  transfers between devices with their start and end apart: 38 -> 44, of which waited for: 14 -> 13; matrix products, arithmetic and copies ran while one was open for 1% -> 1% of each run, Pallas kernels for 30% -> 31%
where the time goes in v3:
time: 169 us; the launch traced here: 168 us
  starting transfers between devices  58.9 us (35%)
  Pallas kernels  53.9 us (32%)
  waiting for transfers between devices  47.8 us (28%)
  local copies, waits for them, and re-layouts  5 us (3%)
  other arithmetic  2.05 us (1%)
    ppermute x44, starting transfers between devices, swap(): return lax.ppermute(x, 'freq', [(i, i ^ mask) for i in range(n)])  58.9 us
    ppermute x44, waiting for transfers between devices, swap(): return lax.ppermute(x, 'freq', [(i, i ^ mask) for i in range(n)])  47.8 us
    pallas_call x4, Pallas kernels, first_call(): pl.pallas_call(lambda *r: first_kernel(dict(metas=metas, R=R), *r), out_s...  22.3 us
    pallas_call x4, Pallas kernels, second_call(): pl.pallas_call(lambda *r: second_kernel(dict(last=last, R=R), *r), out_sh...  17.6 us
    pallas_call x2, Pallas kernels, prep_field(): pl.pallas_call(lambda *r: prep_field_kernel(p, sign, *r), out_shape=jax.S...  8.8 us
    unnamed x22, local copies, waits for them, and re-layouts  5 us
  transfers between devices with their start and end apart: 44, of which 13 were waited for; matrix products, arithmetic and copies ran while one was open for 1% of the time, Pallas kernels for 31%

profile of v3, /device:TPU:0, one launch (start us, length us, event | category | flops | bytes accessed | tf_op | source)
XLA Modules:
  0.0 168.2 jit_solution(1506043838859928524)
XLA Ops:
  2.2 3.1 %collective-permute-start.21 = (f32[2,32,512]{2,1,0:T(8,128)S(1)}, f32[2,32,512]{2,1,0:T(8,128)S(1)}, u32[]{:S(2)}, u32[]{:S(2)}) collective-permute-start(f32[2,32,512]{2,1,0:T(8,128)S(1)} %prep_models.3), channel_id=1, source_target_pairs={{0,4},{1,5},{2,6},{3,7},{4,0},{5,1},{6,2},{7,3},{8,12},{9,13},{10,... | collective-permute-start | bytes 393224 | tf_op jit(solution)/shard_map/ppermute | solution.py:404
  13.0 3.5 %collective-permute-start.16 = (f32[2,32,512]{2,1,0:T(8,128)S(1)}, f32[2,32,512]{2,1,0:T(8,128)S(1)}, u32[]{:S(2)}, u32[]{:S(2)}) collective-permute-start(f32[2,32,512]{2,1,0:T(8,128)S(1)} %get-tuple-element.38), channel_id=1, source_target_pairs={{0,8},{1,9},{2,10},{3,11},{4,12},{5,13},{6,14},{7,15},{8,0},{9,1},... | collective-permute-start | bytes 393224 | tf_op jit(solution)/shard_map/ppermute | solution.py:404
  18.2 2.8 %collective-permute-start.17 = (f32[2,32,512]{2,1,0:T(8,128)S(1)}, f32[2,32,512]{2,1,0:T(8,128)S(1)}, u32[]{:S(2)}, u32[]{:S(2)}) collective-permute-start(f32[2,32,512]{2,1,0:T(8,128)S(1)} %get-tuple-element.38), channel_id=1, source_target_pairs={{0,12},{1,13},{2,14},{3,15},{4,8},{5,9},{6,10},{7,11},{8,4},{9,5},... | collective-permute-start | bytes 393224 | tf_op jit(solution)/shard_map/ppermute | solution.py:404
  22.0 9.3 %collective-permute-start.9 = (f32[2,32,512]{2,1,0:T(8,128)S(1)}, f32[2,32,512]{2,1,0:T(8,128)S(1)}, u32[]{:S(2)}, u32[]{:S(2)}) collective-permute-start(f32[2,32,512]{2,1,0:T(8,128)S(1)} %get-tuple-element.37), channel_id=1, source_target_pairs={{0,4},{1,5},{2,6},{3,7},{4,0},{5,1},{6,2},{7,3},{8,12},{9,13},{10,... | collective-permute-start | bytes 393224 | tf_op jit(solution)/shard_map/ppermute | solution.py:404
  36.4 3.4 %collective-permute-start.3 = (f32[2,32,512]{2,1,0:T(8,128)S(1)}, f32[2,32,512]{2,1,0:T(8,128)S(1)}, u32[]{:S(2)}, u32[]{:S(2)}) collective-permute-start(f32[2,32,512]{2,1,0:T(8,128)S(1)} %get-tuple-element.36), channel_id=1, source_target_pairs={{0,4},{1,5},{2,6},{3,7},{4,0},{5,1},{6,2},{7,3},{8,12},{9,13},{10,... | collective-permute-start | bytes 393224 | tf_op jit(solution)/shard_map/ppermute | solution.py:404
  42.3 3.9 %collective-permute-done.3 = f32[2,32,512]{2,1,0:T(8,128)S(1)} collective-permute-done((f32[2,32,512]{2,1,0:T(8,128)S(1)}, f32[2,32,512]{2,1,0:T(8,128)S(1)}, u32[]{:S(2)}, u32[]{:S(2)}) %collective-permute-start.3) | collective-permute-done | bytes 131104 | tf_op jit(solution)/shard_map/ppermute | solution.py:404
  47.8 6.5 %collective-permute-done.4 = f32[2,32,512]{2,1,0:T(8,128)S(1)} collective-permute-done((f32[2,32,512]{2,1,0:T(8,128)S(1)}, f32[2,32,512]{2,1,0:T(8,128)S(1)}, u32[]{:S(2)}, u32[]{:S(2)}) %collective-permute-start.4) | collective-permute-done | bytes 131104 | tf_op jit(solution)/shard_map/ppermute | solution.py:404
  59.0 8.9 %collective-permute-done.18.r_7_ = f32[3,2,32,512]{3,2,1,0:T(8,128)} collective-permute-done((f32[3,2,32,512]{3,2,1,0:T(8,128)}, f32[3,2,32,512]{3,2,1,0:T(8,128)}, u32[]{:S(2)}, u32[]{:S(2)}) %collective-permute-start.18) | collective-permute-done | bytes 393248 | tf_op jit(solution)/shard_map/ppermute | solution.py:404
  72.3 4.5 %prep_field.2.r_10_ = f32[2,64,8,512]{3,2,1,0:T(8,128)S(1)} custom-call(s32[2]{0:T(128)S(1)} %pad_add_fusion.r_0_, f32[1,2,512,512]{3,2,1,0:T(8,128)S(1)} %copy-done), custom_call_target="tpu_custom_call" | custom-call | tf_op jit(solution)/shard_map/prep_field/pallas_call | solution.py:158
  76.9 4.3 %prep_field.3.r_11_ = f32[2,64,8,512]{3,2,1,0:T(8,128)S(1)} custom-call(s32[2]{0:T(128)S(1)} %pad_add_fusion.r_0_, f32[1,2,512,512]{3,2,1,0:T(8,128)S(1)} %copy-done.1), custom_call_target="tpu_custom_call" | custom-call | tf_op jit(solution)/shard_map/prep_field/pallas_call | solution.py:158
  81.8 5.1 %first_half.4 = (f32[4,66,8,512]{3,2,1,0:T(8,128)S(1)}, f32[4,66,8,512]{3,2,1,0:T(8,128)S(1)}, f32[2,64,8,512]{3,2,1,0:T(8,128)S(1)}) custom-call(s32[2]{0:T(128)S(1)} %pad_add_fusion.r_0_, f32[1]{0:T(128)} %bitcast.4.r_1_, f32[4,2,32,512]{3,2,1,0:T(8,128)S(1)} %get-tuple-element.35.r_2_, f32[4,2,32,512]{3,2,1,0:T(8,128)S(1)} %collective-permute-done.r_3_, ...), custom_call_target="tpu_custom_call" | custom-call | tf_op jit(solution)/shard_map/first_half/pallas_call | solution.py:373
  86.9 4.4 %second_half.4 = (f32[8,32,512]{2,1,0:T(8,128)S(1)}, f32[8,32,512]{2,1,0:T(8,128)S(1)}, f32[2,64,8,512]{3,2,1,0:T(8,128)S(1)}, f32[2,64,8,512]{3,2,1,0:T(8,128)S(1)}) custom-call(s32[2]{0:T(128)S(1)} %pad_add_fusion.r_0_, f32[4,66,8,512]{3,2,1,0:T(8,128)S(1)} %get-tuple-element.39.r_1_, f32[4,66,8,512]{3,2,1,0:T(8,128)S(1)} %get-tuple-element.40.r_2_, ...), custom_call_target="tpu_custom_call" | custom-call | tf_op jit(solution)/shard_map/second_half/pallas_call | solution.py:391
  92.5 6.0 %first_half.5 = (f32[4,66,8,512]{3,2,1,0:T(8,128)S(1)}, f32[4,66,8,512]{3,2,1,0:T(8,128)S(1)}, f32[2,64,8,512]{3,2,1,0:T(8,128)S(1)}) custom-call(s32[2]{0:T(128)S(1)} %pad_add_fusion.r_0_, f32[1]{0:T(128)} %bitcast.4.r_1_, f32[4,2,32,512]{3,2,1,0:T(8,128)S(1)} %get-tuple-element.35.r_2_, f32[4,2,32,512]{3,2,1,0:T(8,128)S(1)} %collective-permute-done.r_3_, ...), custom_call_target="tpu_custom_call" | custom-call | tf_op jit(solution)/shard_map/first_half/pallas_call | solution.py:373
  98.5 4.4 %second_half.5 = (f32[8,32,512]{2,1,0:T(8,128)S(1)}, f32[8,32,512]{2,1,0:T(8,128)S(1)}, f32[2,64,8,512]{3,2,1,0:T(8,128)S(1)}, f32[2,64,8,512]{3,2,1,0:T(8,128)S(1)}) custom-call(s32[2]{0:T(128)S(1)} %pad_add_fusion.r_0_, f32[4,66,8,512]{3,2,1,0:T(8,128)S(1)} %get-tuple-element.44.r_1_, f32[4,66,8,512]{3,2,1,0:T(8,128)S(1)} %get-tuple-element.45.r_2_, ...), custom_call_target="tpu_custom_call" | custom-call | tf_op jit(solution)/shard_map/second_half/pallas_call | solution.py:391
  103.1 5.6 %first_half.6 = (f32[4,66,8,512]{3,2,1,0:T(8,128)S(1)}, f32[4,66,8,512]{3,2,1,0:T(8,128)S(1)}, f32[2,64,8,512]{3,2,1,0:T(8,128)S(1)}) custom-call(s32[2]{0:T(128)S(1)} %pad_add_fusion.r_0_, f32[1]{0:T(128)} %bitcast.4.r_1_, f32[4,2,32,512]{3,2,1,0:T(8,128)S(1)} %get-tuple-element.35.r_2_, f32[4,2,32,512]{3,2,1,0:T(8,128)S(1)} %collective-permute-done.r_3_, ...), custom_call_target="tpu_custom_call" | custom-call | tf_op jit(solution)/shard_map/first_half/pallas_call | solution.py:373
  108.7 4.4 %second_half.6 = (f32[8,32,512]{2,1,0:T(8,128)S(1)}, f32[8,32,512]{2,1,0:T(8,128)S(1)}, f32[2,64,8,512]{3,2,1,0:T(8,128)S(1)}, f32[2,64,8,512]{3,2,1,0:T(8,128)S(1)}) custom-call(s32[2]{0:T(128)S(1)} %pad_add_fusion.r_0_, f32[4,66,8,512]{3,2,1,0:T(8,128)S(1)} %get-tuple-element.49.r_1_, f32[4,66,8,512]{3,2,1,0:T(8,128)S(1)} %get-tuple-element.50.r_2_, ...), custom_call_target="tpu_custom_call" | custom-call | tf_op jit(solution)/shard_map/second_half/pallas_call | solution.py:391
  113.5 5.6 %first_half.7 = (f32[4,66,8,512]{3,2,1,0:T(8,128)S(1)}, f32[4,66,8,512]{3,2,1,0:T(8,128)S(1)}, f32[2,64,8,512]{3,2,1,0:T(8,128)S(1)}) custom-call(s32[2]{0:T(128)S(1)} %pad_add_fusion.r_0_, f32[1]{0:T(128)} %bitcast.4.r_1_, f32[4,2,32,512]{3,2,1,0:T(8,128)S(1)} %get-tuple-element.35.r_2_, f32[4,2,32,512]{3,2,1,0:T(8,128)S(1)} %collective-permute-done.r_3_, ...), custom_call_target="tpu_custom_call" | custom-call | tf_op jit(solution)/shard_map/first_half/pallas_call | solution.py:373
  119.2 4.4 %second_half.7 = (f32[8,32,512]{2,1,0:T(8,128)S(1)}, f32[8,32,512]{2,1,0:T(8,128)S(1)}) custom-call(s32[2]{0:T(128)S(1)} %pad_add_fusion.r_0_, f32[4,66,8,512]{3,2,1,0:T(8,128)S(1)} %get-tuple-element.54.r_1_, f32[4,66,8,512]{3,2,1,0:T(8,128)S(1)} %get-tuple-element.55.r_2_, f32[2,64,8,512]{3,2,1,0:T(8,128)S(1)} %get-tuple-element.56.r_3_), custom_call_target="tpu_custom_call" | custom-call | tf_op jit(solution)/shard_map/second_half/pallas_call | solution.py:391
  128.1 4.8 %collective-permute-done.33 = f32[4,32,512]{2,1,0:T(8,128)S(1)} collective-permute-done((f32[4,32,512]{2,1,0:T(8,128)S(1)}, f32[4,32,512]{2,1,0:T(8,128)S(1)}, u32[]{:S(2)}, u32[]{:S(2)}) %collective-permute-start.33) | collective-permute-done | bytes 262176 | tf_op jit(solution)/shard_map/ppermute | solution.py:404
  133.0 5.5 %collective-permute-done.35 = f32[4,32,512]{2,1,0:T(8,128)S(1)} collective-permute-done((f32[4,32,512]{2,1,0:T(8,128)S(1)}, f32[4,32,512]{2,1,0:T(8,128)S(1)}, u32[]{:S(2)}, u32[]{:S(2)}) %collective-permute-start.35) | collective-permute-done | bytes 262176 | tf_op jit(solution)/shard_map/ppermute | solution.py:404
  141.1 3.1 %collective-permute-done.40 = f32[4,32,512]{2,1,0:T(8,128)S(1)} collective-permute-done((f32[4,32,512]{2,1,0:T(8,128)S(1)}, f32[4,32,512]{2,1,0:T(8,128)S(1)}, u32[]{:S(2)}, u32[]{:S(2)}) %collective-permute-start.40) | collective-permute-done | bytes 262176 | tf_op jit(solution)/shard_map/ppermute | solution.py:404
  153.3 2.7 %collective-permute-done.43 = f32[32,512]{1,0:T(8,128)S(1)} collective-permute-done((f32[32,512]{1,0:T(8,128)S(1)}, f32[32,512]{1,0:T(8,128)S(1)}, u32[]{:S(2)}, u32[]{:S(2)}) %collective-permute-start.43) | collective-permute-done | bytes 65568 | tf_op jit(solution)/shard_map/ppermute | solution.py:404
  156.0 4.6 %collective-permute-start.30 = (f32[32,512]{1,0:T(8,128)S(1)}, f32[32,512]{1,0:T(8,128)S(1)}, u32[]{:S(2)}, u32[]{:S(2)}) collective-permute-start(f32[32,512]{1,0:T(8,128)S(1)} %get-tuple-element.77), channel_id=1, source_target_pairs={{0,8},{1,9},{2,10},{3,11},{4,12},{5,13},{6,14},{7,15},{8,0},{9,1},... | collective-permute-start | bytes 196616 | tf_op jit(solution)/shard_map/ppermute | solution.py:404
  162.1 2.8 %collective-permute-done.30.r_2_ = f32[32,512]{1,0:T(8,128)S(1)} collective-permute-done((f32[32,512]{1,0:T(8,128)S(1)}, f32[32,512]{1,0:T(8,128)S(1)}, u32[]{:S(2)}, u32[]{:S(2)}) %collective-permute-start.30) | collective-permute-done | bytes 65568 | tf_op jit(solution)/shard_map/ppermute | solution.py:404
  (120 shorter events, 53.8 us)
Async XLA Ops:
  5.3 12.9 %collective-permute-start.22 = (f32[2,32,512]{2,1,0:T(8,128)S(1)}, f32[2,32,512]{2,1,0:T(8,128)S(1)}, u32[]{:S(2)}, u32[]{:S(2)}) collective-permute-start(f32[2,32,512]{2,1,0:T(8,128)S(1)} %prep_models.3), channel_id=1, source_target_pairs={{0,8},{1,9},{2,10},{3,11},{4,12},{5,13},{6,14},{7,15},{8,0},{9,1},... | collective-permute-start | bytes 393224 | tf_op jit(solution)/shard_map/ppermute | solution.py:404
  7.9 13.1 %collective-permute-start.23 = (f32[2,32,512]{2,1,0:T(8,128)S(1)}, f32[2,32,512]{2,1,0:T(8,128)S(1)}, u32[]{:S(2)}, u32[]{:S(2)}) collective-permute-start(f32[2,32,512]{2,1,0:T(8,128)S(1)} %prep_models.3), channel_id=1, source_target_pairs={{0,12},{1,13},{2,14},{3,15},{4,8},{5,9},{6,10},{7,11},{8,4},{9,5},... | collective-permute-start | bytes 393224 | tf_op jit(solution)/shard_map/ppermute | solution.py:404
  10.5 43.8 %collective-permute-start = (f32[4,2,32,512]{3,2,1,0:T(8,128)S(1)}, f32[4,2,32,512]{3,2,1,0:T(8,128)S(1)}, u32[]{:S(2)}, u32[]{:S(2)}) collective-permute-start(f32[4,2,32,512]{3,2,1,0:T(8,128)S(1)} %get-tuple-element.35.r_2_), channel_id=1, source_target_pairs={{0,2},{1,3},{2,0},{3,1},{4,6},{5,7},{6,4},{7,5},{8,10},{9,11},{10,... | collective-permute-start | bytes 1572872 | tf_op jit(solution)/shard_map/ppermute | solution.py:404
  13.0 19.2 %collective-permute-start.16 = (f32[2,32,512]{2,1,0:T(8,128)S(1)}, f32[2,32,512]{2,1,0:T(8,128)S(1)}, u32[]{:S(2)}, u32[]{:S(2)}) collective-permute-start(f32[2,32,512]{2,1,0:T(8,128)S(1)} %get-tuple-element.38), channel_id=1, source_target_pairs={{0,8},{1,9},{2,10},{3,11},{4,12},{5,13},{6,14},{7,15},{8,0},{9,1},... | collective-permute-start | bytes 393224 | tf_op jit(solution)/shard_map/ppermute | solution.py:404
  18.2 15.6 %collective-permute-start.17 = (f32[2,32,512]{2,1,0:T(8,128)S(1)}, f32[2,32,512]{2,1,0:T(8,128)S(1)}, u32[]{:S(2)}, u32[]{:S(2)}) collective-permute-start(f32[2,32,512]{2,1,0:T(8,128)S(1)} %get-tuple-element.38), channel_id=1, source_target_pairs={{0,12},{1,13},{2,14},{3,15},{4,8},{5,9},{6,10},{7,11},{8,4},{9,5},... | collective-permute-start | bytes 393224 | tf_op jit(solution)/shard_map/ppermute | solution.py:404
  21.0 15.4 %collective-permute-start.11 = (f32[2,32,512]{2,1,0:T(8,128)S(1)}, f32[2,32,512]{2,1,0:T(8,128)S(1)}, u32[]{:S(2)}, u32[]{:S(2)}) collective-permute-start(f32[2,32,512]{2,1,0:T(8,128)S(1)} %get-tuple-element.37), channel_id=1, source_target_pairs={{0,12},{1,13},{2,14},{3,15},{4,8},{5,9},{6,10},{7,11},{8,4},{9,5},... | collective-permute-start | bytes 393224 | tf_op jit(solution)/shard_map/ppermute | solution.py:404
  22.0 14.4 %collective-permute-start.9 = (f32[2,32,512]{2,1,0:T(8,128)S(1)}, f32[2,32,512]{2,1,0:T(8,128)S(1)}, u32[]{:S(2)}, u32[]{:S(2)}) collective-permute-start(f32[2,32,512]{2,1,0:T(8,128)S(1)} %get-tuple-element.37), channel_id=1, source_target_pairs={{0,4},{1,5},{2,6},{3,7},{4,0},{5,1},{6,2},{7,3},{8,12},{9,13},{10,... | collective-permute-start | bytes 393224 | tf_op jit(solution)/shard_map/ppermute | solution.py:404
  32.2 24.9 %collective-permute-start.24 = (f32[3,2,32,512]{3,2,1,0:T(8,128)S(1)}, f32[3,2,32,512]{3,2,1,0:T(8,128)S(1)}, u32[]{:S(2)}, u32[]{:S(2)}) collective-permute-start(f32[3,2,32,512]{3,2,1,0:T(8,128)S(1)} %pad_maximum_fusion.3.r_6_), channel_id=1, source_target_pairs={{0,2},{1,3},{2,0},{3,1},{4,6},{5,7},{6,4},{7,5},{8,10},{9,11},{10,... | collective-permute-start | bytes 1179656 | tf_op jit(solution)/shard_map/ppermute | solution.py:404
  36.4 20.7 %collective-permute-start.1 = (f32[4,2,32,512]{3,2,1,0:T(8,128)S(1)}, f32[4,2,32,512]{3,2,1,0:T(8,128)S(1)}, u32[]{:S(2)}, u32[]{:S(2)}) collective-permute-start(f32[4,2,32,512]{3,2,1,0:T(8,128)S(1)} %get-tuple-element.35.r_2_), channel_id=1, source_target_pairs={{0,1},{1,0},{2,3},{3,2},{4,5},{5,4},{6,7},{7,6},{8,9},{9,8},{10,11... | collective-permute-start | bytes 1572872 | tf_op jit(solution)/shard_map/ppermute | solution.py:404
  54.3 15.9 %collective-permute-start.2 = (f32[4,2,32,512]{3,2,1,0:T(8,128)S(1)}, f32[4,2,32,512]{3,2,1,0:T(8,128)S(1)}, u32[]{:S(2)}, u32[]{:S(2)}) collective-permute-start(f32[4,2,32,512]{3,2,1,0:T(8,128)S(1)} %collective-permute-done.r_3_), channel_id=1, source_target_pairs={{0,1},{1,0},{2,3},{3,2},{4,5},{5,4},{6,7},{7,6},{8,9},{9,8},{10,11... | collective-permute-start | bytes 1572872 | tf_op jit(solution)/shard_map/ppermute | solution.py:404
  57.1 34.3 %collective-permute-start.19 = (f32[3,2,32,512]{3,2,1,0:T(8,128)}, f32[3,2,32,512]{3,2,1,0:T(8,128)}, u32[]{:S(2)}, u32[]{:S(2)}) collective-permute-start(f32[3,2,32,512]{3,2,1,0:T(8,128)} %pad_maximum_fusion.2.r_6_), channel_id=1, source_target_pairs={{0,1},{1,0},{2,3},{3,2},{4,5},{5,4},{6,7},{7,6},{8,9},{9,8},{10,11... | collective-permute-start | bytes 1179656 | tf_op jit(solution)/shard_map/ppermute | solution.py:404
  58.4 33.1 %collective-permute-start.12 = (f32[3,2,32,512]{3,2,1,0:T(8,128)S(1)}, f32[3,2,32,512]{3,2,1,0:T(8,128)}, u32[]{:S(2)}, u32[]{:S(2)}) collective-permute-start(f32[3,2,32,512]{3,2,1,0:T(8,128)S(1)} %pad_maximum_fusion.1.r_6_), channel_id=1, source_target_pairs={{0,2},{1,3},{2,0},{3,1},{4,6},{5,7},{6,4},{7,5},{8,10},{9,11},{10,... | collective-permute-start | bytes 1179656 | tf_op jit(solution)/shard_map/ppermute | solution.py:404
  67.9 24.1 %collective-permute-start.6 = (f32[3,2,32,512]{3,2,1,0:T(8,128)S(1)}, f32[3,2,32,512]{3,2,1,0:T(8,128)}, u32[]{:S(2)}, u32[]{:S(2)}) collective-permute-start(f32[3,2,32,512]{3,2,1,0:T(8,128)S(1)} %pad_maximum_fusion.r_6_), channel_id=1, source_target_pairs={{0,2},{1,3},{2,0},{3,1},{4,6},{5,7},{6,4},{7,5},{8,10},{9,11},{10,... | collective-permute-start | bytes 1179656 | tf_op jit(solution)/shard_map/ppermute | solution.py:404
  70.2 21.9 %collective-permute-start.20 = (f32[3,2,32,512]{3,2,1,0:T(8,128)}, f32[3,2,32,512]{3,2,1,0:T(8,128)}, u32[]{:S(2)}, u32[]{:S(2)}) collective-permute-start(f32[3,2,32,512]{3,2,1,0:T(8,128)} %collective-permute-done.18.r_7_), channel_id=1, source_target_pairs={{0,1},{1,0},{2,3},{3,2},{4,5},{5,4},{6,7},{7,6},{8,9},{9,8},{10,11... | collective-permute-start | bytes 1179656 | tf_op jit(solution)/shard_map/ppermute | solution.py:404
  70.2 32.7 %collective-permute-start.13 = (f32[3,2,32,512]{3,2,1,0:T(8,128)S(1)}, f32[3,2,32,512]{3,2,1,0:T(8,128)S(1)}, u32[]{:S(2)}, u32[]{:S(2)}) collective-permute-start(f32[3,2,32,512]{3,2,1,0:T(8,128)S(1)} %pad_maximum_fusion.1.r_6_), channel_id=1, source_target_pairs={{0,1},{1,0},{2,3},{3,2},{4,5},{5,4},{6,7},{7,6},{8,9},{9,8},{10,11... | collective-permute-start | bytes 1179656 | tf_op jit(solution)/shard_map/ppermute | solution.py:404
  91.4 32.3 %collective-permute-start.32 = (f32[8,32,512]{2,1,0:T(8,128)S(1)}, f32[8,32,512]{2,1,0:T(8,128)S(1)}, u32[]{:S(2)}, u32[]{:S(2)}) collective-permute-start(f32[8,32,512]{2,1,0:T(8,128)S(1)} %get-tuple-element.60), channel_id=1, source_target_pairs={{0,1},{1,0},{2,3},{3,2},{4,5},{5,4},{6,7},{7,6},{8,9},{9,8},{10,11... | collective-permute-start | bytes 1572872 | tf_op jit(solution)/shard_map/ppermute | solution.py:404
  92.0 21.6 %collective-permute-start.7 = (f32[3,2,32,512]{3,2,1,0:T(8,128)S(1)}, f32[3,2,32,512]{3,2,1,0:T(8,128)S(1)}, u32[]{:S(2)}, u32[]{:S(2)}) collective-permute-start(f32[3,2,32,512]{3,2,1,0:T(8,128)S(1)} %pad_maximum_fusion.r_6_), channel_id=1, source_target_pairs={{0,1},{1,0},{2,3},{3,2},{4,5},{5,4},{6,7},{7,6},{8,9},{9,8},{10,11... | collective-permute-start | bytes 1179656 | tf_op jit(solution)/shard_map/ppermute | solution.py:404
  92.1 21.5 %collective-permute-start.8 = (f32[3,2,32,512]{3,2,1,0:T(8,128)}, f32[3,2,32,512]{3,2,1,0:T(8,128)S(1)}, u32[]{:S(2)}, u32[]{:S(2)}) collective-permute-start(f32[3,2,32,512]{3,2,1,0:T(8,128)} %collective-permute-done.6.r_7_), channel_id=1, source_target_pairs={{0,1},{1,0},{2,3},{3,2},{4,5},{5,4},{6,7},{7,6},{8,9},{9,8},{10,11... | collective-permute-start | bytes 1179656 | tf_op jit(solution)/shard_map/ppermute | solution.py:404
  102.9 21.4 %collective-permute-start.34 = (f32[8,32,512]{2,1,0:T(8,128)S(1)}, f32[8,32,512]{2,1,0:T(8,128)S(1)}, u32[]{:S(2)}, u32[]{:S(2)}) collective-permute-start(f32[8,32,512]{2,1,0:T(8,128)S(1)} %get-tuple-element.62), channel_id=1, source_target_pairs={{0,1},{1,0},{2,3},{3,2},{4,5},{5,4},{6,7},{7,6},{8,9},{9,8},{10,11... | collective-permute-start | bytes 1572872 | tf_op jit(solution)/shard_map/ppermute | solution.py:404
  124.3 14.2 %collective-permute-start.35 = (f32[4,32,512]{2,1,0:T(8,128)S(1)}, f32[4,32,512]{2,1,0:T(8,128)S(1)}, u32[]{:S(2)}, u32[]{:S(2)}) collective-permute-start(f32[4,32,512]{2,1,0:T(8,128)S(1)} %slice_add_fusion.1), channel_id=1, source_target_pairs={{0,2},{1,3},{2,0},{3,1},{4,6},{5,7},{6,4},{7,5},{8,10},{9,11},{10,... | collective-permute-start | bytes 786440 | tf_op jit(solution)/shard_map/ppermute | solution.py:404
  125.9 18.2 %collective-permute-start.40 = (f32[4,32,512]{2,1,0:T(8,128)S(1)}, f32[4,32,512]{2,1,0:T(8,128)S(1)}, u32[]{:S(2)}, u32[]{:S(2)}) collective-permute-start(f32[4,32,512]{2,1,0:T(8,128)S(1)} %slice_add_fusion), channel_id=1, source_target_pairs={{0,2},{1,3},{2,0},{3,1},{4,6},{5,7},{6,4},{7,5},{8,10},{9,11},{10,... | collective-permute-start | bytes 786440 | tf_op jit(solution)/shard_map/ppermute | solution.py:404
  126.6 22.7 %collective-permute-start.28 = (f32[4,32,512]{2,1,0:T(8,128)S(1)}, f32[4,32,512]{2,1,0:T(8,128)S(1)}, u32[]{:S(2)}, u32[]{:S(2)}) collective-permute-start(f32[4,32,512]{2,1,0:T(8,128)S(1)} %slice_add_fusion.3), channel_id=1, source_target_pairs={{0,2},{1,3},{2,0},{3,1},{4,6},{5,7},{6,4},{7,5},{8,10},{9,11},{10,... | collective-permute-start | bytes 786440 | tf_op jit(solution)/shard_map/ppermute | solution.py:404
  138.6 22.0 %collective-permute-start.36 = (f32[2,32,512]{2,1,0:T(8,128)S(1)}, f32[2,32,512]{2,1,0:T(8,128)S(1)}, u32[]{:S(2)}, u32[]{:S(2)}) collective-permute-start(f32[2,32,512]{2,1,0:T(8,128)S(1)} %pad_maximum_fusion.5), channel_id=1, source_target_pairs={{0,4},{1,5},{2,6},{3,7},{4,0},{5,1},{6,2},{7,3},{8,12},{9,13},{10,... | collective-permute-start | bytes 393224 | tf_op jit(solution)/shard_map/ppermute | solution.py:404
  139.5 21.4 %collective-permute-start.37 = (f32[2,32,512]{2,1,0:T(8,128)S(1)}, f32[2,32,512]{2,1,0:T(8,128)S(1)}, u32[]{:S(2)}, u32[]{:S(2)}) collective-permute-start(f32[2,32,512]{2,1,0:T(8,128)S(1)} %pad_maximum_fusion.6), channel_id=1, source_target_pairs={{0,8},{1,9},{2,10},{3,11},{4,12},{5,13},{6,14},{7,15},{8,0},{9,1},... | collective-permute-start | bytes 393224 | tf_op jit(solution)/shard_map/ppermute | solution.py:404
  (31 other events, 210.9 us)

commit v4 on v3

--- a/solution.py
+++ b/solution.py
@@ -56,23 +56,18 @@
 
 
 def spread(parts):
-    if len(parts) != 4:
-        return spread_any(parts)
-    lane = iotas()[1]
-    w = LANES // 4
-    index = (lane % w) * 4 + lane // w
-    p = [jnp.take_along_axis(x, index, axis=1) for x in parts]
-    low, even = lane < 2 * w, (lane // w) % 2 == 0
-    q = [None] * 4
-    for a in range(2):
-        x, y = p[a], p[a + 2]
-        q[a] = jnp.where(low, x, pltpu.roll(y, 2 * w, 1))
-        q[a + 2] = jnp.where(low, pltpu.roll(x, 2 * w, 1), y)
-    out = [None] * 4
-    for a in (0, 2):
-        x, y = q[a], q[a + 1]
-        out[a] = jnp.where(even, x, pltpu.roll(y, w, 1))
-        out[a + 1] = jnp.where(even, pltpu.roll(x, LANES - w, 1), y)
+    nb, lane = len(parts), iotas()[1]
+    w = LANES // nb
+    place = lane // w
+    sorted_parts = [
+        jnp.take_along_axis(x, (lane % w) * nb + (place + (nb - a)) % nb, axis=1) for a, x in enumerate(parts)
+    ]
+    out = []
+    for b in range(nb):
+        mixed = sorted_parts[0]
+        for a in range(1, nb):
+            mixed = jnp.where(place == (a + b) % nb, sorted_parts[a], mixed)
+        out.append(pltpu.roll(mixed, LANES - w * b, 1) if b else mixed)
     return out
 
 
@@ -91,11 +86,6 @@
     return v
 
 
-def spread_any(parts):
-    nb, lane = len(parts), iotas()[1]
-    return [pick(parts, lane // (LANES // nb), (lane * nb + b) % LANES) for b in range(nb)]
-
-
 def gather_back(parts):
     nb, lane = len(parts), iotas()[1]
     return [pick(parts, lane % nb, lane // nb + a * (LANES // nb)) for a in range(nb)]
@@ -105,28 +95,46 @@
     return [pl.BlockSpec(memory_space=s) for s in (pltpu.SMEM, pltpu.VMEM, pltpu.HBM)]
 
 
-def prep_models_kernel(depths, vel, ani, *outs):
+def prep_first_kernel(both, out):
+    _, R, NY = both.shape
+    nb = NY // LANES
+    for m in range(2):
+        for j in range(R // SUB):
+            rows = slice(j * SUB, (j + 1) * SUB)
+            for b, v in enumerate(spread([both[m, rows, cut(b)] for b in range(nb)])):
+                out[m, rows, cut(b)] = v
+
+
+def prep_first(both):
+    return pl.pallas_call(
+        prep_first_kernel, out_shape=jax.ShapeDtypeStruct(both.shape, jnp.float32), name="prep_first",
+        compiler_params=pltpu.CompilerParams(vmem_limit_bytes=4 << 20),
+    )(both)
+
+
+def prep_models_kernel(groups, vel, ani, *outs):
+    depth, R, NY = vel.shape
+    nb = NY // LANES
+
+    def body(j, _):
+        rows = pl.ds(pl.multiple_of(j * SUB, SUB), SUB)
+        for d in range(depth):
+            for m, ref in enumerate((vel, ani)):
+                for b, v in enumerate(spread([ref[d, rows, cut(b)] for b in range(nb)])):
+                    for group, out in zip(groups, outs):
+                        if d in group:
+                            out[group.index(d), m, rows, cut(b)] = v
+        return 0
+
+    lax.fori_loop(0, R // SUB, body, 0)
+
+
+def prep_models(vel, ani, groups):
     _, R, NY = vel.shape
-    nb = NY // LANES
-    for d in range(vel.shape[0]) if len(outs) > len(depths) else depths:
-        for m, ref in enumerate((vel, ani)):
-            for j in range(R // SUB):
-                rows = slice(j * SUB, (j + 1) * SUB)
-                new = spread([ref[d, rows, cut(b)] for b in range(nb)])
-                for b in range(nb):
-                    if d in depths:
-                        outs[depths.index(d)][m, rows, cut(b)] = new[b]
-                    if len(outs) > len(depths):
-                        outs[-1][d, m, rows, cut(b)] = new[b]
-
-
-def prep_models(vel, ani, depths, everything):
-    depth, R, NY = vel.shape
     _, vmem, _ = spaces()
-    shapes = [(2, R, NY)] * len(depths) + [(depth, 2, R, NY)] * everything
-    return pl.pallas_call(
-        lambda *r: prep_models_kernel(depths, *r), out_shape=[jax.ShapeDtypeStruct(x, jnp.float32) for x in shapes],
-        in_specs=[vmem] * 2, out_specs=[vmem] * len(shapes),
+    return pl.pallas_call(
+        lambda *r: prep_models_kernel(groups, *r), out_shape=[jax.ShapeDtypeStruct((len(g), 2, R, NY), jnp.float32) for g in groups],
+        in_specs=[vmem] * 2, out_specs=[vmem] * len(groups),
         name="prep_models", compiler_params=pltpu.CompilerParams(vmem_limit_bytes=4 << 20),
     )(vel, ani)
 
@@ -279,7 +287,7 @@
         for k in range(kb):
             places[half][k0 + k] = (ref, first + k)
     halos, sweep = wave_tools(where, G, NB)
-    om = om_ref[0]
+    om = om_ref[where[2]]
     k1 = 6.0 / om
     kp = 0.01 * om
 
@@ -366,7 +374,7 @@
         sweep(e2, put3, bases[o_i], R, send)
 
 
-def first_call(where, omega, blocks, metas, state, R):
+def first_call(where, frequency, blocks, metas, state, R):
     _, G, _, NY = state[0].shape
     smem, vmem, _ = spaces()
     pad = jax.ShapeDtypeStruct((4, G + 2, SUB, NY), jnp.float32)
@@ -374,7 +382,7 @@
         lambda *r: first_kernel(dict(metas=metas, R=R), *r), out_shape=[pad, pad, jax.ShapeDtypeStruct((2, G, SUB, NY), jnp.float32)],
         in_specs=[smem, smem] + [vmem] * (len(blocks) + 2), out_specs=[vmem] * 3, name="first_half",
         compiler_params=pltpu.CompilerParams(vmem_limit_bytes=VLIM),
-    )(where, omega, *blocks, *state)
+    )(where, frequency, *blocks, *state)
 
 
 def second_call(where, sh, e1, mod, last, R):
@@ -404,13 +412,15 @@
     return lax.ppermute(x, "freq", [(i, i ^ mask) for i in range(n)])
 
 
-def exchange_path(source, receiver, velocity, anisotropy, omega, scale):
+def exchange_path(source, receiver, velocity, anisotropy, frequency, scale):
     me = lax.axis_index("freq")
     depth_count, R, _ = velocity.shape
     G = R * lax.axis_size("freq") // SUB
-    where = jnp.stack([me >> 1, me & 1]).astype(jnp.int32)
-    own = list(prep_models(velocity, anisotropy, (0,), False))
-    *rest, all_own = prep_models(velocity, anisotropy, tuple(range(1, depth_count)), True)
+    where = jnp.stack([me >> 1, me & 1, lax.rem(me, frequency.shape[0])]).astype(jnp.int32)
+    first = jnp.stack([velocity[0], anisotropy[0]])
+    own = [prep_first(first)[None]]
+    groups = ((1,), tuple(range(2, depth_count)), tuple(range(depth_count)))
+    *rest, all_own = prep_models(velocity, anisotropy, groups)
     own += rest
     state = [prep_field(where, source, 0, 1.0, G)]
     state.append(prep_field(where, receiver, 0, -1.0, G))
@@ -420,12 +430,14 @@
     sums = []
     for d in range(depth_count):
         last = d == depth_count - 1
-        parts = [swap(own[d], far << 2) for far in range(1, HALF)]
+        if d < len(own):
+            come = [swap(own[d], far << 2) for far in range(1, HALF)]
+        parts = [x[max(0, d - 2)] for x in come]
         mine = jnp.stack(parts)
         near = swap(mine, 2)
         blocks = shared + [mine, near, swap(mine, 1), swap(near, 1)]
         metas = [(k0, 1, half, d) for k0, half in corners] + [(k0 + 1, HALF - 1, half, 0) for k0, half in corners]
-        mid = first_call(where, omega, blocks, metas, state, R)
+        mid = first_call(where, frequency, blocks, metas, state, R)
         kept, sent, *state = second_call(where, *mid, last, R)
         got = swap(sent, 1)
         upper = kept[HALF:] + got[HALF:]
@@ -439,7 +451,8 @@
     early = z_sum(sums[:-2])
     middle = z_sum(sums[-2:-1])
     tail = z_sum(sums[-1:])
-    before = finish_early(scale, jnp.concatenate([sum(early[1:], early[0]), sum(middle[1:], middle[0])[None]]))
+    before = jnp.concatenate([sum(early[1:], early[0]), sum(middle[1:], middle[0])[None]])
+    before = finish_early(scale, before)
     return finish_last(scale, tail, before)
 
 
@@ -453,7 +466,7 @@
     return jnp.swapaxes(x.reshape(x.shape[:-1] + (nb, LANES)), -1, -2).reshape(x.shape)
 
 
-def gather_path(source, receiver, velocity, anisotropy, omega, scale):
+def gather_path(source, receiver, velocity, anisotropy, frequency, scale):
     depth_count = velocity.shape[0]
     both = lax.all_gather(apart(jnp.stack([velocity, anisotropy], axis=1)), "freq", axis=2, tiled=True)
     NX, NY = both.shape[2:]
@@ -462,15 +475,17 @@
     back = [places.index(g) for g in range(SUB)]
     both = both.reshape(depth_count, 2, SUB, G, NY)
     both = jnp.stack([both[:, :, g] for g in places], axis=1)
-    where = jnp.zeros((2,), jnp.int32)
-    states = [[prep_field(where, source, p, 1.0, G), prep_field(where, receiver, p, -1.0, G)] for p in range(source.shape[0])]
+    pairs = source.shape[0]
+    ids = lax.axis_index("freq") * pairs + jnp.arange(pairs, dtype=jnp.int32)
+    wheres = [jnp.stack([0 * i, 0 * i, lax.rem(i, frequency.shape[0])]).astype(jnp.int32) for i in ids]
+    states = [[prep_field(wheres[p], source, p, 1.0, G), prep_field(wheres[p], receiver, p, -1.0, G)] for p in range(pairs)]
     layers = []
     for d in range(depth_count):
         total = None
         for p, state in enumerate(states):
             last = d == depth_count - 1
-            mid = first_call(where, omega[p : p + 1], [both[d]], [(0, SUB, 0, 0)], state, G)
-            res = second_call(where, *mid, last, G)
+            mid = first_call(wheres[p], frequency, [both[d]], [(0, SUB, 0, 0)], state, G)
+            res = second_call(wheres[p], *mid, last, G)
             total = res[0] if total is None else total + res[0]
             states[p] = None if last else res[1:]
         whole = jnp.concatenate([total[k] for k in back], axis=0)
@@ -485,13 +500,9 @@
 def on_device(source, receiver, velocity, anisotropy, frequency):
     pair_count = source.shape[0]
     n = lax.axis_size("freq")
-    freq_total = frequency.shape[0]
-    pair_ids = lax.axis_index("freq") * pair_count + jnp.arange(pair_count, dtype=jnp.int32)
-    lookup = pair_ids[:, None] % freq_total == jnp.arange(freq_total, dtype=jnp.int32)[None, :]
-    omega = jnp.sum(jnp.where(lookup, frequency[None, :], 0.0), axis=1)
     exchange = use_exchange(n, velocity.shape[1], pair_count, velocity.shape[0])
     path = exchange_path if exchange else gather_path
-    return path(source, receiver, velocity, anisotropy, omega, 1.0 / math.sqrt(pair_count * n))
+    return path(source, receiver, velocity, anisotropy, frequency, 1.0 / math.sqrt(pair_count * n))
 
 
 def solution(mesh):

time: 169 us -> 164 us (0.970)
  waiting for transfers between devices: 47.8 us -> 56.4 us
  starting transfers between devices: 58.9 us -> 52.5 us
  Pallas kernels: 53.9 us -> 47.9 us
    ppermute x44 -> x41, waiting for transfers between devices: 47.8 us -> 56.4 us  [swap(): return lax.ppermute(x, 'freq', [(i, i ^ mask) for i in range(n)])]
    ppermute x44 -> x41, starting transfers between devices: 58.9 us -> 52.5 us  [swap(): return lax.ppermute(x, 'freq', [(i, i ^ mask) for i in range(n)])]
    pallas_call x4, Pallas kernels: 22.3 us -> 19.8 us  [first_call(): pl.pallas_call(lambda *r: first_kernel(dict(metas=metas, R=R), *r), out_s...]
    pallas_call x2, Pallas kernels: 2.89 us -> 1.09 us  [the longest x1 0.88 us: prep_models(): pl.pallas_call(lambda *r: prep_models_kernel(groups, *r), out_shape=[jax....]
    pallas_call x2, Pallas kernels: 8.8 us -> 7.05 us  [prep_field(): pl.pallas_call(lambda *r: prep_field_kernel(p, sign, *r), out_shape=jax.S...]
    slice x0 -> x5, local copies, waits for them, and re-layouts: none -> 1.74 us  [the longest x2 1.69 us: exchange_path(): first = jnp.stack([velocity[0], anisotropy[0]])]
    unnamed x22 -> x30, local copies, waits for them, and re-layouts: 5 us -> 4.32 us
  transfers between devices with their start and end apart: 44 -> 41, of which waited for: 13 -> 11; matrix products, arithmetic and copies ran while one was open for 1% -> 0% of each run, Pallas kernels for 31% -> 28%
where the time goes in v4:
time: 164 us
  waiting for transfers between devices  56.4 us (34%)
  starting transfers between devices  52.5 us (32%)
  Pallas kernels  47.9 us (29%)
  local copies, waits for them, and re-layouts  6.09 us (4%)
    ppermute x41, waiting for transfers between devices, swap(): return lax.ppermute(x, 'freq', [(i, i ^ mask) for i in range(n)])  56.4 us
    ppermute x41, starting transfers between devices, swap(): return lax.ppermute(x, 'freq', [(i, i ^ mask) for i in range(n)])  52.5 us
    pallas_call x4, Pallas kernels, first_call(): pl.pallas_call(lambda *r: first_kernel(dict(metas=metas, R=R), *r), out_s...  19.8 us
    pallas_call x4, Pallas kernels, second_call(): pl.pallas_call(lambda *r: second_kernel(dict(last=last, R=R), *r), out_sh...  17.6 us
    pallas_call x2, Pallas kernels, prep_field(): pl.pallas_call(lambda *r: prep_field_kernel(p, sign, *r), out_shape=jax.S...  7.05 us
    unnamed x30, local copies, waits for them, and re-layouts  4.32 us
  transfers between devices with their start and end apart: 41, of which 11 were waited for; matrix products, arithmetic and copies ran while one was open for 0% of the time, Pallas kernels for 28%

profile of v4, /device:TPU:0, one launch (start us, length us, event | category | flops | bytes accessed | tf_op | source)
XLA Modules:
  0.0 163.9 jit_solution(17119276518494067455)
XLA Ops:
  1.9 3.1 %collective-permute-start.18 = (f32[1,2,32,512]{3,2,1,0:T(8,128)S(1)}, f32[1,2,32,512]{3,2,1,0:T(8,128)S(1)}, u32[]{:S(2)}, u32[]{:S(2)}) collective-permute-start(f32[1,2,32,512]{3,2,1,0:T(8,128)S(1)} %bitcast.30), channel_id=1, source_target_pairs={{0,4},{1,5},{2,6},{3,7},{4,0},{5,1},{6,2},{7,3},{8,12},{9,13},{10,... | collective-permute-start | bytes 393224 | tf_op jit(solution)/shard_map/ppermute | solution.py:412
  15.6 10.0 %collective-permute-done.19 = f32[1,2,32,512]{3,2,1,0:T(8,128)S(1)} collective-permute-done((f32[1,2,32,512]{3,2,1,0:T(8,128)S(1)}, f32[1,2,32,512]{3,2,1,0:T(8,128)S(1)}, u32[]{:S(2)}, u32[]{:S(2)}) %collective-permute-start.19) | collective-permute-done | bytes 131104 | tf_op jit(solution)/shard_map/ppermute | solution.py:412
  25.6 3.1 %collective-permute-start.14 = (f32[1,2,32,512]{3,2,1,0:T(8,128)S(1)}, f32[1,2,32,512]{3,2,1,0:T(8,128)S(1)}, u32[]{:S(2)}, u32[]{:S(2)}) collective-permute-start(f32[1,2,32,512]{3,2,1,0:T(8,128)S(1)} %get-tuple-element.36), channel_id=1, source_target_pairs={{0,12},{1,13},{2,14},{3,15},{4,8},{5,9},{6,10},{7,11},{8,4},{9,5},... | collective-permute-start | bytes 393224 | tf_op jit(solution)/shard_map/ppermute | solution.py:412
  28.9 5.1 %collective-permute-done.13 = f32[1,2,32,512]{3,2,1,0:T(8,128)S(1)} collective-permute-done((f32[1,2,32,512]{3,2,1,0:T(8,128)S(1)}, f32[1,2,32,512]{3,2,1,0:T(8,128)S(1)}, u32[]{:S(2)}, u32[]{:S(2)}) %collective-permute-start.13) | collective-permute-done | bytes 131104 | tf_op jit(solution)/shard_map/ppermute | solution.py:412
  34.1 3.1 %collective-permute-start.5 = (f32[2,2,32,512]{3,2,1,0:T(8,128)S(1)}, f32[2,2,32,512]{3,2,1,0:T(8,128)S(1)}, u32[]{:S(2)}, u32[]{:S(2)}) collective-permute-start(f32[2,2,32,512]{3,2,1,0:T(8,128)S(1)} %get-tuple-element.35), channel_id=1, source_target_pairs={{0,12},{1,13},{2,14},{3,15},{4,8},{5,9},{6,10},{7,11},{8,4},{9,5},... | collective-permute-start | bytes 786440 | tf_op jit(solution)/shard_map/ppermute | solution.py:412
  37.2 3.5 %collective-permute-done.3 = f32[2,2,32,512]{3,2,1,0:T(8,128)S(1)} collective-permute-done((f32[2,2,32,512]{3,2,1,0:T(8,128)S(1)}, f32[2,2,32,512]{3,2,1,0:T(8,128)S(1)}, u32[]{:S(2)}, u32[]{:S(2)}) %collective-permute-start.3) | collective-permute-done | bytes 262176 | tf_op jit(solution)/shard_map/ppermute | solution.py:412
  40.9 14.1 %collective-permute-done.4 = f32[2,2,32,512]{3,2,1,0:T(8,128)S(1)} collective-permute-done((f32[2,2,32,512]{3,2,1,0:T(8,128)S(1)}, f32[2,2,32,512]{3,2,1,0:T(8,128)S(1)}, u32[]{:S(2)}, u32[]{:S(2)}) %collective-permute-start.4) | collective-permute-done | bytes 262176 | tf_op jit(solution)/shard_map/ppermute | solution.py:412
  58.2 9.1 %collective-permute-done.15.r_7_ = f32[3,2,32,512]{3,2,1,0:T(8,128)} collective-permute-done((f32[3,2,32,512]{3,2,1,0:T(8,128)S(1)}, f32[3,2,32,512]{3,2,1,0:T(8,128)}, u32[]{:S(2)}, u32[]{:S(2)}) %collective-permute-start.15) | collective-permute-done | bytes 393248 | tf_op jit(solution)/shard_map/ppermute | solution.py:412
  70.6 3.5 %prep_field.2.r_10_ = f32[2,64,8,512]{3,2,1,0:T(8,128)S(1)} custom-call(s32[3]{0:T(128)S(1)} %pad_add_fusion.r_0_, f32[1,2,512,512]{3,2,1,0:T(8,128)S(1)} %copy-done), custom_call_target="tpu_custom_call" | custom-call | tf_op jit(solution)/shard_map/prep_field/pallas_call | solution.py:166
  74.2 3.5 %prep_field.3.r_11_ = f32[2,64,8,512]{3,2,1,0:T(8,128)S(1)} custom-call(s32[3]{0:T(128)S(1)} %pad_add_fusion.r_0_, f32[1,2,512,512]{3,2,1,0:T(8,128)S(1)} %copy-done.1), custom_call_target="tpu_custom_call" | custom-call | tf_op jit(solution)/shard_map/prep_field/pallas_call | solution.py:166
  77.7 4.5 %first_half.4 = (f32[4,66,8,512]{3,2,1,0:T(8,128)S(1)}, f32[4,66,8,512]{3,2,1,0:T(8,128)S(1)}, f32[2,64,8,512]{3,2,1,0:T(8,128)S(1)}) custom-call(s32[3]{0:T(128)S(1)} %pad_add_fusion.r_0_, f32[2]{0:T(128)S(1)} %copy-done.12, f32[4,2,32,512]{3,2,1,0:T(8,128)S(1)} %get-tuple-element.34.r_2_, f32[4,2,32,512]{3,2,1,0:T(8,128)S(1)} %collective-permute-done.r_3_, ...), custom_call_target="tpu_custom_call" | custom-call | tf_op jit(solution)/shard_map/first_half/pallas_call | solution.py:381
  82.3 4.4 %second_half.4 = (f32[8,32,512]{2,1,0:T(8,128)S(1)}, f32[8,32,512]{2,1,0:T(8,128)S(1)}, f32[2,64,8,512]{3,2,1,0:T(8,128)S(1)}, f32[2,64,8,512]{3,2,1,0:T(8,128)S(1)}) custom-call(s32[3]{0:T(128)S(1)} %pad_add_fusion.r_0_, f32[4,66,8,512]{3,2,1,0:T(8,128)S(1)} %get-tuple-element.37.r_1_, f32[4,66,8,512]{3,2,1,0:T(8,128)S(1)} %get-tuple-element.38.r_2_, ...), custom_call_target="tpu_custom_call" | custom-call | tf_op jit(solution)/shard_map/second_half/pallas_call | solution.py:399
  87.8 5.2 %first_half.5 = (f32[4,66,8,512]{3,2,1,0:T(8,128)S(1)}, f32[4,66,8,512]{3,2,1,0:T(8,128)S(1)}, f32[2,64,8,512]{3,2,1,0:T(8,128)S(1)}) custom-call(s32[3]{0:T(128)S(1)} %pad_add_fusion.r_0_, f32[2]{0:T(128)S(1)} %copy-done.12, f32[4,2,32,512]{3,2,1,0:T(8,128)S(1)} %get-tuple-element.34.r_2_, f32[4,2,32,512]{3,2,1,0:T(8,128)S(1)} %collective-permute-done.r_3_, ...), custom_call_target="tpu_custom_call" | custom-call | tf_op jit(solution)/shard_map/first_half/pallas_call | solution.py:381
  93.0 4.4 %second_half.5 = (f32[8,32,512]{2,1,0:T(8,128)S(1)}, f32[8,32,512]{2,1,0:T(8,128)S(1)}, f32[2,64,8,512]{3,2,1,0:T(8,128)S(1)}, f32[2,64,8,512]{3,2,1,0:T(8,128)S(1)}) custom-call(s32[3]{0:T(128)S(1)} %pad_add_fusion.r_0_, f32[4,66,8,512]{3,2,1,0:T(8,128)S(1)} %get-tuple-element.42.r_1_, f32[4,66,8,512]{3,2,1,0:T(8,128)S(1)} %get-tuple-element.43.r_2_, ...), custom_call_target="tpu_custom_call" | custom-call | tf_op jit(solution)/shard_map/second_half/pallas_call | solution.py:399
  97.6 5.1 %first_half.6 = (f32[4,66,8,512]{3,2,1,0:T(8,128)S(1)}, f32[4,66,8,512]{3,2,1,0:T(8,128)S(1)}, f32[2,64,8,512]{3,2,1,0:T(8,128)S(1)}) custom-call(s32[3]{0:T(128)S(1)} %pad_add_fusion.r_0_, f32[2]{0:T(128)S(1)} %copy-done.12, f32[4,2,32,512]{3,2,1,0:T(8,128)S(1)} %get-tuple-element.34.r_2_, f32[4,2,32,512]{3,2,1,0:T(8,128)S(1)} %collective-permute-done.r_3_, ...), custom_call_target="tpu_custom_call" | custom-call | tf_op jit(solution)/shard_map/first_half/pallas_call | solution.py:381
  102.8 4.4 %second_half.6 = (f32[8,32,512]{2,1,0:T(8,128)S(1)}, f32[8,32,512]{2,1,0:T(8,128)S(1)}, f32[2,64,8,512]{3,2,1,0:T(8,128)S(1)}, f32[2,64,8,512]{3,2,1,0:T(8,128)S(1)}) custom-call(s32[3]{0:T(128)S(1)} %pad_add_fusion.r_0_, f32[4,66,8,512]{3,2,1,0:T(8,128)S(1)} %get-tuple-element.47.r_1_, f32[4,66,8,512]{3,2,1,0:T(8,128)S(1)} %get-tuple-element.48.r_2_, ...), custom_call_target="tpu_custom_call" | custom-call | tf_op jit(solution)/shard_map/second_half/pallas_call | solution.py:399
  107.6 5.0 %first_half.7 = (f32[4,66,8,512]{3,2,1,0:T(8,128)S(1)}, f32[4,66,8,512]{3,2,1,0:T(8,128)S(1)}, f32[2,64,8,512]{3,2,1,0:T(8,128)S(1)}) custom-call(s32[3]{0:T(128)S(1)} %pad_add_fusion.r_0_, f32[2]{0:T(128)S(1)} %copy-done.12, f32[4,2,32,512]{3,2,1,0:T(8,128)S(1)} %get-tuple-element.34.r_2_, f32[4,2,32,512]{3,2,1,0:T(8,128)S(1)} %collective-permute-done.r_3_, ...), custom_call_target="tpu_custom_call" | custom-call | tf_op jit(solution)/shard_map/first_half/pallas_call | solution.py:381
  112.6 4.4 %second_half.7 = (f32[8,32,512]{2,1,0:T(8,128)S(1)}, f32[8,32,512]{2,1,0:T(8,128)S(1)}) custom-call(s32[3]{0:T(128)S(1)} %pad_add_fusion.r_0_, f32[4,66,8,512]{3,2,1,0:T(8,128)S(1)} %get-tuple-element.52.r_1_, f32[4,66,8,512]{3,2,1,0:T(8,128)S(1)} %get-tuple-element.53.r_2_, f32[2,64,8,512]{3,2,1,0:T(8,128)S(1)} %get-tuple-element.54.r_3_), custom_call_target="tpu_custom_call" | custom-call | tf_op jit(solution)/shard_map/second_half/pallas_call | solution.py:399
  121.6 4.8 %collective-permute-done.30 = f32[4,32,512]{2,1,0:T(8,128)S(1)} collective-permute-done((f32[4,32,512]{2,1,0:T(8,128)S(1)}, f32[4,32,512]{2,1,0:T(8,128)S(1)}, u32[]{:S(2)}, u32[]{:S(2)}) %collective-permute-start.30) | collective-permute-done | bytes 262176 | tf_op jit(solution)/shard_map/ppermute | solution.py:412
  126.5 5.5 %collective-permute-done.32 = f32[4,32,512]{2,1,0:T(8,128)S(1)} collective-permute-done((f32[4,32,512]{2,1,0:T(8,128)S(1)}, f32[4,32,512]{2,1,0:T(8,128)S(1)}, u32[]{:S(2)}, u32[]{:S(2)}) %collective-permute-start.32) | collective-permute-done | bytes 262176 | tf_op jit(solution)/shard_map/ppermute | solution.py:412
  132.1 5.3 %collective-permute-start.33 = (f32[2,32,512]{2,1,0:T(8,128)S(1)}, f32[2,32,512]{2,1,0:T(8,128)S(1)}, u32[]{:S(2)}, u32[]{:S(2)}) collective-permute-start(f32[2,32,512]{2,1,0:T(8,128)S(1)} %pad_maximum_fusion.4), channel_id=1, source_target_pairs={{0,4},{1,5},{2,6},{3,7},{4,0},{5,1},{6,2},{7,3},{8,12},{9,13},{10,... | collective-permute-start | bytes 393224 | tf_op jit(solution)/shard_map/ppermute | solution.py:412
  139.5 3.5 %collective-permute-start.38 = (f32[32,512]{1,0:T(8,128)S(1)}, f32[32,512]{1,0:T(8,128)S(1)}, u32[]{:S(2)}, u32[]{:S(2)}) collective-permute-start(f32[32,512]{1,0:T(8,128)S(1)} %get-tuple-element.71), channel_id=1, source_target_pairs={{0,4},{1,5},{2,6},{3,7},{4,0},{5,1},{6,2},{7,3},{8,12},{9,13},{10,... | collective-permute-start | bytes 196616 | tf_op jit(solution)/shard_map/ppermute | solution.py:412
  146.5 3.4 %collective-permute-start.35 = (f32[2,32,512]{2,1,0:T(8,128)S(1)}, f32[2,32,512]{2,1,0:T(8,128)S(1)}, u32[]{:S(2)}, u32[]{:S(2)}) collective-permute-start(f32[2,32,512]{2,1,0:T(8,128)S(1)} %pad_maximum_fusion.6), channel_id=1, source_target_pairs={{0,12},{1,13},{2,14},{3,15},{4,8},{5,9},{6,10},{7,11},{8,4},{9,5},... | collective-permute-start | bytes 393224 | tf_op jit(solution)/shard_map/ppermute | solution.py:412
  152.0 4.4 %collective-permute-start.27 = (f32[32,512]{1,0:T(8,128)S(1)}, f32[32,512]{1,0:T(8,128)S(1)}, u32[]{:S(2)}, u32[]{:S(2)}) collective-permute-start(f32[32,512]{1,0:T(8,128)S(1)} %get-tuple-element.75), channel_id=1, source_target_pairs={{0,8},{1,9},{2,10},{3,11},{4,12},{5,13},{6,14},{7,15},{8,0},{9,1},... | collective-permute-start | bytes 196616 | tf_op jit(solution)/shard_map/ppermute | solution.py:412
  (127 shorter events, 41.0 us)
Async XLA Ops:
  7.9 47.6 %collective-permute-start = (f32[4,2,32,512]{3,2,1,0:T(8,128)S(1)}, f32[4,2,32,512]{3,2,1,0:T(8,128)S(1)}, u32[]{:S(2)}, u32[]{:S(2)}) collective-permute-start(f32[4,2,32,512]{3,2,1,0:T(8,128)S(1)} %get-tuple-element.34.r_2_), channel_id=1, source_target_pairs={{0,2},{1,3},{2,0},{3,1},{4,6},{5,7},{6,4},{7,5},{8,10},{9,11},{10,... | collective-permute-start | bytes 1572872 | tf_op jit(solution)/shard_map/ppermute | solution.py:412
  9.9 46.2 %collective-permute-start.1 = (f32[4,2,32,512]{3,2,1,0:T(8,128)S(1)}, f32[4,2,32,512]{3,2,1,0:T(8,128)S(1)}, u32[]{:S(2)}, u32[]{:S(2)}) collective-permute-start(f32[4,2,32,512]{3,2,1,0:T(8,128)S(1)} %get-tuple-element.34.r_2_), channel_id=1, source_target_pairs={{0,1},{1,0},{2,3},{3,2},{4,5},{5,4},{6,7},{7,6},{8,9},{9,8},{10,11... | collective-permute-start | bytes 1572872 | tf_op jit(solution)/shard_map/ppermute | solution.py:412
  9.9 15.7 %collective-permute-start.19 = (f32[1,2,32,512]{3,2,1,0:T(8,128)S(1)}, f32[1,2,32,512]{3,2,1,0:T(8,128)S(1)}, u32[]{:S(2)}, u32[]{:S(2)}) collective-permute-start(f32[1,2,32,512]{3,2,1,0:T(8,128)S(1)} %bitcast.31), channel_id=1, source_target_pairs={{0,8},{1,9},{2,10},{3,11},{4,12},{5,13},{6,14},{7,15},{8,0},{9,1},... | collective-permute-start | bytes 393224 | tf_op jit(solution)/shard_map/ppermute | solution.py:412
  12.4 16.2 %collective-permute-start.20 = (f32[1,2,32,512]{3,2,1,0:T(8,128)S(1)}, f32[1,2,32,512]{3,2,1,0:T(8,128)S(1)}, u32[]{:S(2)}, u32[]{:S(2)}) collective-permute-start(f32[1,2,32,512]{3,2,1,0:T(8,128)S(1)} %bitcast.32), channel_id=1, source_target_pairs={{0,12},{1,13},{2,14},{3,15},{4,8},{5,9},{6,10},{7,11},{8,4},{9,5},... | collective-permute-start | bytes 393224 | tf_op jit(solution)/shard_map/ppermute | solution.py:412
  13.8 20.2 %collective-permute-start.13 = (f32[1,2,32,512]{3,2,1,0:T(8,128)S(1)}, f32[1,2,32,512]{3,2,1,0:T(8,128)S(1)}, u32[]{:S(2)}, u32[]{:S(2)}) collective-permute-start(f32[1,2,32,512]{3,2,1,0:T(8,128)S(1)} %get-tuple-element.36), channel_id=1, source_target_pairs={{0,8},{1,9},{2,10},{3,11},{4,12},{5,13},{6,14},{7,15},{8,0},{9,1},... | collective-permute-start | bytes 393224 | tf_op jit(solution)/shard_map/ppermute | solution.py:412
  34.0 21.1 %collective-permute-start.4 = (f32[2,2,32,512]{3,2,1,0:T(8,128)S(1)}, f32[2,2,32,512]{3,2,1,0:T(8,128)S(1)}, u32[]{:S(2)}, u32[]{:S(2)}) collective-permute-start(f32[2,2,32,512]{3,2,1,0:T(8,128)S(1)} %get-tuple-element.35), channel_id=1, source_target_pairs={{0,8},{1,9},{2,10},{3,11},{4,12},{5,13},{6,14},{7,15},{8,0},{9,1},... | collective-permute-start | bytes 786440 | tf_op jit(solution)/shard_map/ppermute | solution.py:412
  34.1 21.1 %collective-permute-start.5 = (f32[2,2,32,512]{3,2,1,0:T(8,128)S(1)}, f32[2,2,32,512]{3,2,1,0:T(8,128)S(1)}, u32[]{:S(2)}, u32[]{:S(2)}) collective-permute-start(f32[2,2,32,512]{3,2,1,0:T(8,128)S(1)} %get-tuple-element.35), channel_id=1, source_target_pairs={{0,12},{1,13},{2,14},{3,15},{4,8},{5,9},{6,10},{7,11},{8,4},{9,5},... | collective-permute-start | bytes 786440 | tf_op jit(solution)/shard_map/ppermute | solution.py:412
  40.7 15.1 %collective-permute-start.21 = (f32[3,2,32,512]{3,2,1,0:T(8,128)S(1)}, f32[3,2,32,512]{3,2,1,0:T(8,128)S(1)}, u32[]{:S(2)}, u32[]{:S(2)}) collective-permute-start(f32[3,2,32,512]{3,2,1,0:T(8,128)S(1)} %constant_dynamic-update-slice_fusion.3.r_6_), channel_id=1, source_target_pairs={{0,2},{1,3},{2,0},{3,1},{4,6},{5,7},{6,4},{7,5},{8,10},{9,11},{10,... | collective-permute-start | bytes 1179656 | tf_op jit(solution)/shard_map/ppermute | solution.py:412
  55.5 12.9 %collective-permute-start.2 = (f32[4,2,32,512]{3,2,1,0:T(8,128)S(1)}, f32[4,2,32,512]{3,2,1,0:T(8,128)S(1)}, u32[]{:S(2)}, u32[]{:S(2)}) collective-permute-start(f32[4,2,32,512]{3,2,1,0:T(8,128)S(1)} %collective-permute-done.r_3_), channel_id=1, source_target_pairs={{0,1},{1,0},{2,3},{3,2},{4,5},{5,4},{6,7},{7,6},{8,9},{9,8},{10,11... | collective-permute-start | bytes 1572872 | tf_op jit(solution)/shard_map/ppermute | solution.py:412
  56.1 30.6 %collective-permute-start.16 = (f32[3,2,32,512]{3,2,1,0:T(8,128)S(1)}, f32[3,2,32,512]{3,2,1,0:T(8,128)}, u32[]{:S(2)}, u32[]{:S(2)}) collective-permute-start(f32[3,2,32,512]{3,2,1,0:T(8,128)S(1)} %constant_dynamic-update-slice_fusion.r_6_), channel_id=1, source_target_pairs={{0,1},{1,0},{2,3},{3,2},{4,5},{5,4},{6,7},{7,6},{8,9},{9,8},{10,11... | collective-permute-start | bytes 1179656 | tf_op jit(solution)/shard_map/ppermute | solution.py:412
  56.8 30.0 %collective-permute-start.9 = (f32[3,2,32,512]{3,2,1,0:T(8,128)S(1)}, f32[3,2,32,512]{3,2,1,0:T(8,128)}, u32[]{:S(2)}, u32[]{:S(2)}) collective-permute-start(f32[3,2,32,512]{3,2,1,0:T(8,128)S(1)} %pad_maximum_fusion.1.r_6_), channel_id=1, source_target_pairs={{0,2},{1,3},{2,0},{3,1},{4,6},{5,7},{6,4},{7,5},{8,10},{9,11},{10,... | collective-permute-start | bytes 1179656 | tf_op jit(solution)/shard_map/ppermute | solution.py:412
  67.3 20.0 %collective-permute-start.6 = (f32[3,2,32,512]{3,2,1,0:T(8,128)S(1)}, f32[3,2,32,512]{3,2,1,0:T(8,128)}, u32[]{:S(2)}, u32[]{:S(2)}) collective-permute-start(f32[3,2,32,512]{3,2,1,0:T(8,128)S(1)} %pad_maximum_fusion.r_6_), channel_id=1, source_target_pairs={{0,2},{1,3},{2,0},{3,1},{4,6},{5,7},{6,4},{7,5},{8,10},{9,11},{10,... | collective-permute-start | bytes 1179656 | tf_op jit(solution)/shard_map/ppermute | solution.py:412
  68.4 19.0 %collective-permute-start.17 = (f32[3,2,32,512]{3,2,1,0:T(8,128)}, f32[3,2,32,512]{3,2,1,0:T(8,128)}, u32[]{:S(2)}, u32[]{:S(2)}) collective-permute-start(f32[3,2,32,512]{3,2,1,0:T(8,128)} %collective-permute-done.15.r_7_), channel_id=1, source_target_pairs={{0,1},{1,0},{2,3},{3,2},{4,5},{5,4},{6,7},{7,6},{8,9},{9,8},{10,11... | collective-permute-start | bytes 1179656 | tf_op jit(solution)/shard_map/ppermute | solution.py:412
  68.4 29.1 %collective-permute-start.10 = (f32[3,2,32,512]{3,2,1,0:T(8,128)S(1)}, f32[3,2,32,512]{3,2,1,0:T(8,128)}, u32[]{:S(2)}, u32[]{:S(2)}) collective-permute-start(f32[3,2,32,512]{3,2,1,0:T(8,128)S(1)} %pad_maximum_fusion.1.r_6_), channel_id=1, source_target_pairs={{0,1},{1,0},{2,3},{3,2},{4,5},{5,4},{6,7},{7,6},{8,9},{9,8},{10,11... | collective-permute-start | bytes 1179656 | tf_op jit(solution)/shard_map/ppermute | solution.py:412
  86.7 30.4 %collective-permute-start.29 = (f32[8,32,512]{2,1,0:T(8,128)S(1)}, f32[8,32,512]{2,1,0:T(8,128)S(1)}, u32[]{:S(2)}, u32[]{:S(2)}) collective-permute-start(f32[8,32,512]{2,1,0:T(8,128)S(1)} %get-tuple-element.58), channel_id=1, source_target_pairs={{0,1},{1,0},{2,3},{3,2},{4,5},{5,4},{6,7},{7,6},{8,9},{9,8},{10,11... | collective-permute-start | bytes 1572872 | tf_op jit(solution)/shard_map/ppermute | solution.py:412
  87.3 20.3 %collective-permute-start.7 = (f32[3,2,32,512]{3,2,1,0:T(8,128)S(1)}, f32[3,2,32,512]{3,2,1,0:T(8,128)S(1)}, u32[]{:S(2)}, u32[]{:S(2)}) collective-permute-start(f32[3,2,32,512]{3,2,1,0:T(8,128)S(1)} %pad_maximum_fusion.r_6_), channel_id=1, source_target_pairs={{0,1},{1,0},{2,3},{3,2},{4,5},{5,4},{6,7},{7,6},{8,9},{9,8},{10,11... | collective-permute-start | bytes 1179656 | tf_op jit(solution)/shard_map/ppermute | solution.py:412
  87.4 20.3 %collective-permute-start.8 = (f32[3,2,32,512]{3,2,1,0:T(8,128)}, f32[3,2,32,512]{3,2,1,0:T(8,128)S(1)}, u32[]{:S(2)}, u32[]{:S(2)}) collective-permute-start(f32[3,2,32,512]{3,2,1,0:T(8,128)} %collective-permute-done.6.r_7_), channel_id=1, source_target_pairs={{0,1},{1,0},{2,3},{3,2},{4,5},{5,4},{6,7},{7,6},{8,9},{9,8},{10,11... | collective-permute-start | bytes 1179656 | tf_op jit(solution)/shard_map/ppermute | solution.py:412
  97.5 21.5 %collective-permute-start.31 = (f32[8,32,512]{2,1,0:T(8,128)S(1)}, f32[8,32,512]{2,1,0:T(8,128)S(1)}, u32[]{:S(2)}, u32[]{:S(2)}) collective-permute-start(f32[8,32,512]{2,1,0:T(8,128)S(1)} %get-tuple-element.60), channel_id=1, source_target_pairs={{0,1},{1,0},{2,3},{3,2},{4,5},{5,4},{6,7},{7,6},{8,9},{9,8},{10,11... | collective-permute-start | bytes 1572872 | tf_op jit(solution)/shard_map/ppermute | solution.py:412
  107.2 12.2 %collective-permute-start.36 = (f32[8,32,512]{2,1,0:T(8,128)S(1)}, f32[8,32,512]{2,1,0:T(8,128)S(1)}, u32[]{:S(2)}, u32[]{:S(2)}) collective-permute-start(f32[8,32,512]{2,1,0:T(8,128)S(1)} %get-tuple-element.62), channel_id=1, source_target_pairs={{0,1},{1,0},{2,3},{3,2},{4,5},{5,4},{6,7},{7,6},{8,9},{9,8},{10,11... | collective-permute-start | bytes 1572872 | tf_op jit(solution)/shard_map/ppermute | solution.py:412
  119.0 13.1 %collective-permute-start.32 = (f32[4,32,512]{2,1,0:T(8,128)S(1)}, f32[4,32,512]{2,1,0:T(8,128)S(1)}, u32[]{:S(2)}, u32[]{:S(2)}) collective-permute-start(f32[4,32,512]{2,1,0:T(8,128)S(1)} %slice_add_fusion.1), channel_id=1, source_target_pairs={{0,2},{1,3},{2,0},{3,1},{4,6},{5,7},{6,4},{7,5},{8,10},{9,11},{10,... | collective-permute-start | bytes 786440 | tf_op jit(solution)/shard_map/ppermute | solution.py:412
  119.4 20.0 %collective-permute-start.37 = (f32[4,32,512]{2,1,0:T(8,128)S(1)}, f32[4,32,512]{2,1,0:T(8,128)S(1)}, u32[]{:S(2)}, u32[]{:S(2)}) collective-permute-start(f32[4,32,512]{2,1,0:T(8,128)S(1)} %slice_add_fusion), channel_id=1, source_target_pairs={{0,2},{1,3},{2,0},{3,1},{4,6},{5,7},{6,4},{7,5},{8,10},{9,11},{10,... | collective-permute-start | bytes 786440 | tf_op jit(solution)/shard_map/ppermute | solution.py:412
  121.2 23.8 %collective-permute-start.25 = (f32[4,32,512]{2,1,0:T(8,128)S(1)}, f32[4,32,512]{2,1,0:T(8,128)S(1)}, u32[]{:S(2)}, u32[]{:S(2)}) collective-permute-start(f32[4,32,512]{2,1,0:T(8,128)S(1)} %slice_add_fusion.3), channel_id=1, source_target_pairs={{0,2},{1,3},{2,0},{3,1},{4,6},{5,7},{6,4},{7,5},{8,10},{9,11},{10,... | collective-permute-start | bytes 786440 | tf_op jit(solution)/shard_map/ppermute | solution.py:412
  132.1 24.3 %collective-permute-start.33 = (f32[2,32,512]{2,1,0:T(8,128)S(1)}, f32[2,32,512]{2,1,0:T(8,128)S(1)}, u32[]{:S(2)}, u32[]{:S(2)}) collective-permute-start(f32[2,32,512]{2,1,0:T(8,128)S(1)} %pad_maximum_fusion.4), channel_id=1, source_target_pairs={{0,4},{1,5},{2,6},{3,7},{4,0},{5,1},{6,2},{7,3},{8,12},{9,13},{10,... | collective-permute-start | bytes 393224 | tf_op jit(solution)/shard_map/ppermute | solution.py:412
  137.4 20.6 %collective-permute-start.34 = (f32[2,32,512]{2,1,0:T(8,128)S(1)}, f32[2,32,512]{2,1,0:T(8,128)S(1)}, u32[]{:S(2)}, u32[]{:S(2)}) collective-permute-start(f32[2,32,512]{2,1,0:T(8,128)S(1)} %pad_maximum_fusion.5), channel_id=1, source_target_pairs={{0,8},{1,9},{2,10},{3,11},{4,12},{5,13},{6,14},{7,15},{8,0},{9,1},... | collective-permute-start | bytes 393224 | tf_op jit(solution)/shard_map/ppermute | solution.py:412
  (30 other events, 224.2 us)
